TPU v7x, 512 devices: a whole 4x8x8 slice. The times are simulated.
512 devices in a mesh: dp: 32 (over y, x), seq: 16 (over z, core).
Axes of the slice: x: 4, y: 8, z: 8, core: 2. Of those that a mesh axis runs over, the one named last changes fastest.
Arguments:
- grad_out: bfloat16 [65536, 1280], P(('dp', 'seq')), may hold values from -6 to 6
- saved_input: bfloat16 [65536, 1280], P(('dp', 'seq')), may hold values from -6 to 6
- pre_glu: bfloat16 [65536, 2560], P(('dp', 'seq')), may hold values from -6 to 6
- queries: bfloat16 [65536, 1280], P('dp', 'seq'), may hold values from -8 to 8
- keys: bfloat16 [65536, 1280], P('dp', 'seq'), may hold values from -8 to 8
- values: bfloat16 [65536, 1280], P('dp', 'seq'), may hold values from -6 to 6
- frame_counts: int32 [32, 8], P('dp'), may hold values from 1 to 1024, 2048 in all within a row
- norm_gain: float32 [1280], replicated, may hold values from 0.5 to 1.5
- kernel: float32 [31, 1280], replicated, may hold values from -1 to 1
- w_in: bfloat16 [1280, 2560], P('dp'), may hold values from -0.15625 to 0.15625
- w_conv_out: bfloat16 [1280, 1280], P('dp'), may hold values from -0.15625 to 0.15625
- w_attn_out: bfloat16 [1280, 1280], P('dp'), may hold values from -0.15625 to 0.15625
Outputs:
- resid_grad: bfloat16 [65536, 1280], P(('dp', 'seq'))
- query_grad: bfloat16 [65536, 1280], P('dp', 'seq')
- key_grad: bfloat16 [65536, 1280], P('dp', 'seq')
- value_grad: bfloat16 [65536, 1280], P('dp', 'seq')
- kernel_grad: float32 [31, 1280], replicated
- gain_grad: float32 [1280], replicated
Inputs may be any that keep to these rules, and one draw needn't show every extreme that they name: `frame_counts`: each row sums to 2048; its largest entry is exactly 1024.
All inputs are finite; a program needn't handle non-finite values.
Results may differ from a plain program's by a relative error of at most 0.018.
Values may be sent and summed in bfloat16 or wider, within the bound.
No kernel may reach another device: no remote copies, remote signals or barrier semaphores. Data moves between devices by JAX's collectives and lax.ppermute only.
A program may use at most 64 MiB of HBM per device.

v0:
```python
import math

import jax
import jax.numpy as jnp
from jax import lax
from jax.sharding import PartitionSpec as P

HD = 80
KW = 31


def padded(block, sides, width):
    for axis, dim in sides:
        count = lax.axis_size(axis)
        forward = [(i, i + 1) for i in range(count - 1)]
        backward = [(target, source) for source, target in forward]
        low = lax.ppermute(
            lax.slice_in_dim(block, block.shape[dim] - width, None, axis=dim), axis, forward
        )
        high = lax.ppermute(lax.slice_in_dim(block, 0, width, axis=dim), axis, backward)
        block = jnp.concatenate([low, block, high], axis=dim)
    return block


def segments_of(frame_lens, positions):
    ends = jnp.cumsum(frame_lens)
    counted = jnp.sum((positions[:, None] >= ends[None, :]).astype(jnp.int32), axis=1)
    return jnp.where(positions < 0, jnp.int32(-1), counted)


def row_product(active, piece):
    return jnp.einsum("tc,rc->tr", active, piece, preferred_element_type=jnp.float32)


def attention_backward(query_rows, key_rows, value_rows, out_grad, seg_all):
    total, columns = query_rows.shape
    heads = columns // HD
    scale = 1.0 / math.sqrt(HD)
    query_heads = query_rows.reshape(total, heads, HD)
    key_heads = key_rows.reshape(total, heads, HD)
    value_heads = value_rows.reshape(total, heads, HD)
    grad_heads = out_grad.reshape(total, heads, HD)
    qblock = min(512, total)
    nblocks = total // qblock

    def block_step(block, carry):
        query_out, key_acc, value_acc = carry
        qstart = block * qblock
        query_block = lax.dynamic_slice_in_dim(query_heads, qstart, qblock, 0)
        grad_block = lax.dynamic_slice_in_dim(grad_heads, qstart, qblock, 0)
        seg_query = lax.dynamic_slice_in_dim(seg_all, qstart, qblock, 0)
        scores = (
            jnp.einsum("qhd,khd->hqk", query_block, key_heads, preferred_element_type=jnp.float32)
            * scale
        )
        scores = jnp.where((seg_query[:, None] == seg_all[None, :])[None], scores, -1e30)
        peak = jnp.max(scores, axis=2, keepdims=True)
        expd = jnp.exp(scores - peak)
        probs = expd / jnp.sum(expd, axis=2, keepdims=True)
        probs_low = probs.astype(jnp.bfloat16)
        value_part = jnp.einsum(
            "hqk,qhd->khd", probs_low, grad_block, preferred_element_type=jnp.float32
        )
        prob_grad = jnp.einsum(
            "qhd,khd->hqk", grad_block, value_heads, preferred_element_type=jnp.float32
        )
        delta = jnp.sum(probs * prob_grad, axis=2, keepdims=True)
        score_grad = (probs * (prob_grad - delta)).astype(jnp.bfloat16)
        query_part = (
            jnp.einsum("hqk,khd->qhd", score_grad, key_heads, preferred_element_type=jnp.float32)
            * scale
        ).astype(jnp.bfloat16)
        key_part = jnp.einsum(
            "hqk,qhd->khd", score_grad, query_block, preferred_element_type=jnp.float32
        )
        query_out = lax.dynamic_update_slice_in_dim(query_out, query_part, qstart, 0)
        return (query_out, key_acc + key_part, value_acc + value_part)

    initial = (
        jnp.zeros((total, heads, HD), jnp.bfloat16),
        jnp.zeros((total, heads, HD), jnp.float32),
        jnp.zeros((total, heads, HD), jnp.float32),
    )
    query_out, key_acc, value_acc = lax.fori_loop(0, nblocks, block_step, initial)
    key_grad = (key_acc * scale).astype(jnp.bfloat16)
    value_grad = value_acc.astype(jnp.bfloat16)
    return (
        query_out.reshape(total, columns),
        key_grad.reshape(total, columns),
        value_grad.reshape(total, columns),
    )


def local(
    grad_out,
    saved_input,
    pre_glu,
    queries,
    keys,
    values,
    frame_counts,
    norm_gain,
    kernel,
    w_in,
    w_conv_out,
    w_attn_out,
):
    t_dev, width = grad_out.shape
    n_seq = lax.axis_size("seq")
    total = t_dev * n_seq
    half = KW // 2
    frame_lens = frame_counts[0]
    seq_index = lax.axis_index("seq")
    ext_pos = seq_index * t_dev + jnp.arange(-half, t_dev + half, dtype=jnp.int32)
    seg_ext = segments_of(frame_lens, ext_pos)
    seg_own = seg_ext[half : half + t_dev]
    first_half = pre_glu[:, :width].astype(jnp.float32)
    gate_sig = jax.nn.sigmoid(pre_glu[:, width:].astype(jnp.float32))
    glu_out = (first_half * gate_sig).astype(jnp.bfloat16)
    glu_ext = padded(glu_out, (("seq", 0),), half).astype(jnp.float32)
    matches = [
        (seg_ext[tap_index : tap_index + t_dev] == seg_own).astype(jnp.float32)[:, None]
        for tap_index in range(KW)
    ]
    conv_out = jnp.zeros((t_dev, width), jnp.float32)
    for tap_index in range(KW):
        conv_out = (
            conv_out
            + kernel[tap_index] * glu_ext[tap_index : tap_index + t_dev] * matches[tap_index]
        )
    conv_out_grad = row_product(grad_out, lax.all_gather(w_conv_out, "dp", axis=0, tiled=True))
    conv_sig = jax.nn.sigmoid(conv_out)
    conv_grad = (conv_out_grad * conv_sig * (1.0 + conv_out * (1.0 - conv_sig))).astype(
        jnp.bfloat16
    )
    grad_ext = padded(conv_grad, (("seq", 0),), half).astype(jnp.float32)
    grad_float = grad_ext[half : half + t_dev]
    glu_grad = jnp.zeros((t_dev, width), jnp.float32)
    kernel_rows = []
    for tap_index in range(KW):
        back = 2 * half - tap_index
        glu_grad = glu_grad + kernel[tap_index] * grad_ext[back : back + t_dev] * matches[back]
        kernel_rows.append(
            jnp.sum(
                grad_float * glu_ext[tap_index : tap_index + t_dev] * matches[tap_index], axis=0
            )
        )
    glu_in_grad = jnp.concatenate(
        [glu_grad * gate_sig, glu_grad * first_half * gate_sig * (1.0 - gate_sig)], axis=1
    ).astype(jnp.bfloat16)
    norm_grad = row_product(glu_in_grad, lax.all_gather(w_in, "dp", axis=0, tiled=True))
    inputs = saved_input.astype(jnp.float32)
    centred = inputs - jnp.mean(inputs, axis=1, keepdims=True)
    inv_std = 1.0 / jnp.sqrt(jnp.mean(centred * centred, axis=1, keepdims=True) + 1e-05)
    normed = centred * inv_std
    scaled_grad = norm_grad * norm_gain
    input_grad = inv_std * (
        scaled_grad
        - jnp.mean(scaled_grad, axis=1, keepdims=True)
        - normed * jnp.mean(scaled_grad * normed, axis=1, keepdims=True)
    )
    resid_grad = (grad_out.astype(jnp.float32) + input_grad).astype(jnp.bfloat16)
    gain_term = jnp.sum(norm_grad * normed, axis=0)
    ctx_float = row_product(resid_grad, lax.all_gather(w_attn_out, "dp", axis=0, tiled=True))
    ctx_grad = ctx_float.astype(jnp.bfloat16)
    relayed = lax.all_to_all(ctx_grad, "seq", split_axis=1, concat_axis=0, tiled=True)
    seg_all = segments_of(frame_lens, jnp.arange(total, dtype=jnp.int32))
    query_grad, key_grad, value_grad = attention_backward(queries, keys, values, relayed, seg_all)
    kernel_grad, gain_grad = lax.psum((jnp.stack(kernel_rows), gain_term), ("dp", "seq"))
    return (resid_grad, query_grad, key_grad, value_grad, kernel_grad, gain_grad)


def solution(mesh):
    in_specs = (
        P(("dp", "seq"), None),
        P(("dp", "seq"), None),
        P(("dp", "seq"), None),
        P("dp", "seq"),
        P("dp", "seq"),
        P("dp", "seq"),
        P("dp", None),
        P(),
        P(),
        P("dp", None),
        P("dp", None),
        P("dp", None),
    )
    out_specs = (P(("dp", "seq"), None), P("dp", "seq"), P("dp", "seq"), P("dp", "seq"), P(), P())
    return jax.shard_map(local, mesh=mesh, in_specs=in_specs, out_specs=out_specs, check_vma=False)
```

profile of v0, /device:TPU:1, one launch (start us, length us, event | category | flops | bytes accessed | tf_op | source)
XLA Modules:
  0.0 569.4 jit_solution(128491667545102661)
XLA Ops:
  10.0 5.4 collective-permute-start
  15.4 4.7 collective-permute-start.1
  26.8 71.7 %all-gather.4.cloned.1.call-done = bf16[1280,1280]{1,0:T(8,128)(2,1)} async-done(((bf16[40,1280]{1,0:T(8,128)(2,1)}), bf16[1280,1280]{1,0:T(8,128)(2,1)}) %all-gather.4.cloned.1.call-update) | async-done | bytes 3276816 | tf_op jit(solution)/shard_map/all_gather | solution.py:131
  98.6 5.7 fusion.26
  104.3 7.3 %collective-permute-start.2 = (bf16[15,1280]{1,0:T(8,128)(2,1)S(1)}, bf16[15,1280]{1,0:T(8,128)(2,1)S(1)}, u32[]{:S(2)}, u32[]{:S(2)}) collective-permute-start(bf16[15,1280]{1,0:T(8,128)(2,1)S(1)} %get-tuple-element.284), channel_id=1, source_target_pairs={{0,1},{1,2},{2,3},{3,4},{4,5},{5,6},{6,7},{7,8},{8,9},{9,10},{10,1... | collective-permute-start | bytes 115208 | tf_op jit(solution)/shard_map/ppermute | solution.py:17
  111.6 2.1 collective-permute-start.3
  113.8 3.1 collective-permute-done.3
  119.9 4.4 multiply_convert_fusion.2
  124.5 72.3 %all-gather.6.cloned.1.call-done = bf16[1280,2560]{1,0:T(8,128)(2,1)} async-done(((bf16[40,2560]{1,0:T(8,128)(2,1)}), bf16[1280,2560]{1,0:T(8,128)(2,1)}) %all-gather.6.cloned.1.call-update) | async-done | bytes 6553616 | tf_op jit(solution)/shard_map/all_gather | solution.py:151
  196.9 5.3 fusion.37
  202.6 77.3 %all-gather.8.cloned.1.call-done = bf16[1280,1280]{1,0:T(8,128)(2,1)} async-done(((bf16[40,1280]{1,0:T(8,128)(2,1)}), bf16[1280,1280]{1,0:T(8,128)(2,1)}) %all-gather.8.cloned.1.call-update) | async-done | bytes 3276816 | tf_op jit(solution)/shard_map/all_gather | solution.py:164
  279.9 3.1 convolution_convert_fusion
  284.0 11.6 %all-to-all-start = ((bf16[128,16,80]{0,2,1:T(8,128)(2,1)}), bf16[128,16,80]{0,2,1:T(8,128)(2,1)S(1)}, u32[]{:S(2)}, u32[]{:S(2)}) async-start(bf16[128,16,80]{0,2,1:T(8,128)(2,1)} %bitcast.4), calls=%async_computation | async-start | bytes 655360 | tf_op jit(solution)/shard_map/all_to_all | solution.py:166
  297.4 2.7 stack.127
  300.1 97.6 %psum.15 = f32[1280]{0:T(1024)} all-reduce(f32[1280]{0:T(1024)S(1)} %get-tuple-element.225), channel_id=1, replica_groups=mesh['dp'=32,'seq'=16] {'dp','seq'}, use_global_device_ids=true, to_apply=%region_45.46 | all-reduce | flops 1280 | bytes 10240 | tf_op jit(solution)/shard_map/psum | solution.py:169
  398.0 44.9 %while.18 = (s32[]{:T(128)}, bf16[2048,1,80]{0,2,1:T(8,128)(2,1)S(1)}, f32[2048,1,80]{0,2,1:T(8,128)S(1)}, f32[2048,1,80]{0,2,1:T(8,128)}, s32[2048]{0:T(1024)S(...) while((s32[]{:T(128)}, ...), condition=%wide.region_11.12_spmd.clone, body=%wide.region_7.0_spmd.clone.sunk | while | flops 858470912 | bytes 79810904 | solution.py:84
  399.1 1.9 copy-done
  401.8 3.4 fusion.141
  410.3 1.9 copy-done
  413.0 3.4 fusion.141
  424.2 3.4 fusion.141
  435.4 3.4 fusion.141
  442.9 2.0 convert_bitcast_fusion
  445.6 115.7 %all-reduce.2.cloned.1.call-done = f32[31,1280]{1,0:T(8,128)} async-done(((f32[31,1280]{1,0:T(8,128)}), f32[31,1280]{1,0:T(8,128)}) %all-reduce.2.cloned.1.call-update) | async-done | bytes 158736 | tf_op jit(solution)/shard_map/psum | solution.py:169
  (161 shorter events, 45.5 us)
Async XLA Ops:
  7.2 91.4 %all-gather.4.cloned.1.call-start = ((), (), s32[]{:S(2)}) async-start(), calls=%async_computation.1 | async-start | bytes 3379200 | tf_op jit(solution)/shard_map/all_gather | solution.py:131
  7.9 189.0 %all-gather.6.cloned.1.call-start = ((), (), s32[]{:S(2)}) async-start(), calls=%async_computation.2 | async-start | bytes 6758400 | tf_op jit(solution)/shard_map/all_gather | solution.py:151
  8.6 271.3 %all-gather.8.cloned.1.call-start = ((), (), s32[]{:S(2)}) async-start(), calls=%async_computation.3 | async-start | bytes 3379200 | tf_op jit(solution)/shard_map/all_gather | solution.py:164
  10.0 16.7 %collective-permute-start = (bf16[15,1280]{1,0:T(8,128)(2,1)S(1)}, bf16[15,1280]{1,0:T(8,128)(2,1)S(1)}, u32[]{:S(2)}, u32[]{:S(2)}) collective-permute-start(bf16[15,1280]{1,0:T(8,128)(2,1)S(1)} %get-tuple-element.286), channel_id=1, source_target_pairs={{0,1},{1,2},{2,3},{3,4},{4,5},{5,6},{6,7},{7,8},{8,9},{9,10},{10,1... | collective-permute-start | bytes 115208 | tf_op jit(solution)/shard_map/ppermute | solution.py:17
  15.4 11.3 %collective-permute-start.1 = (bf16[15,1280]{1,0:T(8,128)(2,1)S(1)}, bf16[15,1280]{1,0:T(8,128)(2,1)S(1)}, u32[]{:S(2)}, u32[]{:S(2)}) collective-permute-start(bf16[15,1280]{1,0:T(8,128)(2,1)S(1)} %get-tuple-element.287), channel_id=1, source_target_pairs={{1,0},{2,1},{3,2},{4,3},{5,4},{6,5},{7,6},{8,7},{9,8},{10,9},{11,1... | collective-permute-start | bytes 115208 | tf_op jit(solution)/shard_map/ppermute | solution.py:20
  104.3 9.6 %collective-permute-start.2 = (bf16[15,1280]{1,0:T(8,128)(2,1)S(1)}, bf16[15,1280]{1,0:T(8,128)(2,1)S(1)}, u32[]{:S(2)}, u32[]{:S(2)}) collective-permute-start(bf16[15,1280]{1,0:T(8,128)(2,1)S(1)} %get-tuple-element.284), channel_id=1, source_target_pairs={{0,1},{1,2},{2,3},{3,4},{4,5},{5,6},{6,7},{7,8},{8,9},{9,10},{10,1... | collective-permute-start | bytes 115208 | tf_op jit(solution)/shard_map/ppermute | solution.py:17
  111.6 5.3 collective-permute-start.3
  119.9 77.0 %copy-start.4 = (bf16[128,1280]{1,0:T(8,128)(2,1)S(1)}, bf16[128,1280]{1,0:T(8,128)(2,1)}, u32[]{:S(2)}) copy-start(bf16[128,1280]{1,0:T(8,128)(2,1)} %param.15) | copy-start | bytes 983044
  119.9 77.0 %copy-start.11 = (f32[1280]{0:T(1024)S(1)}, f32[1280]{0:T(1024)}, u32[]{:S(2)}) copy-start(f32[1280]{0:T(1024)} %param.21) | copy-start | bytes 15364
  196.9 5.4 copy-start.10
  202.6 93.8 %copy-start.5 = (bf16[128,1280]{1,0:T(8,128)(2,1)}, bf16[128,1280]{1,0:T(8,128)(2,1)S(1)}, u32[]{:S(2)}) copy-start(bf16[128,1280]{1,0:T(8,128)(2,1)S(1)} %fusion.36) | copy-start | bytes 983044
  284.0 113.7 %all-to-all-start = ((bf16[128,16,80]{0,2,1:T(8,128)(2,1)}), bf16[128,16,80]{0,2,1:T(8,128)(2,1)S(1)}, u32[]{:S(2)}, u32[]{:S(2)}) async-start(bf16[128,16,80]{0,2,1:T(8,128)(2,1)} %bitcast.4), calls=%async_computation | async-start | bytes 655360 | tf_op jit(solution)/shard_map/all_to_all | solution.py:166
  295.5 265.8 %all-reduce.2.cloned.1.call-start = ((), (), s32[]{:S(2)}) async-start(), calls=%async_computation.4 | async-start | bytes 327680 | tf_op jit(solution)/shard_map/psum | solution.py:169
  296.4 101.5 %copy-start.2 = (bf16[2048,80]{0,1:T(8,128)(2,1)S(1)}, bf16[2048,80]{0,1:T(8,128)(2,1)}, u32[]{:S(2)}) copy-start(bf16[2048,80]{0,1:T(8,128)(2,1)} %param.18) | copy-start | bytes 983044
  296.4 101.5 %copy-start.8 = (bf16[2048,80]{0,1:T(8,128)(2,1)S(1)}, bf16[2048,80]{0,1:T(8,128)(2,1)}, u32[]{:S(2)}) copy-start(bf16[2048,80]{0,1:T(8,128)(2,1)} %param.17) | copy-start | bytes 983044
  398.1 3.7 copy-start.6
  401.8 3.5 copy-start.12
  409.3 3.7 copy-start.6
  413.0 3.5 copy-start.12
  420.5 3.7 copy-start.6
  424.2 3.5 copy-start.12
  431.8 3.7 copy-start.6
  435.4 3.5 copy-start.12
  442.9 120.0 %copy-start.9 = (bf16[2048,1,80]{0,2,1:T(8,128)(2,1)}, bf16[2048,1,80]{0,2,1:T(8,128)(2,1)S(1)}, u32[]{:S(2)}) copy-start(bf16[2048,1,80]{0,2,1:T(8,128)(2,1)S(1)} %get-tuple-element.162) | copy-start | bytes 983044
  (13 other events, 28.8 us)
Sparse Core Ops, SparseCore 0:
  11.2 87.3 all-gather.3
  101.7 95.0 all-gather.5
  200.0 79.8 all-gather.7
  301.6 259.6 all-reduce.1
where the time goes:
time: 570 us; the launch traced here: 569 us
  waiting for transfers between devices  342 us (60%)
  blocking collectives  97.6 us (17%)
  matrix products  42 us (7%)
  starting transfers between devices  31.2 us (5%)
  other arithmetic  25.2 us (4%)
  local copies, waits for them, and re-layouts  17.2 us (3%)
  between operations  14.3 us (3%)
    psum x1, waiting for transfers between devices, local(): lax.psum((jnp.stack(kernel_rows), gain_term), ('dp', 'seq'))  116 us
    psum x1, blocking collectives, local(): lax.psum((jnp.stack(kernel_rows), gain_term), ('dp', 'seq'))  97.6 us
    all_gather x1, waiting for transfers between devices, local(): lax.all_gather(w_attn_out, 'dp', axis=0, tiled=True)  77.3 us
    all_gather x1, waiting for transfers between devices, local(): lax.all_gather(w_in, 'dp', axis=0, tiled=True)  72.3 us
    all_gather x1, waiting for transfers between devices, local(): lax.all_gather(w_conv_out, 'dp', axis=0, tiled=True)  71.7 us
    dot_general x3, matrix products, row_product(): jnp.einsum('tc,rc->tr', active, piece, preferred_element_type=jnp.float32)  14.2 us
    dot_general x4, matrix products, block_step(): jnp.einsum('hqk,qhd->khd', probs_low, grad_block, preferred_element_type=...  13.4 us
    ppermute x2, starting transfers between devices, padded(): lax.ppermute(lax.slice_in_dim(block, block.shape[dim] - width, None, axis...  12.7 us
  transfers between devices with their start and end apart: 9, of which 5 were waited for; matrix products, arithmetic and copies ran while one was open for 12% of the time, Pallas kernels for 0%

commit v1 on v0

v1 whole, which is shorter than its diff:
```python
import math

import jax
import jax.numpy as jnp
from jax import lax
from jax.experimental import pallas as pl
from jax.experimental.pallas import tpu as pltpu
from jax.sharding import Mesh
from jax.sharding import PartitionSpec as P

HD = 80
KW = 31
BLK = 256
TIME = ("z", "core")
GROUPS = ("y", "x")


def frame_ends(frame_lens):
    n = frame_lens.shape[0]
    upto = jnp.arange(n)[:, None] >= jnp.arange(n)[None, :]
    return jnp.sum(jnp.where(upto, frame_lens[None, :], 0), axis=1).astype(jnp.int32)


def segments_of(ends, positions):
    counted = jnp.sum((positions[:, None] >= ends[None, :]).astype(jnp.int32), axis=1)
    return jnp.where(positions < 0, jnp.int32(-1), counted)


def padded(block, width):
    count = lax.axis_size(TIME)
    forward = [(i, i + 1) for i in range(count - 1)]
    backward = [(target, source) for source, target in forward]
    low = lax.ppermute(block[block.shape[0] - width :], TIME, forward)
    high = lax.ppermute(block[:width], TIME, backward)
    return jnp.concatenate([low, block, high], axis=0)


def spread(piece, axis):
    count = lax.axis_size(axis)
    copies = jnp.broadcast_to(piece[None], (count,) + piece.shape)
    return lax.all_to_all(copies, axis, split_axis=0, concat_axis=0)


def row_product(active, piece):
    return jnp.einsum("tc,rc->tr", active, piece, preferred_element_type=jnp.float32)


def halves(array, core):
    width = array.shape[1] // 2
    own = lax.dynamic_slice_in_dim(array, core * width, width, 1)
    away = lax.dynamic_slice_in_dim(array, (1 - core) * width, width, 1)
    return own, away


def swap(array):
    return lax.ppermute(array, "core", [(0, 1), (1, 0)])


def pair_product(own, away, piece):
    other = swap(away)
    back = swap(row_product(other, piece))
    return row_product(own, piece) + back


def probs_kernel(bounds, q_t, k, v_t, lo, hi, probs, out_t, inv_sum, scores):
    factor = math.log2(math.e) / math.sqrt(HD)
    block = pl.program_id(0)
    first = bounds[0, block]
    last = bounds[1, block]
    query = q_t[...]
    start = lo[...]
    end = hi[...]
    width = query.shape[1]
    rows = lax.broadcasted_iota(jnp.int32, (BLK, width), 0)

    def score(kb, peak):
        at = pl.multiple_of(kb * BLK, BLK)
        s = jnp.dot(k[pl.ds(at, BLK), :], query, preferred_element_type=jnp.float32)
        valid = (rows >= start - at) & (rows < end - at)
        s = jnp.where(valid, s, -1e30)
        scores[pl.ds(at, BLK), :] = s
        return jnp.maximum(peak, jnp.max(s.reshape(BLK // 8, 8, width), axis=0))

    peak = lax.fori_loop(first, last, score, jnp.full((8, width), -1e30, jnp.float32))
    peak = jnp.max(peak, axis=0, keepdims=True)

    def expo(kb, carry):
        total, acc = carry
        at = pl.multiple_of(kb * BLK, BLK)
        e = jnp.exp2((scores[pl.ds(at, BLK), :] - peak) * factor)
        low = e.astype(jnp.bfloat16)
        probs[pl.ds(at, BLK), :] = low
        acc = acc + jnp.dot(v_t[:, pl.ds(at, BLK)], low, preferred_element_type=jnp.float32)
        return total + jnp.sum(e.reshape(BLK // 8, 8, width), axis=0), acc

    total, acc = lax.fori_loop(
        first,
        last,
        expo,
        (jnp.zeros((8, width), jnp.float32), jnp.zeros((HD, width), jnp.float32)),
    )
    inv = 1.0 / jnp.sum(total, axis=0, keepdims=True)
    inv_sum[...] = inv
    out_t[...] = acc * inv


def attention_probs(bounds, q_t, keys, v_t, lo, hi):
    total = keys.shape[0]
    n = total // BLK
    lanes = lambda rows: pl.BlockSpec((rows, BLK), lambda i, b: (0, i))
    whole = lambda shape: pl.BlockSpec(shape, lambda i, b: (0, 0))
    return pl.pallas_call(
        probs_kernel,
        grid_spec=pltpu.PrefetchScalarGridSpec(
            num_scalar_prefetch=1,
            grid=(n,),
            in_specs=[
                lanes(HD),
                whole((total, HD)),
                whole((HD, total)),
                lanes(1),
                lanes(1),
            ],
            out_specs=[
                pl.BlockSpec((None, total, BLK), lambda i, b: (i, 0, 0)),
                lanes(HD),
                lanes(1),
            ],
            scratch_shapes=[pltpu.VMEM((total, BLK), jnp.float32)],
        ),
        out_shape=[
            jax.ShapeDtypeStruct((n, total, BLK), jnp.bfloat16),
            jax.ShapeDtypeStruct((HD, total), jnp.float32),
            jax.ShapeDtypeStruct((1, total), jnp.float32),
        ],
        compiler_params=pltpu.CompilerParams(vmem_limit_bytes=32 << 20),
        cost_estimate=pl.CostEstimate(
            flops=2 * total * total * HD * 2,
            transcendentals=total * total // 2,
            bytes_accessed=total * total * 2,
        ),
        name="attention_probs",
    )(bounds, q_t, keys, v_t, lo, hi)


def grads_kernel(bounds, probs, ctx_t, out_t, inv_sum, q, k_t, v, dq_t, dk_t, dv_t, dk_acc, dv_acc):
    scale = 1.0 / math.sqrt(HD)
    block = pl.program_id(0)
    first = bounds[0, block]
    last = bounds[1, block]

    @pl.when(block == 0)
    def _():
        dk_acc[...] = jnp.zeros_like(dk_acc)
        dv_acc[...] = jnp.zeros_like(dv_acc)

    pieces = [ctx_t[i].astype(jnp.float32) for i in range(ctx_t.shape[0])]
    grad_t = jnp.concatenate(pieces, axis=1) * inv_sum[...]
    grad_low_t = grad_t.astype(jnp.bfloat16)
    grad_low = grad_t.T.astype(jnp.bfloat16)
    delta = jnp.sum(grad_low_t.astype(jnp.float32) * out_t[...], axis=0, keepdims=True)
    query = q[...]

    def step(kb, acc):
        at = pl.multiple_of(kb * BLK, BLK)
        e = probs[pl.ds(at, BLK), :]
        prob_grad = jnp.dot(v[pl.ds(at, BLK), :], grad_low_t, preferred_element_type=jnp.float32)
        ds = (e.astype(jnp.float32) * (prob_grad - delta)).astype(jnp.bfloat16)
        dv_acc[pl.ds(at, BLK), :] += jnp.dot(e, grad_low, preferred_element_type=jnp.float32)
        dk_acc[pl.ds(at, BLK), :] += jnp.dot(ds, query, preferred_element_type=jnp.float32)
        return acc + jnp.dot(k_t[:, pl.ds(at, BLK)], ds, preferred_element_type=jnp.float32)

    acc = lax.fori_loop(first, last, step, jnp.zeros((HD, query.shape[0]), jnp.float32))
    dq_t[...] = (acc * scale).astype(jnp.bfloat16)

    @pl.when(block == pl.num_programs(0) - 1)
    def _():
        dk_t[...] = (dk_acc[...] * scale).T.astype(jnp.bfloat16)
        dv_t[...] = dv_acc[...].T.astype(jnp.bfloat16)


def attention_grads(bounds, probs, ctx_t, out_t, inv_sum, queries, k_t, values):
    total = queries.shape[0]
    n = total // BLK
    per = BLK // ctx_t.shape[2]
    lanes = lambda rows: pl.BlockSpec((rows, BLK), lambda i, b: (0, i))
    whole = lambda shape: pl.BlockSpec(shape, lambda i, b: (0, 0))
    shape = jax.ShapeDtypeStruct((HD, total), jnp.bfloat16)
    return pl.pallas_call(
        grads_kernel,
        grid_spec=pltpu.PrefetchScalarGridSpec(
            num_scalar_prefetch=1,
            grid=(n,),
            in_specs=[
                pl.BlockSpec((None, total, BLK), lambda i, b: (i, 0, 0)),
                pl.BlockSpec((per, HD, ctx_t.shape[2]), lambda i, b: (i, 0, 0)),
                lanes(HD),
                lanes(1),
                pl.BlockSpec((BLK, HD), lambda i, b: (i, 0)),
                whole((HD, total)),
                whole((total, HD)),
            ],
            out_specs=[lanes(HD), whole((HD, total)), whole((HD, total))],
            scratch_shapes=[pltpu.VMEM((total, HD), jnp.float32)] * 2,
        ),
        out_shape=[shape, shape, shape],
        compiler_params=pltpu.CompilerParams(vmem_limit_bytes=32 << 20),
        cost_estimate=pl.CostEstimate(
            flops=2 * total * total * HD * 4,
            transcendentals=0,
            bytes_accessed=total * total * 2,
        ),
        name="attention_grads",
    )(bounds, probs, ctx_t, out_t, inv_sum, queries, k_t, values)


def local(
    grad_out,
    saved_input,
    pre_glu,
    queries,
    keys,
    values,
    frame_counts,
    norm_gain,
    kernel,
    w_in,
    w_conv_out,
    w_attn_out,
):
    t_dev, width = grad_out.shape
    n_seq = lax.axis_size(TIME)
    total = t_dev * n_seq
    half = KW // 2
    core = lax.axis_index("core")
    ends = frame_ends(frame_counts[0])

    in_low, _ = halves(w_in[:, :width], core)
    in_high, _ = halves(w_in[:, width:], core)
    gathered = lax.all_gather(
        jnp.concatenate([in_low, in_high, w_attn_out], axis=1), GROUPS, axis=0, tiled=True
    )
    w_in_half = gathered[:, :width]
    w_attn = gathered[:, width:]

    conv_half, _ = halves(w_conv_out, core)
    by_y = spread(conv_half, "y")
    by_xy = spread(by_y, "x")
    w_conv_half = by_xy.transpose(1, 0, 2, 3).reshape(width, width // 2)

    positions = jnp.arange(total, dtype=jnp.int32)
    passed = positions[None, :] >= ends[:, None]
    lo = jnp.max(jnp.where(passed, ends[:, None], 0), axis=0, keepdims=True)
    hi = jnp.min(jnp.where(passed, total, ends[:, None]), axis=0, keepdims=True)
    bounds = jnp.stack([lo[0, ::BLK] // BLK, (hi[0, BLK - 1 :: BLK] + BLK - 1) // BLK])
    probs, out_t, inv_sum = attention_probs(bounds, queries.T, keys, values.T, lo, hi)

    seq_index = lax.axis_index(TIME)
    ext_pos = seq_index * t_dev + jnp.arange(-half, t_dev + half, dtype=jnp.int32)
    seg_ext = segments_of(ends, ext_pos)
    seg_own = seg_ext[half : half + t_dev]
    first_half = pre_glu[:, :width].astype(jnp.float32)
    gate_sig = jax.nn.sigmoid(pre_glu[:, width:].astype(jnp.float32))
    glu_out = (first_half * gate_sig).astype(jnp.bfloat16)
    glu_ext = padded(glu_out, half).astype(jnp.float32)
    matches = [
        (seg_ext[tap_index : tap_index + t_dev] == seg_own).astype(jnp.float32)[:, None]
        for tap_index in range(KW)
    ]
    conv_out = jnp.zeros((t_dev, width), jnp.float32)
    for tap_index in range(KW):
        conv_out = (
            conv_out
            + kernel[tap_index] * glu_ext[tap_index : tap_index + t_dev] * matches[tap_index]
        )
    conv_out_grad = pair_product(*halves(grad_out, core), w_conv_half)
    conv_sig = jax.nn.sigmoid(conv_out)
    conv_grad = (conv_out_grad * conv_sig * (1.0 + conv_out * (1.0 - conv_sig))).astype(
        jnp.bfloat16
    )
    grad_ext = padded(conv_grad, half).astype(jnp.float32)
    grad_float = grad_ext[half : half + t_dev]
    glu_grad = jnp.zeros((t_dev, width), jnp.float32)
    kernel_rows = []
    for tap_index in range(KW):
        back = 2 * half - tap_index
        glu_grad = glu_grad + kernel[tap_index] * grad_ext[back : back + t_dev] * matches[back]
        kernel_rows.append(
            jnp.sum(
                grad_float * glu_ext[tap_index : tap_index + t_dev] * matches[tap_index], axis=0
            )
        )
    low_grad = (glu_grad * gate_sig).astype(jnp.bfloat16)
    high_grad = (glu_grad * first_half * gate_sig * (1.0 - gate_sig)).astype(jnp.bfloat16)
    low_own, low_away = halves(low_grad, core)
    high_own, high_away = halves(high_grad, core)

    rows = jnp.stack(kernel_rows + [jnp.zeros((width,), jnp.float32)])
    rows = lax.all_to_all(
        rows.reshape(n_seq, (KW + 1) // n_seq, width), TIME, split_axis=0, concat_axis=0
    )
    rows = jnp.sum(rows, axis=0)
    for axis in GROUPS:
        rows = jnp.sum(spread(rows, axis), axis=0)
    kernel_grad = spread(rows, TIME).reshape(KW + 1, width)[:KW]

    norm_grad = pair_product(
        jnp.concatenate([low_own, high_own], axis=1),
        jnp.concatenate([low_away, high_away], axis=1),
        w_in_half,
    )
    inputs = saved_input.astype(jnp.float32)
    centred = inputs - jnp.mean(inputs, axis=1, keepdims=True)
    inv_std = 1.0 / jnp.sqrt(jnp.mean(centred * centred, axis=1, keepdims=True) + 1e-05)
    normed = centred * inv_std
    scaled_grad = norm_grad * norm_gain
    input_grad = inv_std * (
        scaled_grad
        - jnp.mean(scaled_grad, axis=1, keepdims=True)
        - normed * jnp.mean(scaled_grad * normed, axis=1, keepdims=True)
    )
    resid_grad = (grad_out.astype(jnp.float32) + input_grad).astype(jnp.bfloat16)
    ctx_t = jnp.einsum("rc,tc->rt", w_attn, resid_grad, preferred_element_type=jnp.float32)
    ctx_t = ctx_t.astype(jnp.bfloat16).reshape(n_seq, HD, t_dev)
    ctx_t = lax.all_to_all(ctx_t, TIME, split_axis=0, concat_axis=0)
    grads = attention_grads(
        bounds, probs, ctx_t, out_t, inv_sum, queries, keys.T, values
    )
    query_grad, key_grad, value_grad = [array.T for array in grads]
    gain = jnp.sum(norm_grad * normed, axis=0, keepdims=True)
    for axis in (TIME,) + GROUPS:
        gain = jnp.sum(spread(gain, axis), axis=0)
    return (resid_grad, query_grad, key_grad, value_grad, kernel_grad, gain[0])


def solution(mesh):
    dp, seq = mesh.devices.shape
    shape = (dp // 4, 4, seq // 2, 2)
    fine = Mesh(mesh.devices.reshape(shape), GROUPS + TIME)
    frames = P(GROUPS + TIME, None)
    heads = P(GROUPS, TIME)
    group = P(GROUPS, None)
    in_specs = (
        frames,
        frames,
        frames,
        heads,
        heads,
        heads,
        group,
        P(),
        P(),
        group,
        group,
        group,
    )
    out_specs = (frames, heads, heads, heads, P(), P())
    return jax.shard_map(local, mesh=fine, in_specs=in_specs, out_specs=out_specs, check_vma=False)
```

time: 570 us -> 247 us (0.43)
  waiting for transfers between devices: 342 us -> 65.3 us
  blocking collectives: 97.6 us -> 0 us
  starting transfers between devices: 31.2 us -> 82 us
  matrix products: 42 us -> 12.2 us
  Pallas kernels: 0 us -> 28.2 us
    all_gather x3 -> x1, waiting for transfers between devices: 221 us -> 6.89 us  [local(): lax.all_gather(jnp.concatenate([in_low, in_high, w_attn_out], axis=1), GR...]
    psum x1 -> x0, waiting for transfers between devices: 116 us -> none  [local(): lax.psum((jnp.stack(kernel_rows), gain_term), ('dp', 'seq'))]
    psum x1 -> x0, blocking collectives: 97.6 us -> none  [local(): lax.psum((jnp.stack(kernel_rows), gain_term), ('dp', 'seq'))]
    all_to_all x1 -> x10, waiting for transfers between devices: 0.01 us -> 54.6 us  [the longest x8 54.6 us: spread(): return lax.all_to_all(copies, axis, split_axis=0, concat_axis=0)]
    all_to_all x1 -> x10, starting transfers between devices: 11.6 us -> 57.1 us  [the longest x8 43.3 us: spread(): return lax.all_to_all(copies, axis, split_axis=0, concat_axis=0)]
    pallas_call x0 -> x2, Pallas kernels: none -> 28.2 us  [the longest x1 14.7 us: attention_grads(): pl.pallas_call(grads_kernel, grid_spec=pltpu.PrefetchScalarGridSpec(num_s...]
    dot_general x20 -> x1, matrix products: 27.8 us -> 3.75 us  [local(): jnp.einsum('rc,tc->rt', w_attn, resid_grad, preferred_element_type=jnp.fl...]
    while x40 -> x0, local copies, waits for them, and re-layouts: 8.17 us -> none
  transfers between devices with their start and end apart: 9 -> 19, of which waited for: 5 -> 10; matrix products, arithmetic and copies ran while one was open for 12% -> 15% of each run, Pallas kernels for 0% -> 6%
where the time goes in v1:
time: 247 us; the launch traced here: 245 us
  starting transfers between devices  82 us (33%)
  waiting for transfers between devices  65.3 us (26%)
  Pallas kernels  28.2 us (11%)
  other arithmetic  21.1 us (9%)
  local copies, waits for them, and re-layouts  20.8 us (8%)
  between operations  15.6 us (6%)
  matrix products  12.2 us (5%)
    all_to_all x8, waiting for transfers between devices, spread(): return lax.all_to_all(copies, axis, split_axis=0, concat_axis=0)  54.6 us
    all_to_all x8, starting transfers between devices, spread(): return lax.all_to_all(copies, axis, split_axis=0, concat_axis=0)  43.3 us
    pallas_call x1, Pallas kernels, attention_grads(): pl.pallas_call(grads_kernel, grid_spec=pltpu.PrefetchScalarGridSpec(num_s...  14.7 us
    ppermute x4, starting transfers between devices, swap(): return lax.ppermute(array, 'core', [(0, 1), (1, 0)])  13.9 us
    pallas_call x1, Pallas kernels, attention_probs(): pl.pallas_call(probs_kernel, grid_spec=pltpu.PrefetchScalarGridSpec(num_s...  13.5 us
    all_to_all x1, starting transfers between devices, local(): lax.all_to_all(rows.reshape(n_seq, (KW + 1) // n_seq, width), TIME, split...  10 us
    unnamed x129, local copies, waits for them, and re-layouts  8.71 us
    dot_general x4, matrix products, row_product(): jnp.einsum('tc,rc->tr', active, piece, preferred_element_type=jnp.float32)  8.42 us
  transfers between devices with their start and end apart: 19, of which 10 were waited for; matrix products, arithmetic and copies ran while one was open for 15% of the time, Pallas kernels for 6%

profile of v1, /device:TPU:1, one launch (start us, length us, event | category | flops | bytes accessed | tf_op | source)
XLA Modules:
  0.0 245.2 jit_solution(11049337915959444775)
XLA Ops:
  10.8 7.7 %all-to-all-start = ((bf16[8,40,640]{2,1,0:T(8,128)(2,1)}), bf16[8,40,640]{2,1,0:T(8,128)(2,1)S(1)}, u32[]{:S(2)}, u32[]{:S(2)}) async-start(bf16[8,40,640]{2,1,0:T(8,128)(2,1)} %broadcast_in_dim.58), calls=%async_computation | async-start | bytes 819200 | tf_op jit(solution)/shard_map/all_to_all | solution.py:41
  19.4 4.7 %collective-permute-start = (bf16[128,640]{1,0:T(8,128)(2,1)S(1)}, bf16[128,640]{1,0:T(8,128)(2,1)S(1)}, u32[]{:S(2)}, u32[]{:S(2)}) collective-permute-start(bf16[128,640]{1,0:T(8,128)(2,1)S(1)} %constant_dynamic-slice_fusion.6), channel_id=1, source_target_pairs={{0,1},{1,0},{2,3},{3,2},{4,5},{5,4},{6,7},{7,6},{8,9},{9,8},{10,11... | collective-permute-start | bytes 491528 | tf_op jit(solution)/shard_map/ppermute | solution.py:56
  31.7 6.8 %all-to-all-start.1 = ((bf16[4,8,40,640]{3,2,1,0:T(8,128)(2,1)}), bf16[4,8,40,640]{3,2,1,0:T(8,128)(2,1)S(1)}, u32[]{:S(2)}, u32[]{:S(2)}) async-start(bf16[4,8,40,640]{3,2,1,0:T(8,128)(2,1)} %broadcast_in_dim.59), calls=%async_computation.1 | async-start | bytes 3276800 | tf_op jit(solution)/shard_map/all_to_all | solution.py:41
  42.0 17.7 %all-to-all-done.1 = bf16[4,8,40,640]{3,2,1,0:T(8,128)(2,1)S(1)} async-done(((bf16[4,8,40,640]{3,2,1,0:T(8,128)(2,1)}), bf16[4,8,40,640]{3,2,1,0:T(8,128)(2,1)S(1)}, u32[]{:S(2)}, u32[]{:S(2)}) %all-to-all-start.1) | async-done | bytes 1638432 | tf_op jit(solution)/shard_map/all_to_all | solution.py:41
  60.8 4.2 %collective-permute-start.1 = (f32[128,1280]{1,0:T(8,128)S(1)}, f32[128,1280]{1,0:T(8,128)S(1)}, u32[]{:S(2)}, u32[]{:S(2)}) collective-permute-start(f32[128,1280]{1,0:T(8,128)S(1)} %fusion.101), channel_id=1, source_target_pairs={{0,1},{1,0},{2,3},{3,2},{4,5},{5,4},{6,7},{7,6},{8,9},{9,8},{10,11... | collective-permute-start | bytes 1966088 | tf_op jit(solution)/shard_map/ppermute | solution.py:56
  67.2 4.5 %multiply_convert_fusion.1 = bf16[128,1280]{1,0:T(8,128)(2,1)S(1)} fusion(f32[128,1280]{1,0:T(8,128)S(1)} %fusion.93, f32[128,1280]{1,0:T(8,128)S(1)} %collective-permute-done.1, f32[158,1280]{1,0:T(8,128)S(1)} %maximum_convert_fusion, f32[128]{0:T(128)} %get-tuple-element.125, f32[1280]{0:T(1024)S(1)} %get-tuple-element.80, f32[128]{0:T(128)S(1)} %copy-done.35, ...), kind=kLoop, calls=%fused_computation.149 | loop fusion | flops 16547840 | bytes 22128640 | tf_op jit(solution)/shard_map/convert_element_type | solution.py:278
  71.7 4.2 %collective-permute-start.4 = (bf16[15,1280]{1,0:T(8,128)(2,1)S(1)}, bf16[15,1280]{1,0:T(8,128)(2,1)S(1)}, u32[]{:S(2)}, u32[]{:S(2)}) collective-permute-start(bf16[15,1280]{1,0:T(8,128)(2,1)S(1)} %get-tuple-element.91), channel_id=1, source_target_pairs={{0,1},{1,2},{2,3},{3,4},{4,5},{5,6},{6,7},{7,8},{8,9},{9,10},{10,1... | collective-permute-start | bytes 115208 | tf_op jit(solution)/shard_map/ppermute | solution.py:33
  77.9 3.8 %collective-permute-done.5 = bf16[15,1280]{1,0:T(8,128)(2,1)S(1)} collective-permute-done((bf16[15,1280]{1,0:T(8,128)(2,1)S(1)}, bf16[15,1280]{1,0:T(8,128)(2,1)S(1)}, u32[]{:S(2)}, u32[]{:S(2)}) %collective-permute-start.5) | collective-permute-done | bytes 38432 | tf_op jit(solution)/shard_map/ppermute | solution.py:34
  86.4 3.9 %multiply_convert_fusion = (bf16[128,1280]{1,0:T(8,128)(2,1)S(1)}, f32[128,1280]{1,0:T(8,128)S(1)}) fusion(bf16[128,2560]{1,0:T(8,128)(2,1)S(1)} %copy-done.7, f32[128]{0:T(128)S(1)} %copy-done.58, f32[158,1280]{1,0:T(8,128)S(1)} %maximum_convert_fusion.1, f32[1280]{0:T(1024)S(1)} %get-tuple-element.80, f32[128]{0:T(128)S(1)} %copy-done.34, ...), kind=kLoop, calls=%fused_computation.148 | loop fusion | flops 15892480 | bytes 21800960 | tf_op jit(solution)/shard_map/convert_element_type | solution.py:293
  94.8 10.0 %all-to-all-start.3 = ((f32[16,2,1280]{2,1,0:T(2,128)}), f32[16,2,1280]{2,1,0:T(2,128)S(1)}, u32[]{:S(2)}, u32[]{:S(2)}) async-start(f32[16,2,1280]{2,1,0:T(2,128)} %reshape.105), calls=%async_computation.3 | async-start | bytes 327680 | tf_op jit(solution)/shard_map/all_to_all | solution.py:299
  104.8 6.9 %all-gather.2.cloned.1.call-done = bf16[1280,2560]{1,0:T(8,128)(2,1)} async-done(((bf16[40,2560]{1,0:T(8,128)(2,1)}), bf16[1280,2560]{1,0:T(8,128)(2,1)}) %all-gather.2.cloned.1.call-update) | async-done | bytes 6553616 | tf_op jit(solution)/shard_map/all_gather | solution.py:240
  111.7 4.0 %fusion.2 = f32[128,1280]{1,0:T(8,128)} fusion(bf16[128,1280]{1,0:T(8,128)(2,1)S(1)} %collective-permute-done.6, bf16[1280,2560]{1,0:T(8,128)(2,1)} %all-gather.2.cloned.1.call-done), kind=kOutput, calls=%fused_computation.2 | convolution fusion | flops 419430400 | bytes 4259840 | tf_op jit(solution)/shard_map/tc,rc->tr/dot_general | solution.py:45
  119.4 4.4 %all-to-all-start.4 = ((f32[8,2,1280]{2,1,0:T(2,128)}), f32[8,2,1280]{2,1,0:T(2,128)S(1)}, u32[]{:S(2)}, u32[]{:S(2)}) async-start(f32[8,2,1280]{2,1,0:T(2,128)} %broadcast_in_dim.68), calls=%async_computation.4 | async-start | bytes 163840 | tf_op jit(solution)/shard_map/all_to_all | solution.py:41
  124.0 7.1 %all-to-all-done.4 = f32[8,2,1280]{2,1,0:T(2,128)S(1)} async-done(((f32[8,2,1280]{2,1,0:T(2,128)}), f32[8,2,1280]{2,1,0:T(2,128)S(1)}, u32[]{:S(2)}, u32[]{:S(2)}) %all-to-all-start.4) | async-done | bytes 81952 | tf_op jit(solution)/shard_map/all_to_all | solution.py:41
  135.1 4.3 %all-to-all-done.5 = f32[4,2,1280]{2,1,0:T(2,128)S(1)} async-done(((f32[4,2,1280]{2,1,0:T(2,128)}), f32[4,2,1280]{2,1,0:T(2,128)S(1)}, u32[]{:S(2)}, u32[]{:S(2)}) %all-to-all-start.5) | async-done | bytes 40992 | tf_op jit(solution)/shard_map/all_to_all | solution.py:41
  143.4 10.2 %all-to-all-start.7 = ((f32[16,1,1280]{2,1,0:T(1,128)}), f32[16,1,1280]{2,1,0:T(1,128)S(1)}, u32[]{:S(2)}, u32[]{:S(2)}) async-start(f32[16,1,1280]{2,1,0:T(1,128)} %broadcast_in_dim.71), calls=%async_computation.7 | async-start | bytes 163840 | tf_op jit(solution)/shard_map/all_to_all | solution.py:41
  153.5 8.1 %all-to-all-done.7 = f32[16,1,1280]{2,1,0:T(1,128)S(1)} async-done(((f32[16,1,1280]{2,1,0:T(1,128)}), f32[16,1,1280]{2,1,0:T(1,128)S(1)}, u32[]{:S(2)}, u32[]{:S(2)}) %all-to-all-start.7) | async-done | bytes 81952 | tf_op jit(solution)/shard_map/all_to_all | solution.py:41
  165.7 6.9 %all-to-all-done.8 = f32[8,1,1280]{2,1,0:T(1,128)S(1)} async-done(((f32[8,1,1280]{2,1,0:T(1,128)}), f32[8,1,1280]{2,1,0:T(1,128)S(1)}, u32[]{:S(2)}, u32[]{:S(2)}) %all-to-all-start.8) | async-done | bytes 40992 | tf_op jit(solution)/shard_map/all_to_all | solution.py:41
  173.3 4.5 %all-to-all-start.6 = ((f32[16,2,1280]{2,1,0:T(2,128)}), f32[16,2,1280]{2,1,0:T(2,128)S(1)}, u32[]{:S(2)}, u32[]{:S(2)}) async-start(f32[16,2,1280]{2,1,0:T(2,128)} %broadcast_in_dim.70), calls=%async_computation.6 | async-start | bytes 327680 | tf_op jit(solution)/shard_map/all_to_all | solution.py:41
  178.2 9.5 %all-to-all-done.6 = f32[16,2,1280]{2,1,0:T(2,128)S(1)} async-done(((f32[16,2,1280]{2,1,0:T(2,128)}), f32[16,2,1280]{2,1,0:T(2,128)S(1)}, u32[]{:S(2)}, u32[]{:S(2)}) %all-to-all-start.6) | async-done | bytes 163872 | tf_op jit(solution)/shard_map/all_to_all | solution.py:41
  191.6 3.7 %fusion.6 = bf16[1280,128]{1,0:T(8,128)(2,1)} fusion(bf16[128,1280]{1,0:T(8,128)(2,1)S(1)} %fusion.18, bf16[1280,2560]{1,0:T(8,128)(2,1)} %all-gather.2.cloned.1.call-done), kind=kOutput, calls=%fused_computation.6 | convolution fusion | flops 419594240 | bytes 3932160 | tf_op jit(solution)/shard_map/rc,tc->rt/dot_general | solution.py:323
  196.1 3.7 %all-to-all-start.2 = ((bf16[16,80,128]{2,1,0:T(8,128)(2,1)}), bf16[16,80,128]{2,1,0:T(8,128)(2,1)S(1)}, u32[]{:S(2)}, u32[]{:S(2)}) async-start(bf16[16,80,128]{2,1,0:T(8,128)(2,1)} %bitcast.8), calls=%async_computation.2 | async-start | bytes 655360 | tf_op jit(solution)/shard_map/all_to_all | solution.py:325
  202.1 13.5 %attention_probs.1 = (bf16[8,2048,256]{2,1,0:T(8,128)(2,1)S(1)}, f32[80,2048]{1,0:T(8,128)S(1)}, f32[1,2048]{1,0:T(1,128)S(1)}) custom-call(s32[2,8]{1,0:T(2,128)S(1)} %pad_add_fusion.bounds, bf16[80,2048]{1,0:T(8,128)(2,1)S(1)} %bitcast.20, bf16[2048,80]{1,0:T(8,128)(2,1)S(1)} %copy.38.k, bf16[80,2048]{1,0:T(8,128)(2,1)S(1)} %bitcast.21, ...), custom_call_target="tpu_custom_call" | custom-call | flops 1342177280 | bytes 8388608 | tf_op jit(solution)/shard_map/attention_probs/pallas_call | solution.py:112
  223.7 14.7 %attention_grads.1 = (bf16[80,2048]{1,0:T(8,128)(2,1)}, bf16[80,2048]{1,0:T(8,128)(2,1)}, bf16[80,2048]{1,0:T(8,128)(2,1)}) custom-call(s32[2,8]{1,0:T(2,128)S(1)} %pad_add_fusion.bounds, bf16[8,2048,256]{2,1,0:T(8,128)(2,1)S(1)} %copy-done.2, bf16[16,80,128]{2,1,0:T(8,128)(2,1)S(1)} %all-to-all-done.2.ctx_t, f32[80,2048]{1,0:T(8,128)S(1)} %get-tuple-element.13.out_t, ...), custom_call_target="tpu_custom_call" | custom-call | flops 2684354560 | bytes 8388608 | tf_op jit(solution)/shard_map/attention_grads/pallas_call | solution.py:189
  (243 shorter events, 60.7 us)
Async XLA Ops:
  7.2 22.7 %copy-start.62 = (s32[1,8]{1,0:T(1,128)S(1)}, s32[1,8]{1,0:T(1,128)}, u32[]{:S(2)}) copy-start(s32[1,8]{1,0:T(1,128)} %param.18) | copy-start | bytes 100
  7.2 104.5 %all-gather.2.cloned.1.call-start = ((), (), s32[]{:S(2)}) async-start(), calls=%async_computation.10 | async-start | bytes 6758400 | tf_op jit(solution)/shard_map/all_gather | solution.py:240
  10.8 19.6 %all-to-all-start = ((bf16[8,40,640]{2,1,0:T(8,128)(2,1)}), bf16[8,40,640]{2,1,0:T(8,128)(2,1)S(1)}, u32[]{:S(2)}, u32[]{:S(2)}) async-start(bf16[8,40,640]{2,1,0:T(8,128)(2,1)} %broadcast_in_dim.58), calls=%async_computation | async-start | bytes 819200 | tf_op jit(solution)/shard_map/all_to_all | solution.py:41
  19.3 21.8 %copy-start.11 = (f32[31,1280]{1,0:T(8,128)S(1)}, f32[31,1280]{1,0:T(8,128)}, u32[]{:S(2)}) copy-start(f32[31,1280]{1,0:T(8,128)} %param.20) | copy-start | bytes 476164
  19.4 40.9 %collective-permute-start = (bf16[128,640]{1,0:T(8,128)(2,1)S(1)}, bf16[128,640]{1,0:T(8,128)(2,1)S(1)}, u32[]{:S(2)}, u32[]{:S(2)}) collective-permute-start(bf16[128,640]{1,0:T(8,128)(2,1)S(1)} %constant_dynamic-slice_fusion.6), channel_id=1, source_target_pairs={{0,1},{1,0},{2,3},{3,2},{4,5},{5,4},{6,7},{7,6},{8,9},{9,8},{10,11... | collective-permute-start | bytes 491528 | tf_op jit(solution)/shard_map/ppermute | solution.py:56
  24.9 40.3 %collective-permute-start.2 = (bf16[15,1280]{1,0:T(8,128)(2,1)}, bf16[15,1280]{1,0:T(8,128)(2,1)}, u32[]{:S(2)}, u32[]{:S(2)}) collective-permute-start(bf16[15,1280]{1,0:T(8,128)(2,1)} %get-tuple-element.93), channel_id=1, source_target_pairs={{0,1},{1,2},{2,3},{3,4},{4,5},{5,6},{6,7},{7,8},{8,9},{9,10},{10,1... | collective-permute-start | bytes 115208 | tf_op jit(solution)/shard_map/ppermute | solution.py:33
  27.1 38.2 %collective-permute-start.3 = (bf16[15,1280]{1,0:T(8,128)(2,1)}, bf16[15,1280]{1,0:T(8,128)(2,1)}, u32[]{:S(2)}, u32[]{:S(2)}) collective-permute-start(bf16[15,1280]{1,0:T(8,128)(2,1)} %get-tuple-element.94), channel_id=1, source_target_pairs={{1,0},{2,1},{3,2},{4,3},{5,4},{6,5},{7,6},{8,7},{9,8},{10,9},{11,1... | collective-permute-start | bytes 115208 | tf_op jit(solution)/shard_map/ppermute | solution.py:34
  31.7 28.0 %all-to-all-start.1 = ((bf16[4,8,40,640]{3,2,1,0:T(8,128)(2,1)}), bf16[4,8,40,640]{3,2,1,0:T(8,128)(2,1)S(1)}, u32[]{:S(2)}, u32[]{:S(2)}) async-start(bf16[4,8,40,640]{3,2,1,0:T(8,128)(2,1)} %broadcast_in_dim.59), calls=%async_computation.1 | async-start | bytes 3276800 | tf_op jit(solution)/shard_map/all_to_all | solution.py:41
  42.0 24.1 %copy-start.9 = (bf16[128,1280]{1,0:T(8,128)(2,1)S(1)}, bf16[128,1280]{1,0:T(8,128)(2,1)}, u32[]{:S(2)}) copy-start(bf16[128,1280]{1,0:T(8,128)(2,1)} %param.12) | copy-start | bytes 983044
  60.8 5.9 %collective-permute-start.1 = (f32[128,1280]{1,0:T(8,128)S(1)}, f32[128,1280]{1,0:T(8,128)S(1)}, u32[]{:S(2)}, u32[]{:S(2)}) collective-permute-start(f32[128,1280]{1,0:T(8,128)S(1)} %fusion.101), channel_id=1, source_target_pairs={{0,1},{1,0},{2,3},{3,2},{4,5},{5,4},{6,7},{7,6},{8,9},{9,8},{10,11... | collective-permute-start | bytes 1966088 | tf_op jit(solution)/shard_map/ppermute | solution.py:56
  71.7 6.1 %collective-permute-start.4 = (bf16[15,1280]{1,0:T(8,128)(2,1)S(1)}, bf16[15,1280]{1,0:T(8,128)(2,1)S(1)}, u32[]{:S(2)}, u32[]{:S(2)}) collective-permute-start(bf16[15,1280]{1,0:T(8,128)(2,1)S(1)} %get-tuple-element.91), channel_id=1, source_target_pairs={{0,1},{1,2},{2,3},{3,4},{4,5},{5,6},{6,7},{7,8},{8,9},{9,10},{10,1... | collective-permute-start | bytes 115208 | tf_op jit(solution)/shard_map/ppermute | solution.py:33
  75.9 5.7 %collective-permute-start.5 = (bf16[15,1280]{1,0:T(8,128)(2,1)S(1)}, bf16[15,1280]{1,0:T(8,128)(2,1)S(1)}, u32[]{:S(2)}, u32[]{:S(2)}) collective-permute-start(bf16[15,1280]{1,0:T(8,128)(2,1)S(1)} %get-tuple-element.92), channel_id=1, source_target_pairs={{1,0},{2,1},{3,2},{4,3},{5,4},{6,5},{7,6},{8,7},{9,8},{10,9},{11,1... | collective-permute-start | bytes 115208 | tf_op jit(solution)/shard_map/ppermute | solution.py:34
  90.7 14.1 %collective-permute-start.6 = (bf16[128,1280]{1,0:T(8,128)(2,1)S(1)}, bf16[128,1280]{1,0:T(8,128)(2,1)S(1)}, u32[]{:S(2)}, u32[]{:S(2)}) collective-permute-start(bf16[128,1280]{1,0:T(8,128)(2,1)S(1)} %pad_maximum_fusion), channel_id=1, source_target_pairs={{0,1},{1,0},{2,3},{3,2},{4,5},{5,4},{6,7},{7,6},{8,9},{9,8},{10,11... | collective-permute-start | bytes 983048 | tf_op jit(solution)/shard_map/ppermute | solution.py:56
  93.6 24.9 %copy-start.8 = (bf16[128,1280]{1,0:T(8,128)(2,1)S(1)}, bf16[128,1280]{1,0:T(8,128)(2,1)}, u32[]{:S(2)}) copy-start(bf16[128,1280]{1,0:T(8,128)(2,1)} %param.13) | copy-start | bytes 983044
  94.8 44.6 %copy-start.59 = (f32[1280]{0:T(1024)S(1)}, f32[1280]{0:T(1024)}, u32[]{:S(2)}) copy-start(f32[1280]{0:T(1024)} %param.19) | copy-start | bytes 15364
  94.8 23.9 %all-to-all-start.3 = ((f32[16,2,1280]{2,1,0:T(2,128)}), f32[16,2,1280]{2,1,0:T(2,128)S(1)}, u32[]{:S(2)}, u32[]{:S(2)}) async-start(f32[16,2,1280]{2,1,0:T(2,128)} %reshape.105), calls=%async_computation.3 | async-start | bytes 327680 | tf_op jit(solution)/shard_map/all_to_all | solution.py:299
  115.7 23.7 %collective-permute-start.7 = (f32[128,1280]{1,0:T(8,128)}, f32[128,1280]{1,0:T(8,128)S(1)}, u32[]{:S(2)}, u32[]{:S(2)}) collective-permute-start(f32[128,1280]{1,0:T(8,128)} %fusion.2), channel_id=1, source_target_pairs={{0,1},{1,0},{2,3},{3,2},{4,5},{5,4},{6,7},{7,6},{8,9},{9,8},{10,11... | collective-permute-start | bytes 1966088 | tf_op jit(solution)/shard_map/ppermute | solution.py:56
  119.4 11.7 %all-to-all-start.4 = ((f32[8,2,1280]{2,1,0:T(2,128)}), f32[8,2,1280]{2,1,0:T(2,128)S(1)}, u32[]{:S(2)}, u32[]{:S(2)}) async-start(f32[8,2,1280]{2,1,0:T(2,128)} %broadcast_in_dim.68), calls=%async_computation.4 | async-start | bytes 163840 | tf_op jit(solution)/shard_map/all_to_all | solution.py:41
  131.8 7.6 %all-to-all-start.5 = ((f32[4,2,1280]{2,1,0:T(2,128)}), f32[4,2,1280]{2,1,0:T(2,128)S(1)}, u32[]{:S(2)}, u32[]{:S(2)}) async-start(f32[4,2,1280]{2,1,0:T(2,128)} %broadcast_in_dim.69), calls=%async_computation.5 | async-start | bytes 81920 | tf_op jit(solution)/shard_map/all_to_all | solution.py:41
  143.4 18.3 %all-to-all-start.7 = ((f32[16,1,1280]{2,1,0:T(1,128)}), f32[16,1,1280]{2,1,0:T(1,128)S(1)}, u32[]{:S(2)}, u32[]{:S(2)}) async-start(f32[16,1,1280]{2,1,0:T(1,128)} %broadcast_in_dim.71), calls=%async_computation.7 | async-start | bytes 163840 | tf_op jit(solution)/shard_map/all_to_all | solution.py:41
  162.4 10.2 %all-to-all-start.8 = ((f32[8,1,1280]{2,1,0:T(1,128)}), f32[8,1,1280]{2,1,0:T(1,128)S(1)}, u32[]{:S(2)}, u32[]{:S(2)}) async-start(f32[8,1,1280]{2,1,0:T(1,128)} %broadcast_in_dim.72), calls=%async_computation.8 | async-start | bytes 81920 | tf_op jit(solution)/shard_map/all_to_all | solution.py:41
  173.3 14.4 %all-to-all-start.6 = ((f32[16,2,1280]{2,1,0:T(2,128)}), f32[16,2,1280]{2,1,0:T(2,128)S(1)}, u32[]{:S(2)}, u32[]{:S(2)}) async-start(f32[16,2,1280]{2,1,0:T(2,128)} %broadcast_in_dim.70), calls=%async_computation.6 | async-start | bytes 327680 | tf_op jit(solution)/shard_map/all_to_all | solution.py:41
  188.3 7.8 %all-to-all-start.9 = ((f32[4,1,1280]{2,1,0:T(1,128)}), f32[4,1,1280]{2,1,0:T(1,128)S(1)}, u32[]{:S(2)}, u32[]{:S(2)}) async-start(f32[4,1,1280]{2,1,0:T(1,128)} %broadcast_in_dim.73), calls=%async_computation.9 | async-start | bytes 40960 | tf_op jit(solution)/shard_map/all_to_all | solution.py:41
  196.1 24.2 %all-to-all-start.2 = ((bf16[16,80,128]{2,1,0:T(8,128)(2,1)}), bf16[16,80,128]{2,1,0:T(8,128)(2,1)S(1)}, u32[]{:S(2)}, u32[]{:S(2)}) async-start(bf16[16,80,128]{2,1,0:T(8,128)(2,1)} %bitcast.8), calls=%async_computation.2 | async-start | bytes 655360 | tf_op jit(solution)/shard_map/all_to_all | solution.py:325
  (58 other events, 388.6 us)
Sparse Core Ops, SparseCore 0:
  11.8 99.8 all-gather.1

commit v2 on v1

--- a/solution.py
+++ b/solution.py
@@ -58,8 +58,8 @@
 
 def pair_product(own, away, piece):
     other = swap(away)
-    back = swap(row_product(other, piece))
-    return row_product(own, piece) + back
+    back = swap(row_product(other, piece).astype(jnp.bfloat16))
+    return row_product(own, piece) + back.astype(jnp.float32)
 
 
 def probs_kernel(bounds, q_t, k, v_t, lo, hi, probs, out_t, inv_sum, scores):
@@ -143,16 +143,19 @@
     )(bounds, q_t, keys, v_t, lo, hi)
 
 
-def grads_kernel(bounds, probs, ctx_t, out_t, inv_sum, q, k_t, v, dq_t, dk_t, dv_t, dk_acc, dv_acc):
+def grads_kernel(begin, bounds, probs, ctx_t, out_t, inv_sum, q, k_t, v, *refs):
+    carried = begin > 0
+    dk_in, dv_in = refs[:2] if carried else (None, None)
+    dq_t, dk_t, dv_t, dk_acc, dv_acc = refs[-5:]
     scale = 1.0 / math.sqrt(HD)
-    block = pl.program_id(0)
-    first = bounds[0, block]
-    last = bounds[1, block]
-
-    @pl.when(block == 0)
+    step_id = pl.program_id(0)
+    first = bounds[0, begin + step_id]
+    last = bounds[1, begin + step_id]
+
+    @pl.when(step_id == 0)
     def _():
-        dk_acc[...] = jnp.zeros_like(dk_acc)
-        dv_acc[...] = jnp.zeros_like(dv_acc)
+        dk_acc[...] = dk_in[...] if carried else jnp.zeros_like(dk_acc)
+        dv_acc[...] = dv_in[...] if carried else jnp.zeros_like(dv_acc)
 
     pieces = [ctx_t[i].astype(jnp.float32) for i in range(ctx_t.shape[0])]
     grad_t = jnp.concatenate(pieces, axis=1) * inv_sum[...]
@@ -173,45 +176,61 @@
     acc = lax.fori_loop(first, last, step, jnp.zeros((HD, query.shape[0]), jnp.float32))
     dq_t[...] = (acc * scale).astype(jnp.bfloat16)
 
-    @pl.when(block == pl.num_programs(0) - 1)
+    @pl.when(step_id == pl.num_programs(0) - 1)
     def _():
-        dk_t[...] = (dk_acc[...] * scale).T.astype(jnp.bfloat16)
-        dv_t[...] = dv_acc[...].T.astype(jnp.bfloat16)
-
-
-def attention_grads(bounds, probs, ctx_t, out_t, inv_sum, queries, k_t, values):
+        if dk_t.shape[0] == HD:
+            dk_t[...] = (dk_acc[...] * scale).T.astype(jnp.bfloat16)
+            dv_t[...] = dv_acc[...].T.astype(jnp.bfloat16)
+        else:
+            dk_t[...] = dk_acc[...]
+            dv_t[...] = dv_acc[...]
+
+
+def attention_grads(begin, end, bounds, probs, ctx_t, out_t, inv_sum, queries, k_t, values, *sums):
     total = queries.shape[0]
     n = total // BLK
     per = BLK // ctx_t.shape[2]
-    lanes = lambda rows: pl.BlockSpec((rows, BLK), lambda i, b: (0, i))
+    lanes = lambda rows: pl.BlockSpec((rows, BLK), lambda i, b: (0, i + begin))
     whole = lambda shape: pl.BlockSpec(shape, lambda i, b: (0, 0))
-    shape = jax.ShapeDtypeStruct((HD, total), jnp.bfloat16)
+    if end == n:
+        shape = jax.ShapeDtypeStruct((HD, total), jnp.bfloat16)
+    else:
+        shape = jax.ShapeDtypeStruct((total, HD), jnp.float32)
     return pl.pallas_call(
-        grads_kernel,
+        lambda *refs: grads_kernel(begin, *refs),
         grid_spec=pltpu.PrefetchScalarGridSpec(
             num_scalar_prefetch=1,
-            grid=(n,),
+            grid=(end - begin,),
             in_specs=[
-                pl.BlockSpec((None, total, BLK), lambda i, b: (i, 0, 0)),
-                pl.BlockSpec((per, HD, ctx_t.shape[2]), lambda i, b: (i, 0, 0)),
+                pl.BlockSpec((None, total, BLK), lambda i, b: (i + begin, 0, 0)),
+                pl.BlockSpec((per, HD, ctx_t.shape[2]), lambda i, b: (i + begin, 0, 0)),
                 lanes(HD),
                 lanes(1),
-                pl.BlockSpec((BLK, HD), lambda i, b: (i, 0)),
+                pl.BlockSpec((BLK, HD), lambda i, b: (i + begin, 0)),
                 whole((HD, total)),
                 whole((total, HD)),
+            ]
+            + [whole((total, HD))] * len(sums),
+            out_specs=[
+                pl.BlockSpec((HD, BLK), lambda i, b: (0, i)),
+                whole(shape.shape),
+                whole(shape.shape),
             ],
-            out_specs=[lanes(HD), whole((HD, total)), whole((HD, total))],
             scratch_shapes=[pltpu.VMEM((total, HD), jnp.float32)] * 2,
         ),
-        out_shape=[shape, shape, shape],
+        out_shape=[
+            jax.ShapeDtypeStruct((HD, (end - begin) * BLK), jnp.bfloat16),
+            shape,
+            shape,
+        ],
         compiler_params=pltpu.CompilerParams(vmem_limit_bytes=32 << 20),
         cost_estimate=pl.CostEstimate(
-            flops=2 * total * total * HD * 4,
+            flops=2 * total * BLK * (end - begin) * HD * 4,
             transcendentals=0,
-            bytes_accessed=total * total * 2,
+            bytes_accessed=total * BLK * (end - begin) * 2,
         ),
         name="attention_grads",
-    )(bounds, probs, ctx_t, out_t, inv_sum, queries, k_t, values)
+    )(bounds, probs, ctx_t, out_t, inv_sum, queries, k_t, values, *sums)
 
 
 def local(
@@ -240,20 +259,20 @@
     gathered = lax.all_gather(
         jnp.concatenate([in_low, in_high, w_attn_out], axis=1), GROUPS, axis=0, tiled=True
     )
-    w_in_half = gathered[:, :width]
-    w_attn = gathered[:, width:]
-
-    conv_half, _ = halves(w_conv_out, core)
-    by_y = spread(conv_half, "y")
-    by_xy = spread(by_y, "x")
-    w_conv_half = by_xy.transpose(1, 0, 2, 3).reshape(width, width // 2)
 
     positions = jnp.arange(total, dtype=jnp.int32)
     passed = positions[None, :] >= ends[:, None]
     lo = jnp.max(jnp.where(passed, ends[:, None], 0), axis=0, keepdims=True)
     hi = jnp.min(jnp.where(passed, total, ends[:, None]), axis=0, keepdims=True)
     bounds = jnp.stack([lo[0, ::BLK] // BLK, (hi[0, BLK - 1 :: BLK] + BLK - 1) // BLK])
+
+    conv_half, _ = halves(w_conv_out, core)
+    by_y = spread(conv_half, "y")
+    by_y, lo = lax.optimization_barrier((by_y, lo))
+    by_xy = spread(by_y, "x")
     probs, out_t, inv_sum = attention_probs(bounds, queries.T, keys, values.T, lo, hi)
+    by_xy, probs = lax.optimization_barrier((by_xy, probs))
+    w_conv_half = by_xy.transpose(1, 0, 2, 3).reshape(width, width // 2)
 
     seq_index = lax.axis_index(TIME)
     ext_pos = seq_index * t_dev + jnp.arange(-half, t_dev + half, dtype=jnp.int32)
@@ -300,10 +319,10 @@
         rows.reshape(n_seq, (KW + 1) // n_seq, width), TIME, split_axis=0, concat_axis=0
     )
     rows = jnp.sum(rows, axis=0)
-    for axis in GROUPS:
-        rows = jnp.sum(spread(rows, axis), axis=0)
-    kernel_grad = spread(rows, TIME).reshape(KW + 1, width)[:KW]
-
+
+    gathered, rows = lax.optimization_barrier((gathered, rows))
+    w_in_half = gathered[:, :width]
+    w_attn = gathered[:, width:]
     norm_grad = pair_product(
         jnp.concatenate([low_own, high_own], axis=1),
         jnp.concatenate([low_away, high_away], axis=1),
@@ -322,15 +341,27 @@
     resid_grad = (grad_out.astype(jnp.float32) + input_grad).astype(jnp.bfloat16)
     ctx_t = jnp.einsum("rc,tc->rt", w_attn, resid_grad, preferred_element_type=jnp.float32)
     ctx_t = ctx_t.astype(jnp.bfloat16).reshape(n_seq, HD, t_dev)
+    gain = jnp.sum(norm_grad * normed, axis=0, keepdims=True)
+    ctx_t, gain = lax.optimization_barrier((ctx_t, gain))
     ctx_t = lax.all_to_all(ctx_t, TIME, split_axis=0, concat_axis=0)
-    grads = attention_grads(
-        bounds, probs, ctx_t, out_t, inv_sum, queries, keys.T, values
-    )
-    query_grad, key_grad, value_grad = [array.T for array in grads]
-    gain = jnp.sum(norm_grad * normed, axis=0, keepdims=True)
-    for axis in (TIME,) + GROUPS:
-        gain = jnp.sum(spread(gain, axis), axis=0)
-    return (resid_grad, query_grad, key_grad, value_grad, kernel_grad, gain[0])
+    sums = jnp.concatenate([rows, gain], axis=0)
+    fixed = (bounds, probs, ctx_t, out_t, inv_sum, queries, keys.T, values)
+    n = total // BLK
+    cuts = [0, 3 * n // 8, 6 * n // 8, n]
+    parts = []
+    acc = ()
+    for stage, axis in enumerate(GROUPS + (TIME,)):
+        stacked = spread(sums, axis)
+        part, *acc = attention_grads(cuts[stage], cuts[stage + 1], *fixed, *acc)
+        parts.append(part)
+        if stage < 2:
+            stacked, *acc = lax.optimization_barrier((stacked, *acc))
+            sums = jnp.sum(stacked, axis=0)
+    query_grad = jnp.concatenate(parts, axis=1).T
+    key_grad, value_grad = [array.T for array in acc]
+    kernel_grad = stacked[:, :-1].reshape(KW + 1, width)[:KW]
+    gain_grad = jnp.sum(stacked[:, -1], axis=0)
+    return (resid_grad, query_grad, key_grad, value_grad, kernel_grad, gain_grad)
 
 
 def solution(mesh):

time: 247 us -> 219 us (0.89)
  the two profiles are of different devices: /device:TPU:1 before, /device:TPU:19 now
where the time goes in v2:
time: 219 us; the launch traced here: 217 us
  starting transfers between devices  65 us (30%)
  local copies, waits for them, and re-layouts  38.1 us (17%)
  other arithmetic  34.8 us (16%)
  Pallas kernels  31.3 us (14%)
  waiting for transfers between devices  22.6 us (10%)
  between operations  16 us (7%)
  matrix products  9.71 us (4%)
    all_to_all x5, starting transfers between devices, spread(): return lax.all_to_all(copies, axis, split_axis=0, concat_axis=0)  27.3 us
    unnamed x201, local copies, waits for them, and re-layouts  22.7 us
    pallas_call x3, Pallas kernels, attention_grads(): pl.pallas_call(lambda *refs: grads_kernel(begin, *refs), grid_spec=pltpu....  17 us
    convert_element_type x1, other arithmetic, local(): low_grad = (glu_grad * gate_sig).astype(jnp.bfloat16)  14.6 us
    pallas_call x1, Pallas kernels, attention_probs(): pl.pallas_call(probs_kernel, grid_spec=pltpu.PrefetchScalarGridSpec(num_s...  14.3 us
    all_to_all x1, waiting for transfers between devices, local(): ctx_t = lax.all_to_all(ctx_t, TIME, split_axis=0, concat_axis=0)  13.1 us
    ppermute x4, starting transfers between devices, swap(): return lax.ppermute(array, 'core', [(0, 1), (1, 0)])  9.92 us
    all_to_all x1, starting transfers between devices, local(): lax.all_to_all(rows.reshape(n_seq, (KW + 1) // n_seq, width), TIME, split...  9.6 us
  transfers between devices with their start and end apart: 16, of which 6 were waited for; matrix products, arithmetic and copies ran while one was open for 20% of the time, Pallas kernels for 14%

profile of v2, /device:TPU:19, one launch (start us, length us, event | category | flops | bytes accessed | tf_op | source)
XLA Modules:
  0.0 217.4 jit_solution(7908980865662752541)
XLA Ops:
  10.7 6.9 %all-to-all-start = ((bf16[8,40,640]{2,1,0:T(8,128)(2,1)}), bf16[8,40,640]{2,1,0:T(8,128)(2,1)S(1)}, u32[]{:S(2)}, u32[]{:S(2)}) async-start(bf16[8,40,640]{2,1,0:T(8,128)(2,1)} %broadcast_in_dim.54), calls=%async_computation | async-start | bytes 819200 | tf_op jit(solution)/shard_map/all_to_all | solution.py:41
  19.2 3.3 %collective-permute-start = (bf16[128,640]{1,0:T(8,128)(2,1)}, bf16[128,640]{1,0:T(8,128)(2,1)S(1)}, u32[]{:S(2)}, u32[]{:S(2)}) collective-permute-start(bf16[128,640]{1,0:T(8,128)(2,1)} %constant_dynamic-slice_fusion.6), channel_id=1, source_target_pairs={{0,1},{1,0},{2,3},{3,2},{4,5},{5,4},{6,7},{7,6},{8,9},{9,8},{10,11... | collective-permute-start | bytes 491528 | tf_op jit(solution)/shard_map/ppermute | solution.py:56
  23.3 3.9 %collective-permute-start.2 = (bf16[15,1280]{1,0:T(8,128)(2,1)}, bf16[15,1280]{1,0:T(8,128)(2,1)}, u32[]{:S(2)}, u32[]{:S(2)}) collective-permute-start(bf16[15,1280]{1,0:T(8,128)(2,1)} %get-tuple-element.133), channel_id=1, source_target_pairs={{0,1},{1,2},{2,3},{3,4},{4,5},{5,6},{6,7},{7,8},{8,9},{9,10},{10,1... | collective-permute-start | bytes 115208 | tf_op jit(solution)/shard_map/ppermute | solution.py:33
  32.0 5.3 %all-to-all-start.1 = ((bf16[4,8,40,640]{3,2,1,0:T(8,128)(2,1)}), bf16[4,8,40,640]{3,2,1,0:T(8,128)(2,1)}, u32[]{:S(2)}, u32[]{:S(2)}) async-start(bf16[4,8,40,640]{3,2,1,0:T(8,128)(2,1)} %broadcast_in_dim.60), calls=%async_computation.1 | async-start | bytes 3276800 | tf_op jit(solution)/shard_map/all_to_all | solution.py:41
  41.1 14.3 %attention_probs.1 = (bf16[8,2048,256]{2,1,0:T(8,128)(2,1)S(1)}, f32[80,2048]{1,0:T(8,128)S(1)}, f32[1,2048]{1,0:T(1,128)S(1)}) custom-call(s32[2,8]{1,0:T(2,128)S(1)} %pad_add_fusion.bounds.refs_0_, bf16[80,2048]{1,0:T(8,128)(2,1)S(1)} %bitcast.23, bf16[2048,80]{1,0:T(8,128)(2,1)S(1)} %copy.48.k, bf16[80,2048]{1,0:T(8,128)(2,1)S(1)} %bitcast.24, ...), custom_call_target="tpu_custom_call" | custom-call | flops 1342177280 | bytes 8388608 | tf_op jit(solution)/shard_map/attention_probs/pallas_call | solution.py:112
  55.4 3.2 %copy-done.1 = bf16[8,2048,256]{2,1,0:T(8,128)(2,1)} copy-done((bf16[8,2048,256]{2,1,0:T(8,128)(2,1)}, bf16[8,2048,256]{2,1,0:T(8,128)(2,1)S(1)}, u32[]{:S(2)}) %copy-start.1) | copy-done | bytes 8388632
  66.1 4.7 %multiply_convert_fusion.1 = bf16[128,1280]{1,0:T(8,128)(2,1)S(1)} fusion(f32[128,1280]{1,0:T(8,128)S(1)} %fusion.95, bf16[128,1280]{1,0:T(8,128)(2,1)S(1)} %collective-permute-done.1, f32[158,1280]{1,0:T(8,128)S(1)} %maximum_convert_fusion, f32[128]{0:T(128)S(1)} %copy-done.47, f32[1280]{0:T(1024)S(1)} %copy-done.43, f32[128]{0:T(128)S(1)} %copy-done.53, ...), kind=kLoop, calls=%fused_computation.152 | loop fusion | flops 16711680 | bytes 21800960 | tf_op jit(solution)/shard_map/convert_element_type | solution.py:297
  76.0 3.8 %collective-permute-done.5 = bf16[15,1280]{1,0:T(8,128)(2,1)S(1)} collective-permute-done((bf16[15,1280]{1,0:T(8,128)(2,1)S(1)}, bf16[15,1280]{1,0:T(8,128)(2,1)S(1)}, u32[]{:S(2)}, u32[]{:S(2)}) %collective-permute-start.5) | collective-permute-done | bytes 38432 | tf_op jit(solution)/shard_map/ppermute | solution.py:34
  86.2 9.6 %all-to-all-start.2 = ((f32[16,2,1280]{2,1,0:T(2,128)}), f32[16,2,1280]{2,1,0:T(2,128)}, u32[]{:S(2)}, u32[]{:S(2)}) async-start(f32[16,2,1280]{2,1,0:T(2,128)} %reshape.89), calls=%async_computation.2 | async-start | bytes 327680 | tf_op jit(solution)/shard_map/all_to_all | solution.py:318
  96.0 14.6 %multiply_convert_fusion = (bf16[128,1280]{1,0:T(8,128)(2,1)S(1)}, f32[128,1280]{1,0:T(8,128)S(1)}) fusion(bf16[128,2560]{1,0:T(8,128)(2,1)S(1)} %copy-done.19, f32[128]{0:T(128)S(1)} %copy-done.50, f32[158,1280]{1,0:T(8,128)} %copy-done.18, f32[1280]{0:T(1024)S(1)} %copy-done.43, f32[128]{0:T(128)S(1)} %copy-done.52, f32[1280]{0:T(1024)S(1)} %copy-done.44, ...), kind=kLoop, calls=%fused_computation.151 | loop fusion | flops 15892480 | bytes 21800960 | tf_op jit(solution)/shard_map/convert_element_type | solution.py:312
  115.9 3.3 %fusion.6 = bf16[128,1280]{1,0:T(8,128)(2,1)S(1)} fusion(bf16[128,1280]{1,0:T(8,128)(2,1)S(1)} %collective-permute-done.6, bf16[1280,2560]{1,0:T(8,128)(2,1)} %all-gather.2.cloned.1.call-done), kind=kOutput, calls=%fused_computation.6 | convolution fusion | flops 419594240 | bytes 3932160 | tf_op jit(solution)/shard_map/tc,rc->tr/dot_general | solution.py:45
  122.7 3.5 %fusion.22 = (f32[1280]{0:T(1024)S(1)}, f32[128]{0:T(128)S(1)}, f32[128]{0:T(128)S(1)}, f32[128,1280]{1,0:T(8,128)S(1)}) fusion(bf16[128,1280]{1,0:T(8,128)(2,1)S(1)} %copy-done.20, f32[128]{0:T(128)S(1)} %add_rsqrt_fusion, f32[128]{0:T(128)S(1)} %broadcast_multiply_fusion.2, f32[1280]{0:T(1024)S(1)} %copy-done.95, ...), kind=kOutput, calls=%fused_computation.23 | convolution fusion | flops 421886464 | bytes 4927488 | tf_op jit(solution)/shard_map/tc,rc->tr/dot_general | solution.py:45
  128.4 7.2 %all-to-all-start.3 = ((bf16[16,80,128]{2,1,0:T(8,128)(2,1)}), bf16[16,80,128]{2,1,0:T(8,128)(2,1)S(1)}, u32[]{:S(2)}, u32[]{:S(2)}) async-start(bf16[16,80,128]{2,1,0:T(8,128)(2,1)} %bitcast.8), calls=%async_computation.3 | async-start | bytes 655360 | tf_op jit(solution)/shard_map/all_to_all | solution.py:346
  135.6 13.1 %all-to-all-done.3.refs_2_ = bf16[16,80,128]{2,1,0:T(8,128)(2,1)S(1)} async-done(((bf16[16,80,128]{2,1,0:T(8,128)(2,1)}), bf16[16,80,128]{2,1,0:T(8,128)(2,1)S(1)}, u32[]{:S(2)}, u32[]{:S(2)}) %all-to-all-start.3) | async-done | bytes 327712 | tf_op jit(solution)/shard_map/all_to_all | solution.py:346
  149.4 5.9 %all-to-all-start.4 = ((f32[8,3,1280]{2,1,0:T(4,128)}), f32[8,3,1280]{2,1,0:T(4,128)S(1)}, u32[]{:S(2)}, u32[]{:S(2)}) async-start(f32[8,3,1280]{2,1,0:T(4,128)} %broadcast_in_dim.65), calls=%async_computation.4 | async-start | bytes 327680 | tf_op jit(solution)/shard_map/all_to_all | solution.py:41
  155.9 3.4 %copy-done.2 = bf16[8,2048,256]{2,1,0:T(8,128)(2,1)S(1)} copy-done((bf16[8,2048,256]{2,1,0:T(8,128)(2,1)S(1)}, bf16[8,2048,256]{2,1,0:T(8,128)(2,1)}, u32[]{:S(2)}) %copy-start.2) | copy-done | bytes 8388632
  159.3 5.7 %attention_grads.3 = (bf16[80,768]{1,0:T(8,128)(2,1)S(1)}, f32[2048,80]{1,0:T(8,128)S(1)}, f32[2048,80]{1,0:T(8,128)S(1)}) custom-call(s32[2,8]{1,0:T(2,128)S(1)} %pad_add_fusion.bounds.refs_0_, bf16[8,2048,256]{2,1,0:T(8,128)(2,1)S(1)} %copy-done.2, bf16[16,80,128]{2,1,0:T(8,128)(2,1)S(1)} %all-to-all-done.3.refs_2_, ...), custom_call_target="tpu_custom_call" | custom-call | flops 1006632960 | bytes 3145728 | tf_op jit(solution)/shard_map/attention_grads/pallas_call | solution.py:199
  168.4 5.0 %all-to-all-start.5 = ((f32[4,3,1280]{2,1,0:T(4,128)}), f32[4,3,1280]{2,1,0:T(4,128)}, u32[]{:S(2)}, u32[]{:S(2)}) async-start(f32[4,3,1280]{2,1,0:T(4,128)} %broadcast_in_dim.66), calls=%async_computation.5 | async-start | bytes 163840 | tf_op jit(solution)/shard_map/all_to_all | solution.py:41
  173.4 3.4 %copy-done.3 = bf16[8,2048,256]{2,1,0:T(8,128)(2,1)S(1)} copy-done((bf16[8,2048,256]{2,1,0:T(8,128)(2,1)S(1)}, bf16[8,2048,256]{2,1,0:T(8,128)(2,1)}, u32[]{:S(2)}) %copy-start.3) | copy-done | bytes 8388632
  179.2 7.1 %attention_grads.4 = (bf16[80,768]{1,0:T(8,128)(2,1)S(1)}, f32[2048,80]{1,0:T(8,128)S(1)}, f32[2048,80]{1,0:T(8,128)S(1)}) custom-call(s32[2,8]{1,0:T(2,128)S(1)} %pad_add_fusion.bounds.refs_0_, bf16[8,2048,256]{2,1,0:T(8,128)(2,1)S(1)} %copy-done.3, bf16[16,80,128]{2,1,0:T(8,128)(2,1)S(1)} %all-to-all-done.3.refs_2_, ...), custom_call_target="tpu_custom_call" | custom-call | flops 1006632960 | bytes 3145728 | tf_op jit(solution)/shard_map/attention_grads/pallas_call | solution.py:199
  189.7 4.2 %all-to-all-start.6 = ((f32[16,3,1280]{2,1,0:T(4,128)}), f32[16,3,1280]{2,1,0:T(4,128)}, u32[]{:S(2)}, u32[]{:S(2)}) async-start(f32[16,3,1280]{2,1,0:T(4,128)} %broadcast_in_dim.67), calls=%async_computation.6 | async-start | bytes 655360 | tf_op jit(solution)/shard_map/all_to_all | solution.py:41
  193.9 3.4 %copy-done.4 = bf16[8,2048,256]{2,1,0:T(8,128)(2,1)S(1)} copy-done((bf16[8,2048,256]{2,1,0:T(8,128)(2,1)S(1)}, bf16[8,2048,256]{2,1,0:T(8,128)(2,1)}, u32[]{:S(2)}) %copy-start.4) | copy-done | bytes 8388632
  198.6 4.2 %attention_grads.5 = (bf16[80,512]{1,0:T(8,128)(2,1)S(1)}, bf16[80,2048]{1,0:T(8,128)(2,1)}, bf16[80,2048]{1,0:T(8,128)(2,1)}) custom-call(s32[2,8]{1,0:T(2,128)S(1)} %pad_add_fusion.bounds.refs_0_, bf16[8,2048,256]{2,1,0:T(8,128)(2,1)S(1)} %copy-done.4, bf16[16,80,128]{2,1,0:T(8,128)(2,1)S(1)} %all-to-all-done.3.refs_2_, ...), custom_call_target="tpu_custom_call" | custom-call | flops 671088640 | bytes 2097152 | tf_op jit(solution)/shard_map/attention_grads/pallas_call | solution.py:199
  203.5 3.6 %all-to-all-done.6 = f32[16,3,1280]{2,1,0:T(4,128)} async-done(((f32[16,3,1280]{2,1,0:T(4,128)}), f32[16,3,1280]{2,1,0:T(4,128)}, u32[]{:S(2)}, u32[]{:S(2)}) %all-to-all-start.6) | async-done | bytes 245792 | tf_op jit(solution)/shard_map/all_to_all | solution.py:41
  (312 shorter events, 59.1 us)
Async XLA Ops:
  7.2 15.3 %copy-start.19 = (bf16[128,2560]{1,0:T(8,128)(2,1)S(1)}, bf16[128,2560]{1,0:T(8,128)(2,1)}, u32[]{:S(2)}) copy-start(bf16[128,2560]{1,0:T(8,128)(2,1)} %param.14) | copy-start | bytes 1966084
  7.2 22.0 %copy-start.96 = (s32[1,8]{1,0:T(1,128)S(1)}, s32[1,8]{1,0:T(1,128)}, u32[]{:S(2)}) copy-start(s32[1,8]{1,0:T(1,128)} %param.18) | copy-start | bytes 100
  7.2 22.5 %copy-start.25 = (f32[31,1280]{1,0:T(8,128)S(1)}, f32[31,1280]{1,0:T(8,128)}, u32[]{:S(2)}) copy-start(f32[31,1280]{1,0:T(8,128)} %param.20) | copy-start | bytes 476164
  7.2 108.4 %all-gather.2.cloned.1.call-start = ((), (), s32[]{:S(2)}) async-start(), calls=%async_computation.7 | async-start | bytes 6758400 | tf_op jit(solution)/shard_map/all_gather | solution.py:259
  10.7 19.9 %all-to-all-start = ((bf16[8,40,640]{2,1,0:T(8,128)(2,1)}), bf16[8,40,640]{2,1,0:T(8,128)(2,1)S(1)}, u32[]{:S(2)}, u32[]{:S(2)}) async-start(bf16[8,40,640]{2,1,0:T(8,128)(2,1)} %broadcast_in_dim.54), calls=%async_computation | async-start | bytes 819200 | tf_op jit(solution)/shard_map/all_to_all | solution.py:41
  19.2 21.6 %copy-start.5 = (bf16[2048,80]{0,1:T(8,128)(2,1)S(1)}, bf16[2048,80]{0,1:T(8,128)(2,1)}, u32[]{:S(2)}) copy-start(bf16[2048,80]{0,1:T(8,128)(2,1)} %param.16) | copy-start | bytes 983044
  19.2 41.9 %collective-permute-start = (bf16[128,640]{1,0:T(8,128)(2,1)}, bf16[128,640]{1,0:T(8,128)(2,1)S(1)}, u32[]{:S(2)}, u32[]{:S(2)}) collective-permute-start(bf16[128,640]{1,0:T(8,128)(2,1)} %constant_dynamic-slice_fusion.6), channel_id=1, source_target_pairs={{0,1},{1,0},{2,3},{3,2},{4,5},{5,4},{6,7},{7,6},{8,9},{9,8},{10,11... | collective-permute-start | bytes 491528 | tf_op jit(solution)/shard_map/ppermute | solution.py:56
  23.3 40.9 %collective-permute-start.2 = (bf16[15,1280]{1,0:T(8,128)(2,1)}, bf16[15,1280]{1,0:T(8,128)(2,1)}, u32[]{:S(2)}, u32[]{:S(2)}) collective-permute-start(bf16[15,1280]{1,0:T(8,128)(2,1)} %get-tuple-element.133), channel_id=1, source_target_pairs={{0,1},{1,2},{2,3},{3,4},{4,5},{5,6},{6,7},{7,8},{8,9},{9,10},{10,1... | collective-permute-start | bytes 115208 | tf_op jit(solution)/shard_map/ppermute | solution.py:33
  27.2 37.0 %collective-permute-start.3 = (bf16[15,1280]{1,0:T(8,128)(2,1)}, bf16[15,1280]{1,0:T(8,128)(2,1)}, u32[]{:S(2)}, u32[]{:S(2)}) collective-permute-start(bf16[15,1280]{1,0:T(8,128)(2,1)} %get-tuple-element.134), channel_id=1, source_target_pairs={{1,0},{2,1},{3,2},{4,3},{5,4},{6,5},{7,6},{8,7},{9,8},{10,9},{11,1... | collective-permute-start | bytes 115208 | tf_op jit(solution)/shard_map/ppermute | solution.py:34
  32.0 27.2 %all-to-all-start.1 = ((bf16[4,8,40,640]{3,2,1,0:T(8,128)(2,1)}), bf16[4,8,40,640]{3,2,1,0:T(8,128)(2,1)}, u32[]{:S(2)}, u32[]{:S(2)}) async-start(bf16[4,8,40,640]{3,2,1,0:T(8,128)(2,1)} %broadcast_in_dim.60), calls=%async_computation.1 | async-start | bytes 3276800 | tf_op jit(solution)/shard_map/all_to_all | solution.py:41
  61.8 4.0 %collective-permute-start.1 = (bf16[128,1280]{1,0:T(8,128)(2,1)S(1)}, bf16[128,1280]{1,0:T(8,128)(2,1)S(1)}, u32[]{:S(2)}, u32[]{:S(2)}) collective-permute-start(bf16[128,1280]{1,0:T(8,128)(2,1)S(1)} %convolution_convert_fusion), channel_id=1, source_target_pairs={{0,1},{1,0},{2,3},{3,2},{4,5},{5,4},{6,7},{7,6},{8,9},{9,8},{10,11... | collective-permute-start | bytes 983048 | tf_op jit(solution)/shard_map/ppermute | solution.py:56
  70.8 5.2 %collective-permute-start.4 = (bf16[15,1280]{1,0:T(8,128)(2,1)S(1)}, bf16[15,1280]{1,0:T(8,128)(2,1)S(1)}, u32[]{:S(2)}, u32[]{:S(2)}) collective-permute-start(bf16[15,1280]{1,0:T(8,128)(2,1)S(1)} %get-tuple-element.131), channel_id=1, source_target_pairs={{0,1},{1,2},{2,3},{3,4},{4,5},{5,6},{6,7},{7,8},{8,9},{9,10},{10,1... | collective-permute-start | bytes 115208 | tf_op jit(solution)/shard_map/ppermute | solution.py:33
  74.1 5.7 %collective-permute-start.5 = (bf16[15,1280]{1,0:T(8,128)(2,1)S(1)}, bf16[15,1280]{1,0:T(8,128)(2,1)S(1)}, u32[]{:S(2)}, u32[]{:S(2)}) collective-permute-start(bf16[15,1280]{1,0:T(8,128)(2,1)S(1)} %get-tuple-element.132), channel_id=1, source_target_pairs={{1,0},{2,1},{3,2},{4,3},{5,4},{6,5},{7,6},{8,7},{9,8},{10,9},{11,1... | collective-permute-start | bytes 115208 | tf_op jit(solution)/shard_map/ppermute | solution.py:34
  83.9 11.9 %copy-start.46 = (f32[128]{0:T(128)S(1)}, f32[128]{0:T(128)}, u32[]{:S(2)}) copy-start(f32[128]{0:T(128)} %get-tuple-element.164) | copy-start | bytes 1540
  83.9 11.8 %copy-start.48 = (f32[128]{0:T(128)S(1)}, f32[128]{0:T(128)}, u32[]{:S(2)}) copy-start(f32[128]{0:T(128)} %get-tuple-element.165) | copy-start | bytes 1540
  83.9 11.8 %copy-start.50 = (f32[128]{0:T(128)S(1)}, f32[128]{0:T(128)}, u32[]{:S(2)}) copy-start(f32[128]{0:T(128)} %get-tuple-element.166) | copy-start | bytes 1540
  84.0 11.8 %copy-start.52 = (f32[128]{0:T(128)S(1)}, f32[128]{0:T(128)}, u32[]{:S(2)}) copy-start(f32[128]{0:T(128)} %get-tuple-element.137) | copy-start | bytes 1540
  86.2 28.4 %all-to-all-start.2 = ((f32[16,2,1280]{2,1,0:T(2,128)}), f32[16,2,1280]{2,1,0:T(2,128)}, u32[]{:S(2)}, u32[]{:S(2)}) async-start(f32[16,2,1280]{2,1,0:T(2,128)} %reshape.89), calls=%async_computation.2 | async-start | bytes 327680 | tf_op jit(solution)/shard_map/all_to_all | solution.py:318
  112.3 3.7 %collective-permute-start.6 = (bf16[128,1280]{1,0:T(8,128)(2,1)S(1)}, bf16[128,1280]{1,0:T(8,128)(2,1)S(1)}, u32[]{:S(2)}, u32[]{:S(2)}) collective-permute-start(bf16[128,1280]{1,0:T(8,128)(2,1)S(1)} %pad_maximum_fusion), channel_id=1, source_target_pairs={{0,1},{1,0},{2,3},{3,2},{4,5},{5,4},{6,7},{7,6},{8,9},{9,8},{10,11... | collective-permute-start | bytes 983048 | tf_op jit(solution)/shard_map/ppermute | solution.py:56
  119.2 3.5 %collective-permute-start.7 = (bf16[128,1280]{1,0:T(8,128)(2,1)S(1)}, bf16[128,1280]{1,0:T(8,128)(2,1)S(1)}, u32[]{:S(2)}, u32[]{:S(2)}) collective-permute-start(bf16[128,1280]{1,0:T(8,128)(2,1)S(1)} %fusion.6), channel_id=1, source_target_pairs={{0,1},{1,0},{2,3},{3,2},{4,5},{5,4},{6,7},{7,6},{8,9},{9,8},{10,11... | collective-permute-start | bytes 983048 | tf_op jit(solution)/shard_map/ppermute | solution.py:56
  128.4 20.3 %all-to-all-start.3 = ((bf16[16,80,128]{2,1,0:T(8,128)(2,1)}), bf16[16,80,128]{2,1,0:T(8,128)(2,1)S(1)}, u32[]{:S(2)}, u32[]{:S(2)}) async-start(bf16[16,80,128]{2,1,0:T(8,128)(2,1)} %bitcast.8), calls=%async_computation.3 | async-start | bytes 655360 | tf_op jit(solution)/shard_map/all_to_all | solution.py:346
  149.4 18.3 %all-to-all-start.4 = ((f32[8,3,1280]{2,1,0:T(4,128)}), f32[8,3,1280]{2,1,0:T(4,128)S(1)}, u32[]{:S(2)}, u32[]{:S(2)}) async-start(f32[8,3,1280]{2,1,0:T(4,128)} %broadcast_in_dim.65), calls=%async_computation.4 | async-start | bytes 327680 | tf_op jit(solution)/shard_map/all_to_all | solution.py:41
  168.4 19.7 %all-to-all-start.5 = ((f32[4,3,1280]{2,1,0:T(4,128)}), f32[4,3,1280]{2,1,0:T(4,128)}, u32[]{:S(2)}, u32[]{:S(2)}) async-start(f32[4,3,1280]{2,1,0:T(4,128)} %broadcast_in_dim.66), calls=%async_computation.5 | async-start | bytes 163840 | tf_op jit(solution)/shard_map/all_to_all | solution.py:41
  189.7 17.3 %all-to-all-start.6 = ((f32[16,3,1280]{2,1,0:T(4,128)}), f32[16,3,1280]{2,1,0:T(4,128)}, u32[]{:S(2)}, u32[]{:S(2)}) async-start(f32[16,3,1280]{2,1,0:T(4,128)} %broadcast_in_dim.67), calls=%async_computation.6 | async-start | bytes 655360 | tf_op jit(solution)/shard_map/all_to_all | solution.py:41
  (91 other events, 541.9 us)
Sparse Core Ops, SparseCore 0:
  11.8 96.8 all-gather.1

commit v3 on v2

--- a/solution.py
+++ b/solution.py
@@ -11,6 +11,8 @@
 HD = 80
 KW = 31
 BLK = 256
+HALO = 16
+LANES = 128
 TIME = ("z", "core")
 GROUPS = ("y", "x")
 
@@ -60,6 +62,113 @@
     other = swap(away)
     back = swap(row_product(other, piece).astype(jnp.bfloat16))
     return row_product(own, piece) + back.astype(jnp.float32)
+
+
+def fill_matches(seg, matches):
+    rows = matches.shape[1]
+    own = seg[pl.ds(HALO, rows), :]
+    for tap in range(KW):
+        there = seg[pl.ds(tap + HALO - KW // 2, rows), :]
+        matches[tap] = jnp.where(there == own, 1.0, 0.0)
+
+
+def conv_kernel(seg, glu, taps, factor, matches, wide):
+    rows = factor.shape[0]
+
+    @pl.when(pl.program_id(0) == 0)
+    def _():
+        fill_matches(seg, matches)
+
+    wide[...] = glu[...].astype(jnp.float32)
+    out = jnp.zeros(factor.shape, jnp.float32)
+    for tap in range(KW):
+        seen = wide[pl.ds(tap + HALO - KW // 2, rows), :] * matches[tap]
+        out = out + taps[pl.ds(tap, 1), :] * seen
+    sig = 1.0 / (1.0 + jnp.exp(-out))
+    factor[...] = sig * (1.0 + out * (1.0 - sig))
+
+
+def conv_factor(seg, glu_ext, taps):
+    ext, width = glu_ext.shape
+    rows = ext - 2 * HALO
+    lanes = lambda count: pl.BlockSpec((count, LANES), lambda i: (0, i))
+    return pl.pallas_call(
+        conv_kernel,
+        grid=(width // LANES,),
+        in_specs=[pl.BlockSpec((ext, LANES), lambda i: (0, 0)), lanes(ext), lanes(KW)],
+        out_specs=lanes(rows),
+        out_shape=jax.ShapeDtypeStruct((rows, width), jnp.float32),
+        scratch_shapes=[
+            pltpu.VMEM((KW, rows, LANES), jnp.float32),
+            pltpu.VMEM((ext, LANES), jnp.float32),
+        ],
+        compiler_params=pltpu.CompilerParams(vmem_limit_bytes=10 << 20),
+        cost_estimate=pl.CostEstimate(
+            flops=4 * KW * rows * width, transcendentals=rows * width, bytes_accessed=8 * rows * width
+        ),
+        name="conv_factor",
+    )(seg, glu_ext, taps)
+
+
+def conv_grads_kernel(
+    seg, grad, glu, first_ref, gate_ref, taps, low, high, tap_grad, matches, wide_grad, wide_glu
+):
+    rows = low.shape[0]
+
+    @pl.when(pl.program_id(0) == 0)
+    def _():
+        fill_matches(seg, matches)
+
+    wide_grad[...] = grad[...].astype(jnp.float32)
+    wide_glu[...] = glu[...].astype(jnp.float32)
+    own = wide_grad[pl.ds(HALO, rows), :]
+    glu_grad = jnp.zeros(low.shape, jnp.float32)
+    for tap in range(KW):
+        at = pl.ds(tap + HALO - KW // 2, rows)
+        match = matches[tap]
+        glu_grad = glu_grad + taps[pl.ds(KW - 1 - tap, 1), :] * (wide_grad[at, :] * match)
+        tap_grad[pl.ds(tap, 1), :] = jnp.sum(own * (wide_glu[at, :] * match), axis=0, keepdims=True)
+    tap_grad[pl.ds(KW, 1), :] = jnp.zeros((1, LANES), jnp.float32)
+    first = first_ref[...].astype(jnp.float32)
+    sig = 1.0 / (1.0 + jnp.exp(-gate_ref[...].astype(jnp.float32)))
+    part = glu_grad * sig
+    low[...] = part.astype(jnp.bfloat16)
+    high[...] = (part * first * (1.0 - sig)).astype(jnp.bfloat16)
+
+
+def conv_grads(seg, grad_ext, glu_ext, pre_glu, taps):
+    ext, width = glu_ext.shape
+    rows = ext - 2 * HALO
+    n = width // LANES
+    lanes = lambda count: pl.BlockSpec((count, LANES), lambda i: (0, i))
+    return pl.pallas_call(
+        conv_grads_kernel,
+        grid=(n,),
+        in_specs=[
+            pl.BlockSpec((ext, LANES), lambda i: (0, 0)),
+            lanes(ext),
+            lanes(ext),
+            lanes(rows),
+            pl.BlockSpec((rows, LANES), lambda i: (0, i + n)),
+            lanes(KW),
+        ],
+        out_specs=[lanes(rows), lanes(rows), lanes(KW + 1)],
+        out_shape=[
+            jax.ShapeDtypeStruct((rows, width), jnp.bfloat16),
+            jax.ShapeDtypeStruct((rows, width), jnp.bfloat16),
+            jax.ShapeDtypeStruct((KW + 1, width), jnp.float32),
+        ],
+        scratch_shapes=[
+            pltpu.VMEM((KW, rows, LANES), jnp.float32),
+            pltpu.VMEM((ext, LANES), jnp.float32),
+            pltpu.VMEM((ext, LANES), jnp.float32),
+        ],
+        compiler_params=pltpu.CompilerParams(vmem_limit_bytes=10 << 20),
+        cost_estimate=pl.CostEstimate(
+            flops=8 * KW * rows * width, transcendentals=rows * width, bytes_accessed=16 * rows * width
+        ),
+        name="conv_grads",
+    )(seg, grad_ext, glu_ext, pre_glu, pre_glu, taps)
 
 
 def probs_kernel(bounds, q_t, k, v_t, lo, hi, probs, out_t, inv_sum, scores):
@@ -129,11 +238,11 @@
             scratch_shapes=[pltpu.VMEM((total, BLK), jnp.float32)],
         ),
         out_shape=[
-            jax.ShapeDtypeStruct((n, total, BLK), jnp.bfloat16),
+            pltpu.HBM((n, total, BLK), jnp.bfloat16),
             jax.ShapeDtypeStruct((HD, total), jnp.float32),
             jax.ShapeDtypeStruct((1, total), jnp.float32),
         ],
-        compiler_params=pltpu.CompilerParams(vmem_limit_bytes=32 << 20),
+        compiler_params=pltpu.CompilerParams(vmem_limit_bytes=14 << 20),
         cost_estimate=pl.CostEstimate(
             flops=2 * total * total * HD * 2,
             transcendentals=total * total // 2,
@@ -223,7 +332,7 @@
             shape,
             shape,
         ],
-        compiler_params=pltpu.CompilerParams(vmem_limit_bytes=32 << 20),
+        compiler_params=pltpu.CompilerParams(vmem_limit_bytes=18 << 20),
         cost_estimate=pl.CostEstimate(
             flops=2 * total * BLK * (end - begin) * HD * 4,
             transcendentals=0,
@@ -250,7 +359,6 @@
     t_dev, width = grad_out.shape
     n_seq = lax.axis_size(TIME)
     total = t_dev * n_seq
-    half = KW // 2
     core = lax.axis_index("core")
     ends = frame_ends(frame_counts[0])
 
@@ -268,53 +376,25 @@
 
     conv_half, _ = halves(w_conv_out, core)
     by_y = spread(conv_half, "y")
+    ext_pos = lax.axis_index(TIME) * t_dev + jnp.arange(-HALO, t_dev + HALO, dtype=jnp.int32)
+    seg_ext = jnp.broadcast_to(segments_of(ends, ext_pos)[:, None], (t_dev + 2 * HALO, LANES))
+    gate_sig = jax.nn.sigmoid(pre_glu[:, width:].astype(jnp.float32))
+    glu_out = (pre_glu[:, :width].astype(jnp.float32) * gate_sig).astype(jnp.bfloat16)
+    glu_ext = padded(glu_out, HALO)
     by_y, lo = lax.optimization_barrier((by_y, lo))
     by_xy = spread(by_y, "x")
     probs, out_t, inv_sum = attention_probs(bounds, queries.T, keys, values.T, lo, hi)
-    by_xy, probs = lax.optimization_barrier((by_xy, probs))
+    factor = conv_factor(seg_ext, glu_ext, kernel)
+    by_xy, probs, factor = lax.optimization_barrier((by_xy, probs, factor))
     w_conv_half = by_xy.transpose(1, 0, 2, 3).reshape(width, width // 2)
 
-    seq_index = lax.axis_index(TIME)
-    ext_pos = seq_index * t_dev + jnp.arange(-half, t_dev + half, dtype=jnp.int32)
-    seg_ext = segments_of(ends, ext_pos)
-    seg_own = seg_ext[half : half + t_dev]
-    first_half = pre_glu[:, :width].astype(jnp.float32)
-    gate_sig = jax.nn.sigmoid(pre_glu[:, width:].astype(jnp.float32))
-    glu_out = (first_half * gate_sig).astype(jnp.bfloat16)
-    glu_ext = padded(glu_out, half).astype(jnp.float32)
-    matches = [
-        (seg_ext[tap_index : tap_index + t_dev] == seg_own).astype(jnp.float32)[:, None]
-        for tap_index in range(KW)
-    ]
-    conv_out = jnp.zeros((t_dev, width), jnp.float32)
-    for tap_index in range(KW):
-        conv_out = (
-            conv_out
-            + kernel[tap_index] * glu_ext[tap_index : tap_index + t_dev] * matches[tap_index]
-        )
     conv_out_grad = pair_product(*halves(grad_out, core), w_conv_half)
-    conv_sig = jax.nn.sigmoid(conv_out)
-    conv_grad = (conv_out_grad * conv_sig * (1.0 + conv_out * (1.0 - conv_sig))).astype(
-        jnp.bfloat16
-    )
-    grad_ext = padded(conv_grad, half).astype(jnp.float32)
-    grad_float = grad_ext[half : half + t_dev]
-    glu_grad = jnp.zeros((t_dev, width), jnp.float32)
-    kernel_rows = []
-    for tap_index in range(KW):
-        back = 2 * half - tap_index
-        glu_grad = glu_grad + kernel[tap_index] * grad_ext[back : back + t_dev] * matches[back]
-        kernel_rows.append(
-            jnp.sum(
-                grad_float * glu_ext[tap_index : tap_index + t_dev] * matches[tap_index], axis=0
-            )
-        )
-    low_grad = (glu_grad * gate_sig).astype(jnp.bfloat16)
-    high_grad = (glu_grad * first_half * gate_sig * (1.0 - gate_sig)).astype(jnp.bfloat16)
+    conv_grad = (conv_out_grad * factor).astype(jnp.bfloat16)
+    grad_ext = padded(conv_grad, HALO)
+    low_grad, high_grad, rows = conv_grads(seg_ext, grad_ext, glu_ext, pre_glu, kernel)
     low_own, low_away = halves(low_grad, core)
     high_own, high_away = halves(high_grad, core)
 
-    rows = jnp.stack(kernel_rows + [jnp.zeros((width,), jnp.float32)])
     rows = lax.all_to_all(
         rows.reshape(n_seq, (KW + 1) // n_seq, width), TIME, split_axis=0, concat_axis=0
     )
@@ -345,18 +425,19 @@
     ctx_t, gain = lax.optimization_barrier((ctx_t, gain))
     ctx_t = lax.all_to_all(ctx_t, TIME, split_axis=0, concat_axis=0)
     sums = jnp.concatenate([rows, gain], axis=0)
+    for bit in (1, 2, 4):
+        sums = sums + lax.ppermute(sums, "y", [(i, i ^ bit) for i in range(lax.axis_size("y"))])
+    ctx_t, sums = lax.optimization_barrier((ctx_t, sums))
+    probs = pltpu.with_memory_space_constraint(probs, pltpu.HBM)
     fixed = (bounds, probs, ctx_t, out_t, inv_sum, queries, keys.T, values)
     n = total // BLK
-    cuts = [0, 3 * n // 8, 6 * n // 8, n]
-    parts = []
-    acc = ()
-    for stage, axis in enumerate(GROUPS + (TIME,)):
-        stacked = spread(sums, axis)
-        part, *acc = attention_grads(cuts[stage], cuts[stage + 1], *fixed, *acc)
-        parts.append(part)
-        if stage < 2:
-            stacked, *acc = lax.optimization_barrier((stacked, *acc))
-            sums = jnp.sum(stacked, axis=0)
+    stacked = spread(sums, "x")
+    part_a, *acc = attention_grads(0, n // 2, *fixed)
+    stacked, *acc = lax.optimization_barrier((stacked, *acc))
+    sums = jnp.sum(stacked, axis=0)
+    stacked = spread(sums, TIME)
+    part_b, *acc = attention_grads(n // 2, n, *fixed, *acc)
+    parts = [part_a, part_b]
     query_grad = jnp.concatenate(parts, axis=1).T
     key_grad, value_grad = [array.T for array in acc]
     kernel_grad = stacked[:, :-1].reshape(KW + 1, width)[:KW]

time: 219 us -> 204 us (0.932)
  the two profiles are of different devices: /device:TPU:19 before, /device:TPU:1 now
where the time goes in v3:
time: 204 us; the launch traced here: 201 us
  starting transfers between devices  80.7 us (40%)
  Pallas kernels  42 us (21%)
  waiting for transfers between devices  28.9 us (14%)
  local copies, waits for them, and re-layouts  15.5 us (8%)
  between operations  14.6 us (7%)
  matrix products  10.6 us (5%)
  other arithmetic  8.6 us (4%)
    all_to_all x4, starting transfers between devices, spread(): return lax.all_to_all(copies, axis, split_axis=0, concat_axis=0)  28.5 us
    pallas_call x2, Pallas kernels, attention_grads(): pl.pallas_call(lambda *refs: grads_kernel(begin, *refs), grid_spec=pltpu....  17.9 us
    pallas_call x1, Pallas kernels, attention_probs(): pl.pallas_call(probs_kernel, grid_spec=pltpu.PrefetchScalarGridSpec(num_s...  14.6 us
    ppermute x3, starting transfers between devices, local(): lax.ppermute(sums, 'y', [(i, i ^ bit) for i in range(lax.axis_size('y'))])  11.4 us
    ppermute x4, starting transfers between devices, swap(): return lax.ppermute(array, 'core', [(0, 1), (1, 0)])  10.5 us
    all_to_all x1, starting transfers between devices, local(): lax.all_to_all(rows.reshape(n_seq, (KW + 1) // n_seq, width), TIME, split...  9.8 us
    ppermute x2, starting transfers between devices, padded(): low = lax.ppermute(block[block.shape[0] - width:], TIME, forward)  8.88 us
    dot_general x4, matrix products, row_product(): jnp.einsum('tc,rc->tr', active, piece, preferred_element_type=jnp.float32)  8.87 us
  transfers between devices with their start and end apart: 18, of which 10 were waited for; matrix products, arithmetic and copies ran while one was open for 7% of the time, Pallas kernels for 21%

profile of v3, /device:TPU:1, one launch (start us, length us, event | category | flops | bytes accessed | tf_op | source)
XLA Modules:
  0.0 200.8 jit_solution(5187651829619183449)
XLA Ops:
  10.7 7.7 %all-to-all-start = ((bf16[8,40,640]{2,1,0:T(8,128)(2,1)}), bf16[8,40,640]{2,1,0:T(8,128)(2,1)S(1)}, u32[]{:S(2)}, u32[]{:S(2)}) async-start(bf16[8,40,640]{2,1,0:T(8,128)(2,1)} %broadcast_in_dim.59), calls=%async_computation | async-start | bytes 819200 | tf_op jit(solution)/shard_map/all_to_all | solution.py:43
  19.7 4.8 %collective-permute-start = (bf16[16,1280]{1,0:T(8,128)(2,1)S(1)}, bf16[16,1280]{1,0:T(8,128)(2,1)S(1)}, u32[]{:S(2)}, u32[]{:S(2)}) collective-permute-start(bf16[16,1280]{1,0:T(8,128)(2,1)S(1)} %get-tuple-element.69), channel_id=1, source_target_pairs={{0,1},{1,2},{2,3},{3,4},{4,5},{5,6},{6,7},{7,8},{8,9},{9,10},{10,1... | collective-permute-start | bytes 122888 | tf_op jit(solution)/shard_map/ppermute | solution.py:35
  26.7 3.6 %all-to-all-done = bf16[8,40,640]{2,1,0:T(8,128)(2,1)S(1)} async-done(((bf16[8,40,640]{2,1,0:T(8,128)(2,1)}), bf16[8,40,640]{2,1,0:T(8,128)(2,1)S(1)}, u32[]{:S(2)}, u32[]{:S(2)}) %all-to-all-start) | async-done | bytes 409632 | tf_op jit(solution)/shard_map/all_to_all | solution.py:43
  31.6 6.9 %all-to-all-start.1 = ((bf16[4,8,40,640]{3,2,1,0:T(8,128)(2,1)}), bf16[4,8,40,640]{3,2,1,0:T(8,128)(2,1)}, u32[]{:S(2)}, u32[]{:S(2)}) async-start(bf16[4,8,40,640]{3,2,1,0:T(8,128)(2,1)} %broadcast_in_dim.98), calls=%async_computation.1 | async-start | bytes 3276800 | tf_op jit(solution)/shard_map/all_to_all | solution.py:43
  39.2 3.5 %collective-permute-start.2 = (bf16[128,640]{1,0:T(8,128)(2,1)}, bf16[128,640]{1,0:T(8,128)(2,1)}, u32[]{:S(2)}, u32[]{:S(2)}) collective-permute-start(bf16[128,640]{1,0:T(8,128)(2,1)} %constant_dynamic-slice_fusion.6), channel_id=1, source_target_pairs={{0,1},{1,0},{2,3},{3,2},{4,5},{5,4},{6,7},{7,6},{8,9},{9,8},{10,11... | collective-permute-start | bytes 491528 | tf_op jit(solution)/shard_map/ppermute | solution.py:58
  44.3 2.9 %conv_factor.1 = f32[128,1280]{1,0:T(8,128)S(1)} custom-call(s32[160,128]{1,0:T(8,128)S(1)} %broadcast_in_dim.58.seg, bf16[160,1280]{1,0:T(8,128)(2,1)S(1)} %pad_maximum_fusion.glu, f32[31,1280]{1,0:T(8,128)S(1)} %copy-done.5), custom_call_target="tpu_custom_call" | custom-call | flops 20316160 | bytes 1310720 | tf_op jit(solution)/shard_map/conv_factor/pallas_call | solution.py:95
  48.3 14.6 %attention_probs.1 = (bf16[8,2048,256]{2,1,0:T(8,128)(2,1)}, f32[80,2048]{1,0:T(8,128)S(1)}, f32[1,2048]{1,0:T(1,128)S(1)}) custom-call(s32[2,8]{1,0:T(2,128)S(1)} %pad_add_fusion.bounds.refs_0_, bf16[80,2048]{1,0:T(8,128)(2,1)S(1)} %bitcast.22, bf16[2048,80]{1,0:T(8,128)(2,1)S(1)} %copy-done.6, bf16[80,2048]{1,0:T(8,128)(2,1)S(1)} %bitcast.23, ...), custom_call_target="tpu_custom_call" | custom-call | flops 1342177280 | bytes 8388608 | tf_op jit(solution)/shard_map/attention_probs/pallas_call | solution.py:221
  69.8 4.0 %collective-permute-start.4 = (bf16[16,1280]{1,0:T(8,128)(2,1)S(1)}, bf16[16,1280]{1,0:T(8,128)(2,1)S(1)}, u32[]{:S(2)}, u32[]{:S(2)}) collective-permute-start(bf16[16,1280]{1,0:T(8,128)(2,1)S(1)} %get-tuple-element.67), channel_id=1, source_target_pairs={{0,1},{1,2},{2,3},{3,4},{4,5},{5,6},{6,7},{7,8},{8,9},{9,10},{10,1... | collective-permute-start | bytes 122888 | tf_op jit(solution)/shard_map/ppermute | solution.py:35
  75.7 3.8 %collective-permute-done.5 = bf16[16,1280]{1,0:T(8,128)(2,1)S(1)} collective-permute-done((bf16[16,1280]{1,0:T(8,128)(2,1)S(1)}, bf16[16,1280]{1,0:T(8,128)(2,1)S(1)}, u32[]{:S(2)}, u32[]{:S(2)}) %collective-permute-start.5) | collective-permute-done | bytes 40992 | tf_op jit(solution)/shard_map/ppermute | solution.py:36
  79.6 6.5 %conv_grads.1 = (bf16[128,1280]{1,0:T(8,128)(2,1)S(1)}, bf16[128,1280]{1,0:T(8,128)(2,1)S(1)}, f32[32,1280]{1,0:T(8,128)S(1)}) custom-call(s32[160,128]{1,0:T(8,128)S(1)} %broadcast_in_dim.58.seg, bf16[160,1280]{1,0:T(8,128)(2,1)S(1)} %pad_maximum_fusion.1.grad, bf16[160,1280]{1,0:T(8,128)(2,1)S(1)} %pad_maximum_fusion.glu, bf16[128,2560]{1,0:T(8,128)(2,1)S(1)} %copy-done.1, ...), custom_call_target="tpu_custom_call" | custom-call | flops 40632320 | bytes 2621440 | tf_op jit(solution)/shard_map/conv_grads/pallas_call | solution.py:144
  86.9 9.8 %all-to-all-start.2 = ((f32[16,2,1280]{2,1,0:T(2,128)}), f32[16,2,1280]{2,1,0:T(2,128)S(1)}, u32[]{:S(2)}, u32[]{:S(2)}) async-start(f32[16,2,1280]{2,1,0:T(2,128)} %reshape.64), calls=%async_computation.2 | async-start | bytes 327680 | tf_op jit(solution)/shard_map/all_to_all | solution.py:398
  100.1 6.2 %all-to-all-done.2 = f32[16,2,1280]{2,1,0:T(2,128)S(1)} async-done(((f32[16,2,1280]{2,1,0:T(2,128)}), f32[16,2,1280]{2,1,0:T(2,128)S(1)}, u32[]{:S(2)}, u32[]{:S(2)}) %all-to-all-start.2) | async-done | bytes 163872 | tf_op jit(solution)/shard_map/all_to_all | solution.py:398
  106.4 5.6 %all-gather.2.cloned.1.call-done = bf16[1280,2560]{1,0:T(8,128)(2,1)} async-done(((bf16[40,2560]{1,0:T(8,128)(2,1)}), bf16[1280,2560]{1,0:T(8,128)(2,1)}) %all-gather.2.cloned.1.call-update) | async-done | bytes 6553616 | tf_op jit(solution)/shard_map/all_gather | solution.py:367
  112.0 3.3 %fusion.6 = bf16[128,1280]{1,0:T(8,128)(2,1)S(1)} fusion(bf16[128,1280]{1,0:T(8,128)(2,1)S(1)} %collective-permute-done.6, bf16[1280,2560]{1,0:T(8,128)(2,1)} %all-gather.2.cloned.1.call-done), kind=kOutput, calls=%fused_computation.6 | convolution fusion | flops 419594240 | bytes 3932160 | tf_op jit(solution)/shard_map/tc,rc->tr/dot_general | solution.py:47
  115.2 2.9 %collective-permute-start.7 = (bf16[128,1280]{1,0:T(8,128)(2,1)S(1)}, bf16[128,1280]{1,0:T(8,128)(2,1)S(1)}, u32[]{:S(2)}, u32[]{:S(2)}) collective-permute-start(bf16[128,1280]{1,0:T(8,128)(2,1)S(1)} %fusion.6), channel_id=1, source_target_pairs={{0,1},{1,0},{2,3},{3,2},{4,5},{5,4},{6,7},{7,6},{8,9},{9,8},{10,11... | collective-permute-start | bytes 983048 | tf_op jit(solution)/shard_map/ppermute | solution.py:58
  119.4 3.4 %fusion.22 = (f32[1280]{0:T(1024)S(1)}, f32[128]{0:T(128)S(1)}, f32[128]{0:T(128)S(1)}, f32[128,1280]{1,0:T(8,128)S(1)}) fusion(bf16[128,1280]{1,0:T(8,128)(2,1)S(1)} %copy-done.12, f32[128]{0:T(128)S(1)} %add_rsqrt_fusion, f32[128]{0:T(128)S(1)} %broadcast_multiply_fusion.2, f32[1280]{0:T(1024)S(1)} %copy-done.17, ...), kind=kOutput, calls=%fused_computation.21 | convolution fusion | flops 421886464 | bytes 4927488 | tf_op jit(solution)/shard_map/tc,rc->tr/dot_general | solution.py:47
  125.0 7.8 %all-to-all-start.3 = ((bf16[16,80,128]{2,1,0:T(8,128)(2,1)}), bf16[16,80,128]{2,1,0:T(8,128)(2,1)S(1)}, u32[]{:S(2)}, u32[]{:S(2)}) async-start(bf16[16,80,128]{2,1,0:T(8,128)(2,1)} %bitcast.8), calls=%async_computation.3 | async-start | bytes 655360 | tf_op jit(solution)/shard_map/all_to_all | solution.py:426
  132.8 3.0 %collective-permute-start.8 = (f32[3,1280]{1,0:T(4,128)S(1)}, f32[3,1280]{1,0:T(4,128)S(1)}, u32[]{:S(2)}, u32[]{:S(2)}) collective-permute-start(f32[3,1280]{1,0:T(4,128)S(1)} %pad_maximum_fusion.4), channel_id=1, source_target_pairs={{0,64},{64,0},{128,192},{192,128},{256,320},{320,256},{384,448},{4... | collective-permute-start | bytes 46088 | tf_op jit(solution)/shard_map/ppermute | solution.py:429
  137.6 3.4 %collective-permute-start.9 = (f32[3,1280]{1,0:T(4,128)S(1)}, f32[3,1280]{1,0:T(4,128)S(1)}, u32[]{:S(2)}, u32[]{:S(2)}) collective-permute-start(f32[3,1280]{1,0:T(4,128)S(1)} %fusion.35), channel_id=1, source_target_pairs={{0,128},{64,192},{128,0},{192,64},{256,384},{320,448},{384,256},{4... | collective-permute-start | bytes 46088 | tf_op jit(solution)/shard_map/ppermute | solution.py:429
  143.4 5.0 %collective-permute-start.10 = (f32[3,1280]{1,0:T(4,128)S(1)}, f32[3,1280]{1,0:T(4,128)S(1)}, u32[]{:S(2)}, u32[]{:S(2)}) collective-permute-start(f32[3,1280]{1,0:T(4,128)S(1)} %add.98), channel_id=1, source_target_pairs={{0,256},{64,320},{128,384},{192,448},{256,0},{320,64},{384,128},{4... | collective-permute-start | bytes 46088 | tf_op jit(solution)/shard_map/ppermute | solution.py:429
  152.5 3.9 %all-to-all-start.4 = ((f32[4,3,1280]{2,1,0:T(4,128)}), f32[4,3,1280]{2,1,0:T(4,128)}, u32[]{:S(2)}, u32[]{:S(2)}) async-start(f32[4,3,1280]{2,1,0:T(4,128)} %broadcast_in_dim.102), calls=%async_computation.4 | async-start | bytes 163840 | tf_op jit(solution)/shard_map/all_to_all | solution.py:43
  156.4 7.4 %attention_grads.2 = (bf16[80,1024]{1,0:T(8,128)(2,1)S(1)}, f32[2048,80]{1,0:T(8,128)S(1)}, f32[2048,80]{1,0:T(8,128)S(1)}) custom-call(s32[2,8]{1,0:T(2,128)S(1)} %pad_add_fusion.bounds.refs_0_, bf16[8,2048,256]{2,1,0:T(8,128)(2,1)} %get-tuple-element.41.refs_1_, bf16[16,80,128]{2,1,0:T(8,128)(2,1)S(1)} %all-to-all-done.3.refs_2_, ...), custom_call_target="tpu_custom_call" | custom-call | flops 1342177280 | bytes 4194304 | tf_op jit(solution)/shard_map/attention_grads/pallas_call | solution.py:308
  167.2 10.1 %all-to-all-start.5 = ((f32[16,3,1280]{2,1,0:T(4,128)}), f32[16,3,1280]{2,1,0:T(4,128)}, u32[]{:S(2)}, u32[]{:S(2)}) async-start(f32[16,3,1280]{2,1,0:T(4,128)} %broadcast_in_dim.103), calls=%async_computation.5 | async-start | bytes 655360 | tf_op jit(solution)/shard_map/all_to_all | solution.py:43
  178.5 10.4 %attention_grads.3 = (bf16[80,1024]{1,0:T(8,128)(2,1)S(1)}, bf16[80,2048]{1,0:T(8,128)(2,1)}, bf16[80,2048]{1,0:T(8,128)(2,1)}) custom-call(s32[2,8]{1,0:T(2,128)S(1)} %pad_add_fusion.bounds.refs_0_, bf16[8,2048,256]{2,1,0:T(8,128)(2,1)} %get-tuple-element.41.refs_1_, bf16[16,80,128]{2,1,0:T(8,128)(2,1)S(1)} %all-to-all-done.3.refs_2_, ...), custom_call_target="tpu_custom_call" | custom-call | flops 1342177280 | bytes 4194304 | tf_op jit(solution)/shard_map/attention_grads/pallas_call | solution.py:308
  (117 shorter events, 45.6 us)
Async XLA Ops:
  7.2 19.3 %copy-start.18 = (s32[1,8]{1,0:T(1,128)S(1)}, s32[1,8]{1,0:T(1,128)}, u32[]{:S(2)}) copy-start(s32[1,8]{1,0:T(1,128)} %param.18) | copy-start | bytes 100
  7.2 104.8 %all-gather.2.cloned.1.call-start = ((), (), s32[]{:S(2)}) async-start(), calls=%async_computation.6 | async-start | bytes 6758400 | tf_op jit(solution)/shard_map/all_gather | solution.py:367
  10.7 19.6 %all-to-all-start = ((bf16[8,40,640]{2,1,0:T(8,128)(2,1)}), bf16[8,40,640]{2,1,0:T(8,128)(2,1)S(1)}, u32[]{:S(2)}, u32[]{:S(2)}) async-start(bf16[8,40,640]{2,1,0:T(8,128)(2,1)} %broadcast_in_dim.59), calls=%async_computation | async-start | bytes 819200 | tf_op jit(solution)/shard_map/all_to_all | solution.py:43
  18.3 20.2 %copy-start.13 = (bf16[128,1280]{1,0:T(8,128)(2,1)S(1)}, bf16[128,1280]{1,0:T(8,128)(2,1)}, u32[]{:S(2)}) copy-start(bf16[128,1280]{1,0:T(8,128)(2,1)} %param.12) | copy-start | bytes 983044
  18.3 24.8 %copy-start.2 = (bf16[2048,80]{0,1:T(8,128)(2,1)S(1)}, bf16[2048,80]{0,1:T(8,128)(2,1)}, u32[]{:S(2)}) copy-start(bf16[2048,80]{0,1:T(8,128)(2,1)} %param.16) | copy-start | bytes 983044
  19.7 24.5 %collective-permute-start = (bf16[16,1280]{1,0:T(8,128)(2,1)S(1)}, bf16[16,1280]{1,0:T(8,128)(2,1)S(1)}, u32[]{:S(2)}, u32[]{:S(2)}) collective-permute-start(bf16[16,1280]{1,0:T(8,128)(2,1)S(1)} %get-tuple-element.69), channel_id=1, source_target_pairs={{0,1},{1,2},{2,3},{3,4},{4,5},{5,6},{6,7},{7,8},{8,9},{9,10},{10,1... | collective-permute-start | bytes 122888 | tf_op jit(solution)/shard_map/ppermute | solution.py:35
  24.5 19.6 %collective-permute-start.1 = (bf16[16,1280]{1,0:T(8,128)(2,1)S(1)}, bf16[16,1280]{1,0:T(8,128)(2,1)S(1)}, u32[]{:S(2)}, u32[]{:S(2)}) collective-permute-start(bf16[16,1280]{1,0:T(8,128)(2,1)S(1)} %get-tuple-element.70), channel_id=1, source_target_pairs={{1,0},{2,1},{3,2},{4,3},{5,4},{6,5},{7,6},{8,7},{9,8},{10,9},{11,1... | collective-permute-start | bytes 122888 | tf_op jit(solution)/shard_map/ppermute | solution.py:36
  31.6 31.3 %all-to-all-start.1 = ((bf16[4,8,40,640]{3,2,1,0:T(8,128)(2,1)}), bf16[4,8,40,640]{3,2,1,0:T(8,128)(2,1)}, u32[]{:S(2)}, u32[]{:S(2)}) async-start(bf16[4,8,40,640]{3,2,1,0:T(8,128)(2,1)} %broadcast_in_dim.98), calls=%async_computation.1 | async-start | bytes 3276800 | tf_op jit(solution)/shard_map/all_to_all | solution.py:43
  39.2 25.3 %collective-permute-start.2 = (bf16[128,640]{1,0:T(8,128)(2,1)}, bf16[128,640]{1,0:T(8,128)(2,1)}, u32[]{:S(2)}, u32[]{:S(2)}) collective-permute-start(bf16[128,640]{1,0:T(8,128)(2,1)} %constant_dynamic-slice_fusion.6), channel_id=1, source_target_pairs={{0,1},{1,0},{2,3},{3,2},{4,5},{5,4},{6,7},{7,6},{8,9},{9,8},{10,11... | collective-permute-start | bytes 491528 | tf_op jit(solution)/shard_map/ppermute | solution.py:58
  66.1 3.5 %collective-permute-start.3 = (bf16[128,1280]{1,0:T(8,128)(2,1)S(1)}, bf16[128,1280]{1,0:T(8,128)(2,1)S(1)}, u32[]{:S(2)}, u32[]{:S(2)}) collective-permute-start(bf16[128,1280]{1,0:T(8,128)(2,1)S(1)} %convolution_convert_fusion), channel_id=1, source_target_pairs={{0,1},{1,0},{2,3},{3,2},{4,5},{5,4},{6,7},{7,6},{8,9},{9,8},{10,11... | collective-permute-start | bytes 983048 | tf_op jit(solution)/shard_map/ppermute | solution.py:58
  69.8 6.0 %collective-permute-start.4 = (bf16[16,1280]{1,0:T(8,128)(2,1)S(1)}, bf16[16,1280]{1,0:T(8,128)(2,1)S(1)}, u32[]{:S(2)}, u32[]{:S(2)}) collective-permute-start(bf16[16,1280]{1,0:T(8,128)(2,1)S(1)} %get-tuple-element.67), channel_id=1, source_target_pairs={{0,1},{1,2},{2,3},{3,4},{4,5},{5,6},{6,7},{7,8},{8,9},{9,10},{10,1... | collective-permute-start | bytes 122888 | tf_op jit(solution)/shard_map/ppermute | solution.py:35
  73.8 5.7 %collective-permute-start.5 = (bf16[16,1280]{1,0:T(8,128)(2,1)S(1)}, bf16[16,1280]{1,0:T(8,128)(2,1)S(1)}, u32[]{:S(2)}, u32[]{:S(2)}) collective-permute-start(bf16[16,1280]{1,0:T(8,128)(2,1)S(1)} %get-tuple-element.68), channel_id=1, source_target_pairs={{1,0},{2,1},{3,2},{4,3},{5,4},{6,5},{7,6},{8,7},{9,8},{10,9},{11,1... | collective-permute-start | bytes 122888 | tf_op jit(solution)/shard_map/ppermute | solution.py:36
  86.9 19.5 %all-to-all-start.2 = ((f32[16,2,1280]{2,1,0:T(2,128)}), f32[16,2,1280]{2,1,0:T(2,128)S(1)}, u32[]{:S(2)}, u32[]{:S(2)}) async-start(f32[16,2,1280]{2,1,0:T(2,128)} %reshape.64), calls=%async_computation.2 | async-start | bytes 327680 | tf_op jit(solution)/shard_map/all_to_all | solution.py:398
  96.7 21.4 %copy-start.12 = (bf16[128,1280]{1,0:T(8,128)(2,1)S(1)}, bf16[128,1280]{1,0:T(8,128)(2,1)}, u32[]{:S(2)}) copy-start(bf16[128,1280]{1,0:T(8,128)(2,1)} %param.13) | copy-start | bytes 983044
  96.8 22.6 %copy-start.17 = (f32[1280]{0:T(1024)S(1)}, f32[1280]{0:T(1024)}, u32[]{:S(2)}) copy-start(f32[1280]{0:T(1024)} %param.19) | copy-start | bytes 15364
  96.9 15.1 %collective-permute-start.6 = (bf16[128,1280]{1,0:T(8,128)(2,1)S(1)}, bf16[128,1280]{1,0:T(8,128)(2,1)S(1)}, u32[]{:S(2)}, u32[]{:S(2)}) collective-permute-start(bf16[128,1280]{1,0:T(8,128)(2,1)S(1)} %pad_maximum_fusion.2), channel_id=1, source_target_pairs={{0,1},{1,0},{2,3},{3,2},{4,5},{5,4},{6,7},{7,6},{8,9},{9,8},{10,11... | collective-permute-start | bytes 983048 | tf_op jit(solution)/shard_map/ppermute | solution.py:58
  115.2 4.1 %collective-permute-start.7 = (bf16[128,1280]{1,0:T(8,128)(2,1)S(1)}, bf16[128,1280]{1,0:T(8,128)(2,1)S(1)}, u32[]{:S(2)}, u32[]{:S(2)}) collective-permute-start(bf16[128,1280]{1,0:T(8,128)(2,1)S(1)} %fusion.6), channel_id=1, source_target_pairs={{0,1},{1,0},{2,3},{3,2},{4,5},{5,4},{6,7},{7,6},{8,9},{9,8},{10,11... | collective-permute-start | bytes 983048 | tf_op jit(solution)/shard_map/ppermute | solution.py:58
  123.2 25.4 %copy-start.9 = (bf16[2048,80]{0,1:T(8,128)(2,1)S(1)}, bf16[2048,80]{0,1:T(8,128)(2,1)}, u32[]{:S(2)}) copy-start(bf16[2048,80]{0,1:T(8,128)(2,1)} %param.17) | copy-start | bytes 983044
  125.0 26.8 %all-to-all-start.3 = ((bf16[16,80,128]{2,1,0:T(8,128)(2,1)}), bf16[16,80,128]{2,1,0:T(8,128)(2,1)S(1)}, u32[]{:S(2)}, u32[]{:S(2)}) async-start(bf16[16,80,128]{2,1,0:T(8,128)(2,1)} %bitcast.8), calls=%async_computation.3 | async-start | bytes 655360 | tf_op jit(solution)/shard_map/all_to_all | solution.py:426
  132.8 4.8 %collective-permute-start.8 = (f32[3,1280]{1,0:T(4,128)S(1)}, f32[3,1280]{1,0:T(4,128)S(1)}, u32[]{:S(2)}, u32[]{:S(2)}) collective-permute-start(f32[3,1280]{1,0:T(4,128)S(1)} %pad_maximum_fusion.4), channel_id=1, source_target_pairs={{0,64},{64,0},{128,192},{192,128},{256,320},{320,256},{384,448},{4... | collective-permute-start | bytes 46088 | tf_op jit(solution)/shard_map/ppermute | solution.py:429
  137.6 5.7 %collective-permute-start.9 = (f32[3,1280]{1,0:T(4,128)S(1)}, f32[3,1280]{1,0:T(4,128)S(1)}, u32[]{:S(2)}, u32[]{:S(2)}) collective-permute-start(f32[3,1280]{1,0:T(4,128)S(1)} %fusion.35), channel_id=1, source_target_pairs={{0,128},{64,192},{128,0},{192,64},{256,384},{320,448},{384,256},{4... | collective-permute-start | bytes 46088 | tf_op jit(solution)/shard_map/ppermute | solution.py:429
  143.4 8.4 %collective-permute-start.10 = (f32[3,1280]{1,0:T(4,128)S(1)}, f32[3,1280]{1,0:T(4,128)S(1)}, u32[]{:S(2)}, u32[]{:S(2)}) collective-permute-start(f32[3,1280]{1,0:T(4,128)S(1)} %add.98), channel_id=1, source_target_pairs={{0,256},{64,320},{128,384},{192,448},{256,0},{320,64},{384,128},{4... | collective-permute-start | bytes 46088 | tf_op jit(solution)/shard_map/ppermute | solution.py:429
  152.5 13.1 %all-to-all-start.4 = ((f32[4,3,1280]{2,1,0:T(4,128)}), f32[4,3,1280]{2,1,0:T(4,128)}, u32[]{:S(2)}, u32[]{:S(2)}) async-start(f32[4,3,1280]{2,1,0:T(4,128)} %broadcast_in_dim.102), calls=%async_computation.4 | async-start | bytes 163840 | tf_op jit(solution)/shard_map/all_to_all | solution.py:43
  167.2 23.2 %all-to-all-start.5 = ((f32[16,3,1280]{2,1,0:T(4,128)}), f32[16,3,1280]{2,1,0:T(4,128)}, u32[]{:S(2)}, u32[]{:S(2)}) async-start(f32[16,3,1280]{2,1,0:T(4,128)} %broadcast_in_dim.103), calls=%async_computation.5 | async-start | bytes 655360 | tf_op jit(solution)/shard_map/all_to_all | solution.py:43
  (15 other events, 102.9 us)
Sparse Core Ops, SparseCore 0:
  11.8 100.1 all-gather.1

commit v4 on v3

--- a/solution.py
+++ b/solution.py
@@ -10,11 +10,12 @@
 
 HD = 80
 KW = 31
+QBLK = 512
 BLK = 256
 HALO = 16
 LANES = 128
 TIME = ("z", "core")
-GROUPS = ("y", "x")
+GROUPS = ("far", "y", "x")
 
 
 def frame_ends(frame_lens):
@@ -171,6 +172,19 @@
     )(seg, grad_ext, glu_ext, pre_glu, pre_glu, taps)
 
 
+def over_keys(first, last, step, carry):
+    pairs = (last - first) // 2
+
+    def pair(i, carry):
+        return step(pl.multiple_of((first + 2 * i) * BLK, BLK), 2 * BLK, carry)
+
+    def single(i, carry):
+        return step(pl.multiple_of(i * BLK, BLK), BLK, carry)
+
+    carry = lax.fori_loop(0, pairs, pair, carry)
+    return lax.fori_loop(first + 2 * pairs, last, single, carry)
+
+
 def probs_kernel(bounds, q_t, k, v_t, lo, hi, probs, out_t, inv_sum, scores):
     factor = math.log2(math.e) / math.sqrt(HD)
     block = pl.program_id(0)
@@ -180,29 +194,27 @@
     start = lo[...]
     end = hi[...]
     width = query.shape[1]
-    rows = lax.broadcasted_iota(jnp.int32, (BLK, width), 0)
-
-    def score(kb, peak):
-        at = pl.multiple_of(kb * BLK, BLK)
-        s = jnp.dot(k[pl.ds(at, BLK), :], query, preferred_element_type=jnp.float32)
+
+    def score(at, size, peak):
+        rows = lax.broadcasted_iota(jnp.int32, (size, width), 0)
+        s = jnp.dot(k[pl.ds(at, size), :], query, preferred_element_type=jnp.float32)
         valid = (rows >= start - at) & (rows < end - at)
         s = jnp.where(valid, s, -1e30)
-        scores[pl.ds(at, BLK), :] = s
-        return jnp.maximum(peak, jnp.max(s.reshape(BLK // 8, 8, width), axis=0))
-
-    peak = lax.fori_loop(first, last, score, jnp.full((8, width), -1e30, jnp.float32))
+        scores[pl.ds(at, size), :] = s
+        return jnp.maximum(peak, jnp.max(s.reshape(size // 8, 8, width), axis=0))
+
+    peak = over_keys(first, last, score, jnp.full((8, width), -1e30, jnp.float32))
     peak = jnp.max(peak, axis=0, keepdims=True)
 
-    def expo(kb, carry):
+    def expo(at, size, carry):
         total, acc = carry
-        at = pl.multiple_of(kb * BLK, BLK)
-        e = jnp.exp2((scores[pl.ds(at, BLK), :] - peak) * factor)
+        e = jnp.exp2((scores[pl.ds(at, size), :] - peak) * factor)
         low = e.astype(jnp.bfloat16)
-        probs[pl.ds(at, BLK), :] = low
-        acc = acc + jnp.dot(v_t[:, pl.ds(at, BLK)], low, preferred_element_type=jnp.float32)
-        return total + jnp.sum(e.reshape(BLK // 8, 8, width), axis=0), acc
-
-    total, acc = lax.fori_loop(
+        probs[pl.ds(at, size), :] = low
+        acc = acc + jnp.dot(v_t[:, pl.ds(at, size)], low, preferred_element_type=jnp.float32)
+        return total + jnp.sum(e.reshape(size // 8, 8, width), axis=0), acc
+
+    total, acc = over_keys(
         first,
         last,
         expo,
@@ -215,8 +227,8 @@
 
 def attention_probs(bounds, q_t, keys, v_t, lo, hi):
     total = keys.shape[0]
-    n = total // BLK
-    lanes = lambda rows: pl.BlockSpec((rows, BLK), lambda i, b: (0, i))
+    n = total // QBLK
+    lanes = lambda rows: pl.BlockSpec((rows, QBLK), lambda i, b: (0, i))
     whole = lambda shape: pl.BlockSpec(shape, lambda i, b: (0, 0))
     return pl.pallas_call(
         probs_kernel,
@@ -231,18 +243,18 @@
                 lanes(1),
             ],
             out_specs=[
-                pl.BlockSpec((None, total, BLK), lambda i, b: (i, 0, 0)),
+                pl.BlockSpec((None, total, QBLK), lambda i, b: (i, 0, 0)),
                 lanes(HD),
                 lanes(1),
             ],
-            scratch_shapes=[pltpu.VMEM((total, BLK), jnp.float32)],
+            scratch_shapes=[pltpu.VMEM((total, QBLK), jnp.float32)],
         ),
         out_shape=[
-            pltpu.HBM((n, total, BLK), jnp.bfloat16),
+            pltpu.HBM((n, total, QBLK), jnp.bfloat16),
             jax.ShapeDtypeStruct((HD, total), jnp.float32),
             jax.ShapeDtypeStruct((1, total), jnp.float32),
         ],
-        compiler_params=pltpu.CompilerParams(vmem_limit_bytes=14 << 20),
+        compiler_params=pltpu.CompilerParams(vmem_limit_bytes=20 << 20),
         cost_estimate=pl.CostEstimate(
             flops=2 * total * total * HD * 2,
             transcendentals=total * total // 2,
@@ -252,19 +264,16 @@
     )(bounds, q_t, keys, v_t, lo, hi)
 
 
-def grads_kernel(begin, bounds, probs, ctx_t, out_t, inv_sum, q, k_t, v, *refs):
-    carried = begin > 0
-    dk_in, dv_in = refs[:2] if carried else (None, None)
-    dq_t, dk_t, dv_t, dk_acc, dv_acc = refs[-5:]
+def grads_kernel(bounds, probs, ctx_t, out_t, inv_sum, q, k_t, v, dq_t, dk_t, dv_t, dk_acc, dv_acc):
     scale = 1.0 / math.sqrt(HD)
-    step_id = pl.program_id(0)
-    first = bounds[0, begin + step_id]
-    last = bounds[1, begin + step_id]
-
-    @pl.when(step_id == 0)
+    block = pl.program_id(0)
+    first = bounds[0, block]
+    last = bounds[1, block]
+
+    @pl.when(block == 0)
     def _():
-        dk_acc[...] = dk_in[...] if carried else jnp.zeros_like(dk_acc)
-        dv_acc[...] = dv_in[...] if carried else jnp.zeros_like(dv_acc)
+        dk_acc[...] = jnp.zeros_like(dk_acc)
+        dv_acc[...] = jnp.zeros_like(dv_acc)
 
     pieces = [ctx_t[i].astype(jnp.float32) for i in range(ctx_t.shape[0])]
     grad_t = jnp.concatenate(pieces, axis=1) * inv_sum[...]
@@ -273,73 +282,55 @@
     delta = jnp.sum(grad_low_t.astype(jnp.float32) * out_t[...], axis=0, keepdims=True)
     query = q[...]
 
-    def step(kb, acc):
-        at = pl.multiple_of(kb * BLK, BLK)
-        e = probs[pl.ds(at, BLK), :]
-        prob_grad = jnp.dot(v[pl.ds(at, BLK), :], grad_low_t, preferred_element_type=jnp.float32)
+    def step(at, size, acc):
+        e = probs[pl.ds(at, size), :]
+        prob_grad = jnp.dot(v[pl.ds(at, size), :], grad_low_t, preferred_element_type=jnp.float32)
         ds = (e.astype(jnp.float32) * (prob_grad - delta)).astype(jnp.bfloat16)
-        dv_acc[pl.ds(at, BLK), :] += jnp.dot(e, grad_low, preferred_element_type=jnp.float32)
-        dk_acc[pl.ds(at, BLK), :] += jnp.dot(ds, query, preferred_element_type=jnp.float32)
-        return acc + jnp.dot(k_t[:, pl.ds(at, BLK)], ds, preferred_element_type=jnp.float32)
-
-    acc = lax.fori_loop(first, last, step, jnp.zeros((HD, query.shape[0]), jnp.float32))
+        dv_acc[pl.ds(at, size), :] += jnp.dot(e, grad_low, preferred_element_type=jnp.float32)
+        dk_acc[pl.ds(at, size), :] += jnp.dot(ds, query, preferred_element_type=jnp.float32)
+        return acc + jnp.dot(k_t[:, pl.ds(at, size)], ds, preferred_element_type=jnp.float32)
+
+    acc = over_keys(first, last, step, jnp.zeros((HD, query.shape[0]), jnp.float32))
     dq_t[...] = (acc * scale).astype(jnp.bfloat16)
 
-    @pl.when(step_id == pl.num_programs(0) - 1)
+    @pl.when(block == pl.num_programs(0) - 1)
     def _():
-        if dk_t.shape[0] == HD:
-            dk_t[...] = (dk_acc[...] * scale).T.astype(jnp.bfloat16)
-            dv_t[...] = dv_acc[...].T.astype(jnp.bfloat16)
-        else:
-            dk_t[...] = dk_acc[...]
-            dv_t[...] = dv_acc[...]
-
-
-def attention_grads(begin, end, bounds, probs, ctx_t, out_t, inv_sum, queries, k_t, values, *sums):
+        dk_t[...] = (dk_acc[...] * scale).T.astype(jnp.bfloat16)
+        dv_t[...] = dv_acc[...].T.astype(jnp.bfloat16)
+
+
+def attention_grads(bounds, probs, ctx_t, out_t, inv_sum, queries, k_t, values):
     total = queries.shape[0]
-    n = total // BLK
-    per = BLK // ctx_t.shape[2]
-    lanes = lambda rows: pl.BlockSpec((rows, BLK), lambda i, b: (0, i + begin))
+    n = total // QBLK
+    per = QBLK // ctx_t.shape[2]
+    lanes = lambda rows: pl.BlockSpec((rows, QBLK), lambda i, b: (0, i))
     whole = lambda shape: pl.BlockSpec(shape, lambda i, b: (0, 0))
-    if end == n:
-        shape = jax.ShapeDtypeStruct((HD, total), jnp.bfloat16)
-    else:
-        shape = jax.ShapeDtypeStruct((total, HD), jnp.float32)
     return pl.pallas_call(
-        lambda *refs: grads_kernel(begin, *refs),
+        grads_kernel,
         grid_spec=pltpu.PrefetchScalarGridSpec(
             num_scalar_prefetch=1,
-            grid=(end - begin,),
+            grid=(n,),
             in_specs=[
-                pl.BlockSpec((None, total, BLK), lambda i, b: (i + begin, 0, 0)),
-                pl.BlockSpec((per, HD, ctx_t.shape[2]), lambda i, b: (i + begin, 0, 0)),
+                pl.BlockSpec((None, total, QBLK), lambda i, b: (i, 0, 0)),
+                pl.BlockSpec((per, HD, ctx_t.shape[2]), lambda i, b: (i, 0, 0)),
                 lanes(HD),
                 lanes(1),
-                pl.BlockSpec((BLK, HD), lambda i, b: (i + begin, 0)),
+                pl.BlockSpec((QBLK, HD), lambda i, b: (i, 0)),
                 whole((HD, total)),
                 whole((total, HD)),
-            ]
-            + [whole((total, HD))] * len(sums),
-            out_specs=[
-                pl.BlockSpec((HD, BLK), lambda i, b: (0, i)),
-                whole(shape.shape),
-                whole(shape.shape),
             ],
+            out_specs=[lanes(HD), whole((HD, total)), whole((HD, total))],
             scratch_shapes=[pltpu.VMEM((total, HD), jnp.float32)] * 2,
         ),
-        out_shape=[
-            jax.ShapeDtypeStruct((HD, (end - begin) * BLK), jnp.bfloat16),
-            shape,
-            shape,
-        ],
-        compiler_params=pltpu.CompilerParams(vmem_limit_bytes=18 << 20),
+        out_shape=[jax.ShapeDtypeStruct((HD, total), jnp.bfloat16)] * 3,
+        compiler_params=pltpu.CompilerParams(vmem_limit_bytes=20 << 20),
         cost_estimate=pl.CostEstimate(
-            flops=2 * total * BLK * (end - begin) * HD * 4,
+            flops=2 * total * total * HD * 4,
             transcendentals=0,
-            bytes_accessed=total * BLK * (end - begin) * 2,
+            bytes_accessed=total * total * 2,
         ),
         name="attention_grads",
-    )(bounds, probs, ctx_t, out_t, inv_sum, queries, k_t, values, *sums)
+    )(bounds, probs, ctx_t, out_t, inv_sum, queries, k_t, values)
 
 
 def local(
@@ -372,10 +363,10 @@
     passed = positions[None, :] >= ends[:, None]
     lo = jnp.max(jnp.where(passed, ends[:, None], 0), axis=0, keepdims=True)
     hi = jnp.min(jnp.where(passed, total, ends[:, None]), axis=0, keepdims=True)
-    bounds = jnp.stack([lo[0, ::BLK] // BLK, (hi[0, BLK - 1 :: BLK] + BLK - 1) // BLK])
+    bounds = jnp.stack([lo[0, ::QBLK] // BLK, (hi[0, QBLK - 1 :: QBLK] + BLK - 1) // BLK])
 
     conv_half, _ = halves(w_conv_out, core)
-    by_y = spread(conv_half, "y")
+    by_y = spread(conv_half, ("far", "y"))
     ext_pos = lax.axis_index(TIME) * t_dev + jnp.arange(-HALO, t_dev + HALO, dtype=jnp.int32)
     seg_ext = jnp.broadcast_to(segments_of(ends, ext_pos)[:, None], (t_dev + 2 * HALO, LANES))
     gate_sig = jax.nn.sigmoid(pre_glu[:, width:].astype(jnp.float32))
@@ -425,21 +416,15 @@
     ctx_t, gain = lax.optimization_barrier((ctx_t, gain))
     ctx_t = lax.all_to_all(ctx_t, TIME, split_axis=0, concat_axis=0)
     sums = jnp.concatenate([rows, gain], axis=0)
-    for bit in (1, 2, 4):
+    for bit in (1, 2):
         sums = sums + lax.ppermute(sums, "y", [(i, i ^ bit) for i in range(lax.axis_size("y"))])
     ctx_t, sums = lax.optimization_barrier((ctx_t, sums))
     probs = pltpu.with_memory_space_constraint(probs, pltpu.HBM)
-    fixed = (bounds, probs, ctx_t, out_t, inv_sum, queries, keys.T, values)
-    n = total // BLK
-    stacked = spread(sums, "x")
-    part_a, *acc = attention_grads(0, n // 2, *fixed)
-    stacked, *acc = lax.optimization_barrier((stacked, *acc))
-    sums = jnp.sum(stacked, axis=0)
-    stacked = spread(sums, TIME)
-    part_b, *acc = attention_grads(n // 2, n, *fixed, *acc)
-    parts = [part_a, part_b]
-    query_grad = jnp.concatenate(parts, axis=1).T
-    key_grad, value_grad = [array.T for array in acc]
+    stacked = spread(sums, ("far", "x"))
+    grads = attention_grads(bounds, probs, ctx_t, out_t, inv_sum, queries, keys.T, values)
+    query_grad, key_grad, value_grad = [array.T for array in grads]
+    stacked, query_grad = lax.optimization_barrier((stacked, query_grad))
+    stacked = spread(jnp.sum(stacked, axis=0), TIME)
     kernel_grad = stacked[:, :-1].reshape(KW + 1, width)[:KW]
     gain_grad = jnp.sum(stacked[:, -1], axis=0)
     return (resid_grad, query_grad, key_grad, value_grad, kernel_grad, gain_grad)
@@ -447,7 +432,7 @@
 
 def solution(mesh):
     dp, seq = mesh.devices.shape
-    shape = (dp // 4, 4, seq // 2, 2)
+    shape = (2, dp // 8, 4, seq // 2, 2)
     fine = Mesh(mesh.devices.reshape(shape), GROUPS + TIME)
     frames = P(GROUPS + TIME, None)
     heads = P(GROUPS, TIME)

time: 204 us -> 192 us (0.941)
  blocking collectives: 0 us -> 19.6 us
  Pallas kernels: 42 us -> 30.2 us
  starting transfers between devices: 80.7 us -> 69.7 us
  local copies, waits for them, and re-layouts: 15.5 us -> 9.94 us
  other arithmetic: 8.6 us -> 5.01 us
  waiting for transfers between devices: 28.9 us -> 32 us
    all_to_all x0 -> x1, blocking collectives: none -> 19.6 us  [spread(): return lax.all_to_all(copies, axis, split_axis=0, concat_axis=0)]
    all_to_all x4 -> x3, starting transfers between devices: 28.5 us -> 19.8 us  [spread(): return lax.all_to_all(copies, axis, split_axis=0, concat_axis=0)]
    pallas_call x2 -> x1, Pallas kernels: 17.9 us -> 10.8 us  [attention_grads(): pl.pallas_call(grads_kernel, grid_spec=pltpu.PrefetchScalarGridSpec(num_s...]
    ppermute x3 -> x2, starting transfers between devices: 11.4 us -> 6.4 us  [local(): lax.ppermute(sums, 'y', [(i, i ^ bit) for i in range(lax.axis_size('y'))])]
    pallas_call x1, Pallas kernels: 14.6 us -> 9.94 us  [attention_probs(): pl.pallas_call(probs_kernel, grid_spec=pltpu.PrefetchScalarGridSpec(num_s...]
    unnamed x45 -> x35, local copies, waits for them, and re-layouts: 5.67 us -> 1.86 us
    ppermute x3 -> x2, waiting for transfers between devices: 6.99 us -> 3.59 us  [local(): lax.ppermute(sums, 'y', [(i, i ^ bit) for i in range(lax.axis_size('y'))])]
    all_to_all x1, waiting for transfers between devices: 0.01 us -> 2.46 us  [local(): ctx_t = lax.all_to_all(ctx_t, TIME, split_axis=0, concat_axis=0)]
  transfers between devices with their start and end apart: 18 -> 16, of which waited for: 10 -> 10; matrix products, arithmetic and copies ran while one was open for 7% -> 5% of each run, Pallas kernels for 21% -> 16%
where the time goes in v4:
time: 192 us; the launch traced here: 191 us
  starting transfers between devices  69.7 us (36%)
  waiting for transfers between devices  32 us (17%)
  Pallas kernels  30.2 us (16%)
  blocking collectives  19.6 us (10%)
  between operations  14.6 us (8%)
  local copies, waits for them, and re-layouts  9.94 us (5%)
  matrix products  9.62 us (5%)
  other arithmetic  5.01 us (3%)
    all_to_all x3, starting transfers between devices, spread(): return lax.all_to_all(copies, axis, split_axis=0, concat_axis=0)  19.8 us
    all_to_all x1, blocking collectives, spread(): return lax.all_to_all(copies, axis, split_axis=0, concat_axis=0)  19.6 us
    ppermute x4, starting transfers between devices, swap(): return lax.ppermute(array, 'core', [(0, 1), (1, 0)])  12.7 us
    pallas_call x1, Pallas kernels, attention_grads(): pl.pallas_call(grads_kernel, grid_spec=pltpu.PrefetchScalarGridSpec(num_s...  10.8 us
    pallas_call x1, Pallas kernels, attention_probs(): pl.pallas_call(probs_kernel, grid_spec=pltpu.PrefetchScalarGridSpec(num_s...  9.94 us
    all_to_all x1, starting transfers between devices, local(): lax.all_to_all(rows.reshape(n_seq, (KW + 1) // n_seq, width), TIME, split...  9.67 us
    ppermute x2, starting transfers between devices, padded(): low = lax.ppermute(block[block.shape[0] - width:], TIME, forward)  9.43 us
    dot_general x4, matrix products, row_product(): jnp.einsum('tc,rc->tr', active, piece, preferred_element_type=jnp.float32)  7.87 us
  transfers between devices with their start and end apart: 16, of which 10 were waited for; matrix products, arithmetic and copies ran while one was open for 5% of the time, Pallas kernels for 16%

profile of v4, /device:TPU:1, one launch (start us, length us, event | category | flops | bytes accessed | tf_op | source)
XLA Modules:
  0.0 190.6 jit_solution(6452907872825227770)
XLA Ops:
  10.7 7.7 %all-to-all-start = ((bf16[8,40,640]{2,1,0:T(8,128)(2,1)}), bf16[8,40,640]{2,1,0:T(8,128)(2,1)S(1)}, u32[]{:S(2)}, u32[]{:S(2)}) async-start(bf16[8,40,640]{2,1,0:T(8,128)(2,1)} %broadcast_in_dim.59), calls=%async_computation | async-start | bytes 819200 | tf_op jit(solution)/shard_map/all_to_all | solution.py:44
  19.7 4.8 %collective-permute-start = (bf16[16,1280]{1,0:T(8,128)(2,1)S(1)}, bf16[16,1280]{1,0:T(8,128)(2,1)S(1)}, u32[]{:S(2)}, u32[]{:S(2)}) collective-permute-start(bf16[16,1280]{1,0:T(8,128)(2,1)S(1)} %get-tuple-element.61), channel_id=1, source_target_pairs={{0,1},{1,2},{2,3},{3,4},{4,5},{5,6},{6,7},{7,8},{8,9},{9,10},{10,1... | collective-permute-start | bytes 122888 | tf_op jit(solution)/shard_map/ppermute | solution.py:36
  26.7 3.6 %all-to-all-done = bf16[8,40,640]{2,1,0:T(8,128)(2,1)S(1)} async-done(((bf16[8,40,640]{2,1,0:T(8,128)(2,1)}), bf16[8,40,640]{2,1,0:T(8,128)(2,1)S(1)}, u32[]{:S(2)}, u32[]{:S(2)}) %all-to-all-start) | async-done | bytes 409632 | tf_op jit(solution)/shard_map/all_to_all | solution.py:44
  31.6 6.9 %all-to-all-start.1 = ((bf16[4,8,40,640]{3,2,1,0:T(8,128)(2,1)}), bf16[4,8,40,640]{3,2,1,0:T(8,128)(2,1)}, u32[]{:S(2)}, u32[]{:S(2)}) async-start(bf16[4,8,40,640]{3,2,1,0:T(8,128)(2,1)} %broadcast_in_dim.98), calls=%async_computation.1 | async-start | bytes 3276800 | tf_op jit(solution)/shard_map/all_to_all | solution.py:44
  39.2 3.5 %collective-permute-start.2 = (bf16[128,640]{1,0:T(8,128)(2,1)}, bf16[128,640]{1,0:T(8,128)(2,1)S(1)}, u32[]{:S(2)}, u32[]{:S(2)}) collective-permute-start(bf16[128,640]{1,0:T(8,128)(2,1)} %constant_dynamic-slice_fusion.6), channel_id=1, source_target_pairs={{0,1},{1,0},{2,3},{3,2},{4,5},{5,4},{6,7},{7,6},{8,9},{9,8},{10,11... | collective-permute-start | bytes 491528 | tf_op jit(solution)/shard_map/ppermute | solution.py:59
  43.5 2.9 %conv_factor.1 = f32[128,1280]{1,0:T(8,128)S(1)} custom-call(s32[160,128]{1,0:T(8,128)S(1)} %broadcast_in_dim.58.seg, bf16[160,1280]{1,0:T(8,128)(2,1)S(1)} %pad_maximum_fusion.glu, f32[31,1280]{1,0:T(8,128)S(1)} %copy-done.3), custom_call_target="tpu_custom_call" | custom-call | flops 20316160 | bytes 1310720 | tf_op jit(solution)/shard_map/conv_factor/pallas_call | solution.py:96
  47.5 9.9 %attention_probs.1 = (bf16[4,2048,512]{2,1,0:T(8,128)(2,1)}, f32[80,2048]{1,0:T(8,128)S(1)}, f32[1,2048]{1,0:T(1,128)S(1)}) custom-call(s32[2,4]{1,0:T(2,128)S(1)} %pad_add_fusion.bounds, bf16[80,2048]{1,0:T(8,128)(2,1)S(1)} %bitcast.20, bf16[2048,80]{1,0:T(8,128)(2,1)S(1)} %copy.28.k, bf16[80,2048]{1,0:T(8,128)(2,1)S(1)} %bitcast.21, ...), custom_call_target="tpu_custom_call" | custom-call | flops 1342177280 | bytes 8388608 | tf_op jit(solution)/shard_map/attention_probs/pallas_call | solution.py:233
  62.0 4.3 %collective-permute-start.3 = (bf16[128,1280]{1,0:T(8,128)(2,1)S(1)}, bf16[128,1280]{1,0:T(8,128)(2,1)S(1)}, u32[]{:S(2)}, u32[]{:S(2)}) collective-permute-start(bf16[128,1280]{1,0:T(8,128)(2,1)S(1)} %convolution_convert_fusion), channel_id=1, source_target_pairs={{0,1},{1,0},{2,3},{3,2},{4,5},{5,4},{6,7},{7,6},{8,9},{9,8},{10,11... | collective-permute-start | bytes 983048 | tf_op jit(solution)/shard_map/ppermute | solution.py:59
  67.7 4.6 %collective-permute-start.4 = (bf16[16,1280]{1,0:T(8,128)(2,1)S(1)}, bf16[16,1280]{1,0:T(8,128)(2,1)S(1)}, u32[]{:S(2)}, u32[]{:S(2)}) collective-permute-start(bf16[16,1280]{1,0:T(8,128)(2,1)S(1)} %get-tuple-element.59), channel_id=1, source_target_pairs={{0,1},{1,2},{2,3},{3,4},{4,5},{5,6},{6,7},{7,8},{8,9},{9,10},{10,1... | collective-permute-start | bytes 122888 | tf_op jit(solution)/shard_map/ppermute | solution.py:36
  74.3 3.8 %collective-permute-done.5 = bf16[16,1280]{1,0:T(8,128)(2,1)S(1)} collective-permute-done((bf16[16,1280]{1,0:T(8,128)(2,1)S(1)}, bf16[16,1280]{1,0:T(8,128)(2,1)S(1)}, u32[]{:S(2)}, u32[]{:S(2)}) %collective-permute-start.5) | collective-permute-done | bytes 40992 | tf_op jit(solution)/shard_map/ppermute | solution.py:37
  78.1 6.5 %conv_grads.1 = (bf16[128,1280]{1,0:T(8,128)(2,1)S(1)}, bf16[128,1280]{1,0:T(8,128)(2,1)S(1)}, f32[32,1280]{1,0:T(8,128)S(1)}) custom-call(s32[160,128]{1,0:T(8,128)S(1)} %broadcast_in_dim.58.seg, bf16[160,1280]{1,0:T(8,128)(2,1)S(1)} %pad_maximum_fusion.1.grad, bf16[160,1280]{1,0:T(8,128)(2,1)S(1)} %pad_maximum_fusion.glu, bf16[128,2560]{1,0:T(8,128)(2,1)S(1)} %copy-done.1, ...), custom_call_target="tpu_custom_call" | custom-call | flops 40632320 | bytes 2621440 | tf_op jit(solution)/shard_map/conv_grads/pallas_call | solution.py:145
  85.4 9.7 %all-to-all-start.2 = ((f32[16,2,1280]{2,1,0:T(2,128)}), f32[16,2,1280]{2,1,0:T(2,128)S(1)}, u32[]{:S(2)}, u32[]{:S(2)}) async-start(f32[16,2,1280]{2,1,0:T(2,128)} %reshape.64), calls=%async_computation.2 | async-start | bytes 327680 | tf_op jit(solution)/shard_map/all_to_all | solution.py:389
  97.3 7.4 %all-to-all-done.2 = f32[16,2,1280]{2,1,0:T(2,128)S(1)} async-done(((f32[16,2,1280]{2,1,0:T(2,128)}), f32[16,2,1280]{2,1,0:T(2,128)S(1)}, u32[]{:S(2)}, u32[]{:S(2)}) %all-to-all-start.2) | async-done | bytes 163872 | tf_op jit(solution)/shard_map/all_to_all | solution.py:389
  104.8 7.2 %all-gather.2.cloned.1.call-done = bf16[1280,2560]{1,0:T(8,128)(2,1)} async-done(((bf16[40,2560]{1,0:T(8,128)(2,1)}), bf16[1280,2560]{1,0:T(8,128)(2,1)}) %all-gather.2.cloned.1.call-update) | async-done | bytes 6553616 | tf_op jit(solution)/shard_map/all_gather | solution.py:358
  111.9 3.3 %fusion.6 = bf16[128,1280]{1,0:T(8,128)(2,1)S(1)} fusion(bf16[128,1280]{1,0:T(8,128)(2,1)S(1)} %collective-permute-done.6, bf16[1280,2560]{1,0:T(8,128)(2,1)} %all-gather.2.cloned.1.call-done), kind=kOutput, calls=%fused_computation.6 | convolution fusion | flops 419594240 | bytes 3932160 | tf_op jit(solution)/shard_map/tc,rc->tr/dot_general | solution.py:48
  115.2 2.9 %collective-permute-start.7 = (bf16[128,1280]{1,0:T(8,128)(2,1)S(1)}, bf16[128,1280]{1,0:T(8,128)(2,1)S(1)}, u32[]{:S(2)}, u32[]{:S(2)}) collective-permute-start(bf16[128,1280]{1,0:T(8,128)(2,1)S(1)} %fusion.6), channel_id=1, source_target_pairs={{0,1},{1,0},{2,3},{3,2},{4,5},{5,4},{6,7},{7,6},{8,9},{9,8},{10,11... | collective-permute-start | bytes 983048 | tf_op jit(solution)/shard_map/ppermute | solution.py:59
  119.4 3.4 %fusion.22 = (f32[1280]{0:T(1024)S(1)}, f32[128]{0:T(128)S(1)}, f32[128]{0:T(128)S(1)}, f32[128,1280]{1,0:T(8,128)S(1)}) fusion(bf16[128,1280]{1,0:T(8,128)(2,1)S(1)} %copy-done.7, f32[128]{0:T(128)S(1)} %add_rsqrt_fusion, f32[128]{0:T(128)S(1)} %broadcast_multiply_fusion.2, f32[1280]{0:T(1024)S(1)} %copy-done.12, ...), kind=kOutput, calls=%fused_computation.21 | convolution fusion | flops 421886464 | bytes 4927488 | tf_op jit(solution)/shard_map/tc,rc->tr/dot_general | solution.py:48
  125.0 7.8 %all-to-all-start.3 = ((bf16[16,80,128]{2,1,0:T(8,128)(2,1)}), bf16[16,80,128]{2,1,0:T(8,128)(2,1)S(1)}, u32[]{:S(2)}, u32[]{:S(2)}) async-start(bf16[16,80,128]{2,1,0:T(8,128)(2,1)} %bitcast.8), calls=%async_computation.3 | async-start | bytes 655360 | tf_op jit(solution)/shard_map/all_to_all | solution.py:417
  132.7 3.0 %collective-permute-start.8 = (f32[3,1280]{1,0:T(4,128)S(1)}, f32[3,1280]{1,0:T(4,128)S(1)}, u32[]{:S(2)}, u32[]{:S(2)}) collective-permute-start(f32[3,1280]{1,0:T(4,128)S(1)} %pad_maximum_fusion.4), channel_id=1, source_target_pairs={{0,64},{64,0},{128,192},{192,128},{1,65},{65,1},{129,193},{193,129... | collective-permute-start | bytes 46088 | tf_op jit(solution)/shard_map/ppermute | solution.py:420
  137.6 3.4 %collective-permute-start.9 = (f32[3,1280]{1,0:T(4,128)S(1)}, f32[3,1280]{1,0:T(4,128)S(1)}, u32[]{:S(2)}, u32[]{:S(2)}) collective-permute-start(f32[3,1280]{1,0:T(4,128)S(1)} %fusion.35), channel_id=1, source_target_pairs={{0,128},{64,192},{128,0},{192,64},{1,129},{65,193},{129,1},{193,65... | collective-permute-start | bytes 46088 | tf_op jit(solution)/shard_map/ppermute | solution.py:420
  143.3 2.5 %all-to-all-done.3.ctx_t = bf16[16,80,128]{2,1,0:T(8,128)(2,1)S(1)} async-done(((bf16[16,80,128]{2,1,0:T(8,128)(2,1)}), bf16[16,80,128]{2,1,0:T(8,128)(2,1)S(1)}, u32[]{:S(2)}, u32[]{:S(2)}) %all-to-all-start.3) | async-done | bytes 327712 | tf_op jit(solution)/shard_map/all_to_all | solution.py:417
  146.5 5.2 %all-to-all-start.4 = ((f32[8,3,1280]{2,1,0:T(4,128)}), f32[8,3,1280]{2,1,0:T(4,128)S(1)}, u32[]{:S(2)}, u32[]{:S(2)}) async-start(f32[8,3,1280]{2,1,0:T(4,128)} %broadcast_in_dim.102), calls=%async_computation.4 | async-start | bytes 327680 | tf_op jit(solution)/shard_map/all_to_all | solution.py:44
  151.7 10.8 %attention_grads.1 = (bf16[80,2048]{1,0:T(8,128)(2,1)}, bf16[80,2048]{1,0:T(8,128)(2,1)}, bf16[80,2048]{1,0:T(8,128)(2,1)}) custom-call(s32[2,4]{1,0:T(2,128)S(1)} %pad_add_fusion.bounds, bf16[4,2048,512]{2,1,0:T(8,128)(2,1)} %get-tuple-element.41.probs, bf16[16,80,128]{2,1,0:T(8,128)(2,1)S(1)} %all-to-all-done.3.ctx_t, ...), custom_call_target="tpu_custom_call" | custom-call | flops 2684354560 | bytes 8388608 | tf_op jit(solution)/shard_map/attention_grads/pallas_call | solution.py:308
  162.6 19.6 %all_to_all.30 = f32[16,3,1280]{2,1,0:T(4,128)S(1)} all-to-all(f32[16,3,1280]{2,1,0:T(4,128)S(1)} %broadcast_in_dim.103), channel_id=1, replica_groups=mesh['far'=2,'y'=4,'x'=4,'z'=8,'core'=2] {'z','core'}, dimensions={0} | all-to-all | bytes 491520 | tf_op jit(solution)/shard_map/all_to_all | solution.py:44
  (101 shorter events, 31.4 us)
Async XLA Ops:
  7.2 19.3 %copy-start.13 = (s32[1,8]{1,0:T(1,128)S(1)}, s32[1,8]{1,0:T(1,128)}, u32[]{:S(2)}) copy-start(s32[1,8]{1,0:T(1,128)} %param.18) | copy-start | bytes 100
  7.2 104.7 %all-gather.2.cloned.1.call-start = ((), (), s32[]{:S(2)}) async-start(), calls=%async_computation.6 | async-start | bytes 6758400 | tf_op jit(solution)/shard_map/all_gather | solution.py:358
  10.7 19.6 %all-to-all-start = ((bf16[8,40,640]{2,1,0:T(8,128)(2,1)}), bf16[8,40,640]{2,1,0:T(8,128)(2,1)S(1)}, u32[]{:S(2)}, u32[]{:S(2)}) async-start(bf16[8,40,640]{2,1,0:T(8,128)(2,1)} %broadcast_in_dim.59), calls=%async_computation | async-start | bytes 819200 | tf_op jit(solution)/shard_map/all_to_all | solution.py:44
  18.3 20.2 %copy-start.8 = (bf16[128,1280]{1,0:T(8,128)(2,1)S(1)}, bf16[128,1280]{1,0:T(8,128)(2,1)}, u32[]{:S(2)}) copy-start(bf16[128,1280]{1,0:T(8,128)(2,1)} %param.12) | copy-start | bytes 983044
  18.3 24.8 %copy-start.2 = (bf16[2048,80]{0,1:T(8,128)(2,1)S(1)}, bf16[2048,80]{0,1:T(8,128)(2,1)}, u32[]{:S(2)}) copy-start(bf16[2048,80]{0,1:T(8,128)(2,1)} %param.16) | copy-start | bytes 983044
  19.7 23.7 %collective-permute-start = (bf16[16,1280]{1,0:T(8,128)(2,1)S(1)}, bf16[16,1280]{1,0:T(8,128)(2,1)S(1)}, u32[]{:S(2)}, u32[]{:S(2)}) collective-permute-start(bf16[16,1280]{1,0:T(8,128)(2,1)S(1)} %get-tuple-element.61), channel_id=1, source_target_pairs={{0,1},{1,2},{2,3},{3,4},{4,5},{5,6},{6,7},{7,8},{8,9},{9,10},{10,1... | collective-permute-start | bytes 122888 | tf_op jit(solution)/shard_map/ppermute | solution.py:36
  24.5 18.9 %collective-permute-start.1 = (bf16[16,1280]{1,0:T(8,128)(2,1)S(1)}, bf16[16,1280]{1,0:T(8,128)(2,1)S(1)}, u32[]{:S(2)}, u32[]{:S(2)}) collective-permute-start(bf16[16,1280]{1,0:T(8,128)(2,1)S(1)} %get-tuple-element.62), channel_id=1, source_target_pairs={{1,0},{2,1},{3,2},{4,3},{5,4},{6,5},{7,6},{8,7},{9,8},{10,9},{11,1... | collective-permute-start | bytes 122888 | tf_op jit(solution)/shard_map/ppermute | solution.py:37
  31.6 14.9 %copy-start.4 = (bf16[2048,80]{0,1:T(8,128)(2,1)S(1)}, bf16[2048,80]{0,1:T(8,128)(2,1)}, u32[]{:S(2)}) copy-start(bf16[2048,80]{0,1:T(8,128)(2,1)} %param.15) | copy-start | bytes 983044
  31.6 28.2 %all-to-all-start.1 = ((bf16[4,8,40,640]{3,2,1,0:T(8,128)(2,1)}), bf16[4,8,40,640]{3,2,1,0:T(8,128)(2,1)}, u32[]{:S(2)}, u32[]{:S(2)}) async-start(bf16[4,8,40,640]{3,2,1,0:T(8,128)(2,1)} %broadcast_in_dim.98), calls=%async_computation.1 | async-start | bytes 3276800 | tf_op jit(solution)/shard_map/all_to_all | solution.py:44
  39.2 22.2 %collective-permute-start.2 = (bf16[128,640]{1,0:T(8,128)(2,1)}, bf16[128,640]{1,0:T(8,128)(2,1)S(1)}, u32[]{:S(2)}, u32[]{:S(2)}) collective-permute-start(bf16[128,640]{1,0:T(8,128)(2,1)} %constant_dynamic-slice_fusion.6), channel_id=1, source_target_pairs={{0,1},{1,0},{2,3},{3,2},{4,5},{5,4},{6,7},{7,6},{8,9},{9,8},{10,11... | collective-permute-start | bytes 491528 | tf_op jit(solution)/shard_map/ppermute | solution.py:59
  61.4 16.6 %copy-start.1 = (bf16[128,2560]{1,0:T(8,128)(2,1)S(1)}, bf16[128,2560]{1,0:T(8,128)(2,1)}, u32[]{:S(2)}) copy-start(bf16[128,2560]{1,0:T(8,128)(2,1)} %gate_ref.1) | copy-start | bytes 1966084
  62.0 5.5 %collective-permute-start.3 = (bf16[128,1280]{1,0:T(8,128)(2,1)S(1)}, bf16[128,1280]{1,0:T(8,128)(2,1)S(1)}, u32[]{:S(2)}, u32[]{:S(2)}) collective-permute-start(bf16[128,1280]{1,0:T(8,128)(2,1)S(1)} %convolution_convert_fusion), channel_id=1, source_target_pairs={{0,1},{1,0},{2,3},{3,2},{4,5},{5,4},{6,7},{7,6},{8,9},{9,8},{10,11... | collective-permute-start | bytes 983048 | tf_op jit(solution)/shard_map/ppermute | solution.py:59
  67.7 29.5 %copy-start.7 = (bf16[128,1280]{1,0:T(8,128)(2,1)S(1)}, bf16[128,1280]{1,0:T(8,128)(2,1)}, u32[]{:S(2)}) copy-start(bf16[128,1280]{1,0:T(8,128)(2,1)} %param.13) | copy-start | bytes 983044
  67.7 6.5 %collective-permute-start.4 = (bf16[16,1280]{1,0:T(8,128)(2,1)S(1)}, bf16[16,1280]{1,0:T(8,128)(2,1)S(1)}, u32[]{:S(2)}, u32[]{:S(2)}) collective-permute-start(bf16[16,1280]{1,0:T(8,128)(2,1)S(1)} %get-tuple-element.59), channel_id=1, source_target_pairs={{0,1},{1,2},{2,3},{3,4},{4,5},{5,6},{6,7},{7,8},{8,9},{9,10},{10,1... | collective-permute-start | bytes 122888 | tf_op jit(solution)/shard_map/ppermute | solution.py:36
  72.3 5.7 %collective-permute-start.5 = (bf16[16,1280]{1,0:T(8,128)(2,1)S(1)}, bf16[16,1280]{1,0:T(8,128)(2,1)S(1)}, u32[]{:S(2)}, u32[]{:S(2)}) collective-permute-start(bf16[16,1280]{1,0:T(8,128)(2,1)S(1)} %get-tuple-element.60), channel_id=1, source_target_pairs={{1,0},{2,1},{3,2},{4,3},{5,4},{6,5},{7,6},{8,7},{9,8},{10,9},{11,1... | collective-permute-start | bytes 122888 | tf_op jit(solution)/shard_map/ppermute | solution.py:37
  85.4 19.3 %all-to-all-start.2 = ((f32[16,2,1280]{2,1,0:T(2,128)}), f32[16,2,1280]{2,1,0:T(2,128)S(1)}, u32[]{:S(2)}, u32[]{:S(2)}) async-start(f32[16,2,1280]{2,1,0:T(2,128)} %reshape.64), calls=%async_computation.2 | async-start | bytes 327680 | tf_op jit(solution)/shard_map/all_to_all | solution.py:389
  95.2 24.2 %copy-start.12 = (f32[1280]{0:T(1024)S(1)}, f32[1280]{0:T(1024)}, u32[]{:S(2)}) copy-start(f32[1280]{0:T(1024)} %param.19) | copy-start | bytes 15364
  95.2 16.7 %collective-permute-start.6 = (bf16[128,1280]{1,0:T(8,128)(2,1)S(1)}, bf16[128,1280]{1,0:T(8,128)(2,1)S(1)}, u32[]{:S(2)}, u32[]{:S(2)}) collective-permute-start(bf16[128,1280]{1,0:T(8,128)(2,1)S(1)} %pad_maximum_fusion.2), channel_id=1, source_target_pairs={{0,1},{1,0},{2,3},{3,2},{4,5},{5,4},{6,7},{7,6},{8,9},{9,8},{10,11... | collective-permute-start | bytes 983048 | tf_op jit(solution)/shard_map/ppermute | solution.py:59
  115.2 4.1 %collective-permute-start.7 = (bf16[128,1280]{1,0:T(8,128)(2,1)S(1)}, bf16[128,1280]{1,0:T(8,128)(2,1)S(1)}, u32[]{:S(2)}, u32[]{:S(2)}) collective-permute-start(bf16[128,1280]{1,0:T(8,128)(2,1)S(1)} %fusion.6), channel_id=1, source_target_pairs={{0,1},{1,0},{2,3},{3,2},{4,5},{5,4},{6,7},{7,6},{8,9},{9,8},{10,11... | collective-permute-start | bytes 983048 | tf_op jit(solution)/shard_map/ppermute | solution.py:59
  123.2 18.1 %copy-start.6 = (bf16[2048,80]{0,1:T(8,128)(2,1)S(1)}, bf16[2048,80]{0,1:T(8,128)(2,1)}, u32[]{:S(2)}) copy-start(bf16[2048,80]{0,1:T(8,128)(2,1)} %param.17) | copy-start | bytes 983044
  125.0 20.8 %all-to-all-start.3 = ((bf16[16,80,128]{2,1,0:T(8,128)(2,1)}), bf16[16,80,128]{2,1,0:T(8,128)(2,1)S(1)}, u32[]{:S(2)}, u32[]{:S(2)}) async-start(bf16[16,80,128]{2,1,0:T(8,128)(2,1)} %bitcast.8), calls=%async_computation.3 | async-start | bytes 655360 | tf_op jit(solution)/shard_map/all_to_all | solution.py:417
  132.7 4.8 %collective-permute-start.8 = (f32[3,1280]{1,0:T(4,128)S(1)}, f32[3,1280]{1,0:T(4,128)S(1)}, u32[]{:S(2)}, u32[]{:S(2)}) collective-permute-start(f32[3,1280]{1,0:T(4,128)S(1)} %pad_maximum_fusion.4), channel_id=1, source_target_pairs={{0,64},{64,0},{128,192},{192,128},{1,65},{65,1},{129,193},{193,129... | collective-permute-start | bytes 46088 | tf_op jit(solution)/shard_map/ppermute | solution.py:420
  137.6 5.7 %collective-permute-start.9 = (f32[3,1280]{1,0:T(4,128)S(1)}, f32[3,1280]{1,0:T(4,128)S(1)}, u32[]{:S(2)}, u32[]{:S(2)}) collective-permute-start(f32[3,1280]{1,0:T(4,128)S(1)} %fusion.35), channel_id=1, source_target_pairs={{0,128},{64,192},{128,0},{192,64},{1,129},{65,193},{129,1},{193,65... | collective-permute-start | bytes 46088 | tf_op jit(solution)/shard_map/ppermute | solution.py:420
  146.5 16.0 %all-to-all-start.4 = ((f32[8,3,1280]{2,1,0:T(4,128)}), f32[8,3,1280]{2,1,0:T(4,128)S(1)}, u32[]{:S(2)}, u32[]{:S(2)}) async-start(f32[8,3,1280]{2,1,0:T(4,128)} %broadcast_in_dim.102), calls=%async_computation.4 | async-start | bytes 327680 | tf_op jit(solution)/shard_map/all_to_all | solution.py:44
  (8 other events, 46.1 us)
Sparse Core Ops, SparseCore 0:
  11.8 100.1 all-gather.1

commit v5 on v4

--- a/solution.py
+++ b/solution.py
@@ -386,10 +386,9 @@
     low_own, low_away = halves(low_grad, core)
     high_own, high_away = halves(high_grad, core)
 
-    rows = lax.all_to_all(
-        rows.reshape(n_seq, (KW + 1) // n_seq, width), TIME, split_axis=0, concat_axis=0
-    )
-    rows = jnp.sum(rows, axis=0)
+    rows = rows.reshape(2, n_seq // 2, (KW + 1) // n_seq, width).transpose(1, 0, 2, 3)
+    rows = rows.reshape(n_seq, (KW + 1) // n_seq, width)
+    rows = jnp.sum(lax.all_to_all(rows, TIME, split_axis=0, concat_axis=0), axis=0)
 
     gathered, rows = lax.optimization_barrier((gathered, rows))
     w_in_half = gathered[:, :width]
@@ -416,17 +415,17 @@
     ctx_t, gain = lax.optimization_barrier((ctx_t, gain))
     ctx_t = lax.all_to_all(ctx_t, TIME, split_axis=0, concat_axis=0)
     sums = jnp.concatenate([rows, gain], axis=0)
-    for bit in (1, 2):
-        sums = sums + lax.ppermute(sums, "y", [(i, i ^ bit) for i in range(lax.axis_size("y"))])
+    for axis in (("far", "y"), "x"):
+        sums = jnp.sum(lax.all_gather(sums, axis), axis=0)
     ctx_t, sums = lax.optimization_barrier((ctx_t, sums))
     probs = pltpu.with_memory_space_constraint(probs, pltpu.HBM)
-    stacked = spread(sums, ("far", "x"))
+    stacked = spread(sums, "z")
     grads = attention_grads(bounds, probs, ctx_t, out_t, inv_sum, queries, keys.T, values)
     query_grad, key_grad, value_grad = [array.T for array in grads]
     stacked, query_grad = lax.optimization_barrier((stacked, query_grad))
-    stacked = spread(jnp.sum(stacked, axis=0), TIME)
-    kernel_grad = stacked[:, :-1].reshape(KW + 1, width)[:KW]
-    gain_grad = jnp.sum(stacked[:, -1], axis=0)
+    stacked = lax.all_gather(stacked, "core", axis=0)
+    kernel_grad = stacked[:, :, :-1].reshape(KW + 1, width)[:KW]
+    gain_grad = jnp.sum(stacked[:, :, -1], axis=(0, 1))
     return (resid_grad, query_grad, key_grad, value_grad, kernel_grad, gain_grad)
 
 

time: 192 us -> 200 us (1.042)
  blocking collectives: 19.6 us -> 39.1 us
  waiting for transfers between devices: 32 us -> 26.1 us
  starting transfers between devices: 69.7 us -> 64.4 us
    all_gather x0 -> x3, blocking collectives: none -> 39.1 us  [the longest x2 27.8 us: local(): sums = jnp.sum(lax.all_gather(sums, axis), axis=0)]
    all_to_all x1 -> x0, blocking collectives: 19.6 us -> none  [spread(): return lax.all_to_all(copies, axis, split_axis=0, concat_axis=0)]
    ppermute x2 -> x0, starting transfers between devices: 6.4 us -> none  [local(): lax.ppermute(sums, 'y', [(i, i ^ bit) for i in range(lax.axis_size('y'))])]
    ppermute x2 -> x0, waiting for transfers between devices: 3.59 us -> none  [local(): lax.ppermute(sums, 'y', [(i, i ^ bit) for i in range(lax.axis_size('y'))])]
    all_to_all x1, waiting for transfers between devices: 2.46 us -> 0.01 us  [local(): ctx_t = lax.all_to_all(ctx_t, TIME, split_axis=0, concat_axis=0)]
  transfers between devices with their start and end apart: 16 -> 14, of which waited for: 10 -> 7; matrix products, arithmetic and copies ran while one was open for 5% -> 5% of each run, Pallas kernels for 16% -> 15%
where the time goes in v5:
time: 200 us; the launch traced here: 198 us
  starting transfers between devices  64.4 us (32%)
  blocking collectives  39.1 us (20%)
  Pallas kernels  29.7 us (15%)
  waiting for transfers between devices  26.1 us (13%)
  between operations  14.6 us (7%)
  local copies, waits for them, and re-layouts  10 us (5%)
  matrix products  9.62 us (5%)
  other arithmetic  4.94 us (2%)
    all_gather x2, blocking collectives, local(): sums = jnp.sum(lax.all_gather(sums, axis), axis=0)  27.8 us
    all_to_all x3, starting transfers between devices, spread(): return lax.all_to_all(copies, axis, split_axis=0, concat_axis=0)  20.9 us
    ppermute x4, starting transfers between devices, swap(): return lax.ppermute(array, 'core', [(0, 1), (1, 0)])  12.8 us
    all_gather x1, blocking collectives, local(): stacked = lax.all_gather(stacked, 'core', axis=0)  11.2 us
    pallas_call x1, Pallas kernels, attention_grads(): pl.pallas_call(grads_kernel, grid_spec=pltpu.PrefetchScalarGridSpec(num_s...  10.6 us
    all_to_all x1, starting transfers between devices, local(): lax.all_to_all(rows, TIME, split_axis=0, concat_axis=0)  9.66 us
    pallas_call x1, Pallas kernels, attention_probs(): pl.pallas_call(probs_kernel, grid_spec=pltpu.PrefetchScalarGridSpec(num_s...  9.64 us
    ppermute x2, starting transfers between devices, padded(): low = lax.ppermute(block[block.shape[0] - width:], TIME, forward)  9.47 us
  transfers between devices with their start and end apart: 14, of which 7 were waited for; matrix products, arithmetic and copies ran while one was open for 5% of the time, Pallas kernels for 15%

profile of v5, /device:TPU:1, one launch (start us, length us, event | category | flops | bytes accessed | tf_op | source)
XLA Modules:
  0.0 198.5 jit_solution(1419266431607321031)
XLA Ops:
  10.7 7.7 %all-to-all-start = ((bf16[8,40,640]{2,1,0:T(8,128)(2,1)}), bf16[8,40,640]{2,1,0:T(8,128)(2,1)S(1)}, u32[]{:S(2)}, u32[]{:S(2)}) async-start(bf16[8,40,640]{2,1,0:T(8,128)(2,1)} %broadcast_in_dim.57), calls=%async_computation | async-start | bytes 819200 | tf_op jit(solution)/shard_map/all_to_all | solution.py:44
  19.7 4.8 %collective-permute-start = (bf16[16,1280]{1,0:T(8,128)(2,1)S(1)}, bf16[16,1280]{1,0:T(8,128)(2,1)S(1)}, u32[]{:S(2)}, u32[]{:S(2)}) collective-permute-start(bf16[16,1280]{1,0:T(8,128)(2,1)S(1)} %get-tuple-element.61), channel_id=1, source_target_pairs={{0,1},{1,2},{2,3},{3,4},{4,5},{5,6},{6,7},{7,8},{8,9},{9,10},{10,1... | collective-permute-start | bytes 122888 | tf_op jit(solution)/shard_map/ppermute | solution.py:36
  26.7 3.6 %all-to-all-done = bf16[8,40,640]{2,1,0:T(8,128)(2,1)S(1)} async-done(((bf16[8,40,640]{2,1,0:T(8,128)(2,1)}), bf16[8,40,640]{2,1,0:T(8,128)(2,1)S(1)}, u32[]{:S(2)}, u32[]{:S(2)}) %all-to-all-start) | async-done | bytes 409632 | tf_op jit(solution)/shard_map/all_to_all | solution.py:44
  31.6 6.9 %all-to-all-start.1 = ((bf16[4,8,40,640]{3,2,1,0:T(8,128)(2,1)}), bf16[4,8,40,640]{3,2,1,0:T(8,128)(2,1)}, u32[]{:S(2)}, u32[]{:S(2)}) async-start(bf16[4,8,40,640]{3,2,1,0:T(8,128)(2,1)} %broadcast_in_dim.92), calls=%async_computation.1 | async-start | bytes 3276800 | tf_op jit(solution)/shard_map/all_to_all | solution.py:44
  39.2 3.5 %collective-permute-start.2 = (bf16[128,640]{1,0:T(8,128)(2,1)}, bf16[128,640]{1,0:T(8,128)(2,1)S(1)}, u32[]{:S(2)}, u32[]{:S(2)}) collective-permute-start(bf16[128,640]{1,0:T(8,128)(2,1)} %constant_dynamic-slice_fusion.6), channel_id=1, source_target_pairs={{0,1},{1,0},{2,3},{3,2},{4,5},{5,4},{6,7},{7,6},{8,9},{9,8},{10,11... | collective-permute-start | bytes 491528 | tf_op jit(solution)/shard_map/ppermute | solution.py:59
  43.5 2.9 %conv_factor.1 = f32[128,1280]{1,0:T(8,128)S(1)} custom-call(s32[160,128]{1,0:T(8,128)S(1)} %broadcast_in_dim.56.seg, bf16[160,1280]{1,0:T(8,128)(2,1)S(1)} %pad_maximum_fusion.glu, f32[31,1280]{1,0:T(8,128)S(1)} %copy-done.3), custom_call_target="tpu_custom_call" | custom-call | flops 20316160 | bytes 1310720 | tf_op jit(solution)/shard_map/conv_factor/pallas_call | solution.py:96
  47.5 9.6 %attention_probs.1 = (bf16[4,2048,512]{2,1,0:T(8,128)(2,1)}, f32[80,2048]{1,0:T(8,128)S(1)}, f32[1,2048]{1,0:T(1,128)S(1)}) custom-call(s32[2,4]{1,0:T(2,128)S(1)} %pad_add_fusion.bounds, bf16[80,2048]{1,0:T(8,128)(2,1)S(1)} %bitcast.27, bf16[2048,80]{1,0:T(8,128)(2,1)S(1)} %copy.38.k, bf16[80,2048]{1,0:T(8,128)(2,1)S(1)} %bitcast.28, ...), custom_call_target="tpu_custom_call" | custom-call | flops 1342177280 | bytes 8388608 | tf_op jit(solution)/shard_map/attention_probs/pallas_call | solution.py:233
  57.1 2.7 %all-to-all-done.1 = bf16[4,8,40,640]{3,2,1,0:T(8,128)(2,1)} async-done(((bf16[4,8,40,640]{3,2,1,0:T(8,128)(2,1)}), bf16[4,8,40,640]{3,2,1,0:T(8,128)(2,1)}, u32[]{:S(2)}, u32[]{:S(2)}) %all-to-all-start.1) | async-done | bytes 1638432 | tf_op jit(solution)/shard_map/all_to_all | solution.py:44
  62.0 4.3 %collective-permute-start.3 = (bf16[128,1280]{1,0:T(8,128)(2,1)S(1)}, bf16[128,1280]{1,0:T(8,128)(2,1)S(1)}, u32[]{:S(2)}, u32[]{:S(2)}) collective-permute-start(bf16[128,1280]{1,0:T(8,128)(2,1)S(1)} %convolution_convert_fusion), channel_id=1, source_target_pairs={{0,1},{1,0},{2,3},{3,2},{4,5},{5,4},{6,7},{7,6},{8,9},{9,8},{10,11... | collective-permute-start | bytes 983048 | tf_op jit(solution)/shard_map/ppermute | solution.py:59
  67.7 4.6 %collective-permute-start.4 = (bf16[16,1280]{1,0:T(8,128)(2,1)S(1)}, bf16[16,1280]{1,0:T(8,128)(2,1)S(1)}, u32[]{:S(2)}, u32[]{:S(2)}) collective-permute-start(bf16[16,1280]{1,0:T(8,128)(2,1)S(1)} %get-tuple-element.59), channel_id=1, source_target_pairs={{0,1},{1,2},{2,3},{3,4},{4,5},{5,6},{6,7},{7,8},{8,9},{9,10},{10,1... | collective-permute-start | bytes 122888 | tf_op jit(solution)/shard_map/ppermute | solution.py:36
  74.3 3.8 %collective-permute-done.5 = bf16[16,1280]{1,0:T(8,128)(2,1)S(1)} collective-permute-done((bf16[16,1280]{1,0:T(8,128)(2,1)S(1)}, bf16[16,1280]{1,0:T(8,128)(2,1)S(1)}, u32[]{:S(2)}, u32[]{:S(2)}) %collective-permute-start.5) | collective-permute-done | bytes 40992 | tf_op jit(solution)/shard_map/ppermute | solution.py:37
  78.1 6.5 %conv_grads.1 = (bf16[128,1280]{1,0:T(8,128)(2,1)S(1)}, bf16[128,1280]{1,0:T(8,128)(2,1)S(1)}, f32[32,1280]{1,0:T(8,128)S(1)}) custom-call(s32[160,128]{1,0:T(8,128)S(1)} %broadcast_in_dim.56.seg, bf16[160,1280]{1,0:T(8,128)(2,1)S(1)} %pad_maximum_fusion.1.grad, bf16[160,1280]{1,0:T(8,128)(2,1)S(1)} %pad_maximum_fusion.glu, bf16[128,2560]{1,0:T(8,128)(2,1)S(1)} %copy-done.1, ...), custom_call_target="tpu_custom_call" | custom-call | flops 40632320 | bytes 2621440 | tf_op jit(solution)/shard_map/conv_grads/pallas_call | solution.py:145
  85.4 9.7 %all-to-all-start.2 = ((f32[16,2,1280]{2,1,0:T(2,128)}), f32[16,2,1280]{2,1,0:T(2,128)S(1)}, u32[]{:S(2)}, u32[]{:S(2)}) async-start(f32[16,2,1280]{2,1,0:T(2,128)} %bitcast.9), calls=%async_computation.2 | async-start | bytes 327680 | tf_op jit(solution)/shard_map/all_to_all | solution.py:391
  97.4 7.4 %all-to-all-done.2 = f32[16,2,1280]{2,1,0:T(2,128)S(1)} async-done(((f32[16,2,1280]{2,1,0:T(2,128)}), f32[16,2,1280]{2,1,0:T(2,128)S(1)}, u32[]{:S(2)}, u32[]{:S(2)}) %all-to-all-start.2) | async-done | bytes 163872 | tf_op jit(solution)/shard_map/all_to_all | solution.py:391
  104.8 7.1 %all-gather.7.cloned.1.call-done = bf16[1280,2560]{1,0:T(8,128)(2,1)} async-done(((bf16[40,2560]{1,0:T(8,128)(2,1)}), bf16[1280,2560]{1,0:T(8,128)(2,1)}) %all-gather.7.cloned.1.call-update) | async-done | bytes 6553616 | tf_op jit(solution)/shard_map/all_gather | solution.py:358
  111.9 3.3 %fusion.6 = bf16[128,1280]{1,0:T(8,128)(2,1)S(1)} fusion(bf16[128,1280]{1,0:T(8,128)(2,1)S(1)} %collective-permute-done.6, bf16[1280,2560]{1,0:T(8,128)(2,1)} %all-gather.7.cloned.1.call-done), kind=kOutput, calls=%fused_computation.6 | convolution fusion | flops 419594240 | bytes 3932160 | tf_op jit(solution)/shard_map/tc,rc->tr/dot_general | solution.py:48
  115.2 2.9 %collective-permute-start.7 = (bf16[128,1280]{1,0:T(8,128)(2,1)S(1)}, bf16[128,1280]{1,0:T(8,128)(2,1)S(1)}, u32[]{:S(2)}, u32[]{:S(2)}) collective-permute-start(bf16[128,1280]{1,0:T(8,128)(2,1)S(1)} %fusion.6), channel_id=1, source_target_pairs={{0,1},{1,0},{2,3},{3,2},{4,5},{5,4},{6,7},{7,6},{8,9},{9,8},{10,11... | collective-permute-start | bytes 983048 | tf_op jit(solution)/shard_map/ppermute | solution.py:59
  119.4 3.4 %fusion.22 = (f32[1280]{0:T(1024)S(1)}, f32[128]{0:T(128)S(1)}, f32[128]{0:T(128)S(1)}, f32[128,1280]{1,0:T(8,128)S(1)}) fusion(bf16[128,1280]{1,0:T(8,128)(2,1)S(1)} %copy-done.7, f32[128]{0:T(128)S(1)} %add_rsqrt_fusion, f32[128]{0:T(128)S(1)} %broadcast_multiply_fusion.2, f32[1280]{0:T(1024)S(1)} %copy-done.12, ...), kind=kOutput, calls=%fused_computation.21 | convolution fusion | flops 421886464 | bytes 4927488 | tf_op jit(solution)/shard_map/tc,rc->tr/dot_general | solution.py:48
  125.0 7.8 %all-to-all-start.3 = ((bf16[16,80,128]{2,1,0:T(8,128)(2,1)}), bf16[16,80,128]{2,1,0:T(8,128)(2,1)S(1)}, u32[]{:S(2)}, u32[]{:S(2)}) async-start(bf16[16,80,128]{2,1,0:T(8,128)(2,1)} %bitcast.10), calls=%async_computation.3 | async-start | bytes 655360 | tf_op jit(solution)/shard_map/all_to_all | solution.py:416
  133.3 18.8 %all-gather.3 = f32[8,3,1280]{2,1,0:T(4,128)S(1)} all-gather(f32[1,3,1280]{2,1,0:T(4,128)S(1)} %maximum_bitcast_fusion), channel_id=2, replica_groups=mesh['far'=2,'y'=4,'x'=4,'z'=8,'core'=2] {'far','y'}, dimensions={0}, use_global_device_ids=true | all-gather | bytes 138240 | tf_op jit(solution)/shard_map/all_gather | solution.py:419
  152.2 9.0 %all-gather.4 = f32[4,3,1280]{2,1,0:T(4,128)S(1)} all-gather(f32[1,3,1280]{2,1,0:T(4,128)S(1)} %bitcast.38), channel_id=3, replica_groups=mesh['far'=2,'y'=4,'x'=4,'z'=8,'core'=2] {'x'}, dimensions={0}, use_global_device_ids=true | all-gather | bytes 76800 | tf_op jit(solution)/shard_map/all_gather | solution.py:419
  161.9 6.3 %all-to-all-start.4 = ((f32[8,3,1280]{2,1,0:T(4,128)}), f32[8,3,1280]{2,1,0:T(4,128)S(1)}, u32[]{:S(2)}, u32[]{:S(2)}) async-start(f32[8,3,1280]{2,1,0:T(4,128)} %broadcast_in_dim.96), calls=%async_computation.4 | async-start | bytes 327680 | tf_op jit(solution)/shard_map/all_to_all | solution.py:44
  168.2 10.6 %attention_grads.1 = (bf16[80,2048]{1,0:T(8,128)(2,1)}, bf16[80,2048]{1,0:T(8,128)(2,1)}, bf16[80,2048]{1,0:T(8,128)(2,1)}) custom-call(s32[2,4]{1,0:T(2,128)S(1)} %pad_add_fusion.bounds, bf16[4,2048,512]{2,1,0:T(8,128)(2,1)} %get-tuple-element.41.probs, bf16[16,80,128]{2,1,0:T(8,128)(2,1)S(1)} %all-to-all-done.3.ctx_t, ...), custom_call_target="tpu_custom_call" | custom-call | flops 2684354560 | bytes 8388608 | tf_op jit(solution)/shard_map/attention_grads/pallas_call | solution.py:308
  178.9 11.2 %all-gather.2 = f32[16,3,1280]{2,0,1:T(8,128)S(1)} all-gather(f32[8,3,1280]{2,0,1:T(8,128)S(1)} %copy.43), channel_id=4, replica_groups=mesh['far'=2,'y'=4,'x'=4,'z'=8,'core'=2] {'core'}, dimensions={0}, use_global_device_ids=true | all-gather | bytes 368640 | tf_op jit(solution)/shard_map/all_gather | solution.py:426
  (100 shorter events, 25.4 us)
Async XLA Ops:
  7.2 19.3 %copy-start.13 = (s32[1,8]{1,0:T(1,128)S(1)}, s32[1,8]{1,0:T(1,128)}, u32[]{:S(2)}) copy-start(s32[1,8]{1,0:T(1,128)} %param.18) | copy-start | bytes 100
  7.2 104.7 %all-gather.7.cloned.1.call-start = ((), (), s32[]{:S(2)}) async-start(), calls=%async_computation.5 | async-start | bytes 6758400 | tf_op jit(solution)/shard_map/all_gather | solution.py:358
  10.7 19.6 %all-to-all-start = ((bf16[8,40,640]{2,1,0:T(8,128)(2,1)}), bf16[8,40,640]{2,1,0:T(8,128)(2,1)S(1)}, u32[]{:S(2)}, u32[]{:S(2)}) async-start(bf16[8,40,640]{2,1,0:T(8,128)(2,1)} %broadcast_in_dim.57), calls=%async_computation | async-start | bytes 819200 | tf_op jit(solution)/shard_map/all_to_all | solution.py:44
  18.3 20.2 %copy-start.8 = (bf16[128,1280]{1,0:T(8,128)(2,1)S(1)}, bf16[128,1280]{1,0:T(8,128)(2,1)}, u32[]{:S(2)}) copy-start(bf16[128,1280]{1,0:T(8,128)(2,1)} %param.12) | copy-start | bytes 983044
  18.3 24.8 %copy-start.2 = (bf16[2048,80]{0,1:T(8,128)(2,1)S(1)}, bf16[2048,80]{0,1:T(8,128)(2,1)}, u32[]{:S(2)}) copy-start(bf16[2048,80]{0,1:T(8,128)(2,1)} %param.16) | copy-start | bytes 983044
  19.7 23.7 %collective-permute-start = (bf16[16,1280]{1,0:T(8,128)(2,1)S(1)}, bf16[16,1280]{1,0:T(8,128)(2,1)S(1)}, u32[]{:S(2)}, u32[]{:S(2)}) collective-permute-start(bf16[16,1280]{1,0:T(8,128)(2,1)S(1)} %get-tuple-element.61), channel_id=1, source_target_pairs={{0,1},{1,2},{2,3},{3,4},{4,5},{5,6},{6,7},{7,8},{8,9},{9,10},{10,1... | collective-permute-start | bytes 122888 | tf_op jit(solution)/shard_map/ppermute | solution.py:36
  24.5 18.9 %collective-permute-start.1 = (bf16[16,1280]{1,0:T(8,128)(2,1)S(1)}, bf16[16,1280]{1,0:T(8,128)(2,1)S(1)}, u32[]{:S(2)}, u32[]{:S(2)}) collective-permute-start(bf16[16,1280]{1,0:T(8,128)(2,1)S(1)} %get-tuple-element.62), channel_id=1, source_target_pairs={{1,0},{2,1},{3,2},{4,3},{5,4},{6,5},{7,6},{8,7},{9,8},{10,9},{11,1... | collective-permute-start | bytes 122888 | tf_op jit(solution)/shard_map/ppermute | solution.py:37
  30.3 13.3 %copy-start.3 = (f32[31,1280]{1,0:T(8,128)S(1)}, f32[31,1280]{1,0:T(8,128)}, u32[]{:S(2)}) copy-start(f32[31,1280]{1,0:T(8,128)} %taps.3) | copy-start | bytes 476164
  31.6 14.9 %copy-start.4 = (bf16[2048,80]{0,1:T(8,128)(2,1)S(1)}, bf16[2048,80]{0,1:T(8,128)(2,1)}, u32[]{:S(2)}) copy-start(bf16[2048,80]{0,1:T(8,128)(2,1)} %param.15) | copy-start | bytes 983044
  31.6 28.2 %all-to-all-start.1 = ((bf16[4,8,40,640]{3,2,1,0:T(8,128)(2,1)}), bf16[4,8,40,640]{3,2,1,0:T(8,128)(2,1)}, u32[]{:S(2)}, u32[]{:S(2)}) async-start(bf16[4,8,40,640]{3,2,1,0:T(8,128)(2,1)} %broadcast_in_dim.92), calls=%async_computation.1 | async-start | bytes 3276800 | tf_op jit(solution)/shard_map/all_to_all | solution.py:44
  39.2 22.1 %collective-permute-start.2 = (bf16[128,640]{1,0:T(8,128)(2,1)}, bf16[128,640]{1,0:T(8,128)(2,1)S(1)}, u32[]{:S(2)}, u32[]{:S(2)}) collective-permute-start(bf16[128,640]{1,0:T(8,128)(2,1)} %constant_dynamic-slice_fusion.6), channel_id=1, source_target_pairs={{0,1},{1,0},{2,3},{3,2},{4,5},{5,4},{6,7},{7,6},{8,9},{9,8},{10,11... | collective-permute-start | bytes 491528 | tf_op jit(solution)/shard_map/ppermute | solution.py:59
  61.4 16.7 %copy-start.1 = (bf16[128,2560]{1,0:T(8,128)(2,1)S(1)}, bf16[128,2560]{1,0:T(8,128)(2,1)}, u32[]{:S(2)}) copy-start(bf16[128,2560]{1,0:T(8,128)(2,1)} %gate_ref.1) | copy-start | bytes 1966084
  62.0 5.6 %collective-permute-start.3 = (bf16[128,1280]{1,0:T(8,128)(2,1)S(1)}, bf16[128,1280]{1,0:T(8,128)(2,1)S(1)}, u32[]{:S(2)}, u32[]{:S(2)}) collective-permute-start(bf16[128,1280]{1,0:T(8,128)(2,1)S(1)} %convolution_convert_fusion), channel_id=1, source_target_pairs={{0,1},{1,0},{2,3},{3,2},{4,5},{5,4},{6,7},{7,6},{8,9},{9,8},{10,11... | collective-permute-start | bytes 983048 | tf_op jit(solution)/shard_map/ppermute | solution.py:59
  67.7 29.6 %copy-start.7 = (bf16[128,1280]{1,0:T(8,128)(2,1)S(1)}, bf16[128,1280]{1,0:T(8,128)(2,1)}, u32[]{:S(2)}) copy-start(bf16[128,1280]{1,0:T(8,128)(2,1)} %param.13) | copy-start | bytes 983044
  67.7 6.6 %collective-permute-start.4 = (bf16[16,1280]{1,0:T(8,128)(2,1)S(1)}, bf16[16,1280]{1,0:T(8,128)(2,1)S(1)}, u32[]{:S(2)}, u32[]{:S(2)}) collective-permute-start(bf16[16,1280]{1,0:T(8,128)(2,1)S(1)} %get-tuple-element.59), channel_id=1, source_target_pairs={{0,1},{1,2},{2,3},{3,4},{4,5},{5,6},{6,7},{7,8},{8,9},{9,10},{10,1... | collective-permute-start | bytes 122888 | tf_op jit(solution)/shard_map/ppermute | solution.py:36
  72.3 5.7 %collective-permute-start.5 = (bf16[16,1280]{1,0:T(8,128)(2,1)S(1)}, bf16[16,1280]{1,0:T(8,128)(2,1)S(1)}, u32[]{:S(2)}, u32[]{:S(2)}) collective-permute-start(bf16[16,1280]{1,0:T(8,128)(2,1)S(1)} %get-tuple-element.60), channel_id=1, source_target_pairs={{1,0},{2,1},{3,2},{4,3},{5,4},{6,5},{7,6},{8,7},{9,8},{10,9},{11,1... | collective-permute-start | bytes 122888 | tf_op jit(solution)/shard_map/ppermute | solution.py:37
  85.4 19.3 %all-to-all-start.2 = ((f32[16,2,1280]{2,1,0:T(2,128)}), f32[16,2,1280]{2,1,0:T(2,128)S(1)}, u32[]{:S(2)}, u32[]{:S(2)}) async-start(f32[16,2,1280]{2,1,0:T(2,128)} %bitcast.9), calls=%async_computation.2 | async-start | bytes 327680 | tf_op jit(solution)/shard_map/all_to_all | solution.py:391
  95.2 24.2 %copy-start.12 = (f32[1280]{0:T(1024)S(1)}, f32[1280]{0:T(1024)}, u32[]{:S(2)}) copy-start(f32[1280]{0:T(1024)} %param.19) | copy-start | bytes 15364
  95.2 16.7 %collective-permute-start.6 = (bf16[128,1280]{1,0:T(8,128)(2,1)S(1)}, bf16[128,1280]{1,0:T(8,128)(2,1)S(1)}, u32[]{:S(2)}, u32[]{:S(2)}) collective-permute-start(bf16[128,1280]{1,0:T(8,128)(2,1)S(1)} %pad_maximum_fusion.2), channel_id=1, source_target_pairs={{0,1},{1,0},{2,3},{3,2},{4,5},{5,4},{6,7},{7,6},{8,9},{9,8},{10,11... | collective-permute-start | bytes 983048 | tf_op jit(solution)/shard_map/ppermute | solution.py:59
  111.9 11.2 %slice-start = ((s8[6553600]{0:T(1024)(128)(4,1)}), s8[4194304]{0:T(1024)(128)(4,1)S(1)}, s32[]{:S(2)}) async-start(s8[6553600]{0:T(1024)(128)(4,1)} %bitcast.39), calls=%async_computation.6 | async-start | bytes 8388608
  115.2 4.1 %collective-permute-start.7 = (bf16[128,1280]{1,0:T(8,128)(2,1)S(1)}, bf16[128,1280]{1,0:T(8,128)(2,1)S(1)}, u32[]{:S(2)}, u32[]{:S(2)}) collective-permute-start(bf16[128,1280]{1,0:T(8,128)(2,1)S(1)} %fusion.6), channel_id=1, source_target_pairs={{0,1},{1,0},{2,3},{3,2},{4,5},{5,4},{6,7},{7,6},{8,9},{9,8},{10,11... | collective-permute-start | bytes 983048 | tf_op jit(solution)/shard_map/ppermute | solution.py:59
  123.2 9.8 %copy-start.6 = (bf16[2048,80]{0,1:T(8,128)(2,1)S(1)}, bf16[2048,80]{0,1:T(8,128)(2,1)}, u32[]{:S(2)}) copy-start(bf16[2048,80]{0,1:T(8,128)(2,1)} %param.17) | copy-start | bytes 983044
  125.0 36.2 %all-to-all-start.3 = ((bf16[16,80,128]{2,1,0:T(8,128)(2,1)}), bf16[16,80,128]{2,1,0:T(8,128)(2,1)S(1)}, u32[]{:S(2)}, u32[]{:S(2)}) async-start(bf16[16,80,128]{2,1,0:T(8,128)(2,1)} %bitcast.10), calls=%async_computation.3 | async-start | bytes 655360 | tf_op jit(solution)/shard_map/all_to_all | solution.py:416
  161.9 16.9 %all-to-all-start.4 = ((f32[8,3,1280]{2,1,0:T(4,128)}), f32[8,3,1280]{2,1,0:T(4,128)S(1)}, u32[]{:S(2)}, u32[]{:S(2)}) async-start(f32[8,3,1280]{2,1,0:T(4,128)} %broadcast_in_dim.96), calls=%async_computation.4 | async-start | bytes 327680 | tf_op jit(solution)/shard_map/all_to_all | solution.py:44
  (6 other events, 21.9 us)
Sparse Core Ops, SparseCore 0:
  11.8 100.1 all-gather.6

commit v6 on v5

--- a/solution.py
+++ b/solution.py
@@ -15,7 +15,7 @@
 HALO = 16
 LANES = 128
 TIME = ("z", "core")
-GROUPS = ("far", "y", "x")
+GROUPS = ("y", "x")
 
 
 def frame_ends(frame_lens):
@@ -42,6 +42,16 @@
     count = lax.axis_size(axis)
     copies = jnp.broadcast_to(piece[None], (count,) + piece.shape)
     return lax.all_to_all(copies, axis, split_axis=0, concat_axis=0)
+
+
+def total_over(array, axis):
+    count = lax.axis_size(axis)
+    terms = [array]
+    for bits in range(1, count):
+        terms.append(lax.ppermute(array, axis, [(i, i ^ bits) for i in range(count)]))
+    while len(terms) > 1:
+        terms = [terms[i] + terms[i + 1] for i in range(0, len(terms), 2)]
+    return terms[0]
 
 
 def row_product(active, piece):
@@ -366,7 +376,7 @@
     bounds = jnp.stack([lo[0, ::QBLK] // BLK, (hi[0, QBLK - 1 :: QBLK] + BLK - 1) // BLK])
 
     conv_half, _ = halves(w_conv_out, core)
-    by_y = spread(conv_half, ("far", "y"))
+    by_y = spread(conv_half, "y")
     ext_pos = lax.axis_index(TIME) * t_dev + jnp.arange(-HALO, t_dev + HALO, dtype=jnp.int32)
     seg_ext = jnp.broadcast_to(segments_of(ends, ext_pos)[:, None], (t_dev + 2 * HALO, LANES))
     gate_sig = jax.nn.sigmoid(pre_glu[:, width:].astype(jnp.float32))
@@ -415,8 +425,8 @@
     ctx_t, gain = lax.optimization_barrier((ctx_t, gain))
     ctx_t = lax.all_to_all(ctx_t, TIME, split_axis=0, concat_axis=0)
     sums = jnp.concatenate([rows, gain], axis=0)
-    for axis in (("far", "y"), "x"):
-        sums = jnp.sum(lax.all_gather(sums, axis), axis=0)
+    for axis in ("x", "y"):
+        sums = total_over(sums, axis)
     ctx_t, sums = lax.optimization_barrier((ctx_t, sums))
     probs = pltpu.with_memory_space_constraint(probs, pltpu.HBM)
     stacked = spread(sums, "z")
@@ -431,7 +441,7 @@
 
 def solution(mesh):
     dp, seq = mesh.devices.shape
-    shape = (2, dp // 8, 4, seq // 2, 2)
+    shape = (dp // 4, 4, seq // 2, 2)
     fine = Mesh(mesh.devices.reshape(shape), GROUPS + TIME)
     frames = P(GROUPS + TIME, None)
     heads = P(GROUPS, TIME)

time: 200 us -> 203 us (1.015)
  starting transfers between devices: 64.4 us -> 100 us
  blocking collectives: 39.1 us -> 5.4 us
  waiting for transfers between devices: 26.1 us -> 30.2 us
  Pallas kernels: 29.7 us -> 26.2 us
    ppermute x0 -> x10, starting transfers between devices: none -> 34.6 us  [total_over(): lax.ppermute(array, axis, [(i, i ^ bits) for i in range(count)])]
    all_gather x2 -> x0, blocking collectives: 27.8 us -> none  [local(): sums = jnp.sum(lax.all_gather(sums, axis), axis=0)]
    all_gather x1, blocking collectives: 11.2 us -> 5.4 us  [local(): stacked = lax.all_gather(stacked, 'core', axis=0)]
    ppermute x0 -> x10, waiting for transfers between devices: none -> 2.08 us  [total_over(): lax.ppermute(array, axis, [(i, i ^ bits) for i in range(count)])]
    pallas_call x1, Pallas kernels: 9.64 us -> 7.59 us  [attention_probs(): pl.pallas_call(probs_kernel, grid_spec=pltpu.PrefetchScalarGridSpec(num_s...]
  transfers between devices with their start and end apart: 14 -> 24, of which waited for: 7 -> 8; matrix products, arithmetic and copies ran while one was open for 5% -> 5% of each run, Pallas kernels for 15% -> 13%
where the time goes in v6:
time: 203 us; the launch traced here: 201 us
  starting transfers between devices  100 us (49%)
  waiting for transfers between devices  30.2 us (15%)
  Pallas kernels  26.2 us (13%)
  between operations  14.7 us (7%)
  local copies, waits for them, and re-layouts  10 us (5%)
  matrix products  9.6 us (5%)
  blocking collectives  5.4 us (3%)
  other arithmetic  4.93 us (2%)
    ppermute x10, starting transfers between devices, total_over(): lax.ppermute(array, axis, [(i, i ^ bits) for i in range(count)])  34.6 us
    all_to_all x3, starting transfers between devices, spread(): return lax.all_to_all(copies, axis, split_axis=0, concat_axis=0)  21.1 us
    ppermute x4, starting transfers between devices, swap(): return lax.ppermute(array, 'core', [(0, 1), (1, 0)])  12.8 us
    all_to_all x1, starting transfers between devices, local(): lax.all_to_all(rows, TIME, split_axis=0, concat_axis=0)  9.66 us
    ppermute x2, starting transfers between devices, padded(): low = lax.ppermute(block[block.shape[0] - width:], TIME, forward)  9.49 us
    pallas_call x1, Pallas kernels, attention_grads(): pl.pallas_call(grads_kernel, grid_spec=pltpu.PrefetchScalarGridSpec(num_s...  9.12 us
    all_to_all x1, starting transfers between devices, local(): ctx_t = lax.all_to_all(ctx_t, TIME, split_axis=0, concat_axis=0)  8.61 us
    all_to_all x3, waiting for transfers between devices, spread(): return lax.all_to_all(copies, axis, split_axis=0, concat_axis=0)  8.23 us
  transfers between devices with their start and end apart: 24, of which 8 were waited for; matrix products, arithmetic and copies ran while one was open for 5% of the time, Pallas kernels for 13%

profile of v6, /device:TPU:1, one launch (start us, length us, event | category | flops | bytes accessed | tf_op | source)
XLA Modules:
  0.0 201.2 jit_solution(12357853805953700730)
XLA Ops:
  10.7 7.7 %all-to-all-start = ((bf16[8,40,640]{2,1,0:T(8,128)(2,1)}), bf16[8,40,640]{2,1,0:T(8,128)(2,1)S(1)}, u32[]{:S(2)}, u32[]{:S(2)}) async-start(bf16[8,40,640]{2,1,0:T(8,128)(2,1)} %broadcast_in_dim.57), calls=%async_computation | async-start | bytes 819200 | tf_op jit(solution)/shard_map/all_to_all | solution.py:44
  19.7 4.8 %collective-permute-start = (bf16[16,1280]{1,0:T(8,128)(2,1)S(1)}, bf16[16,1280]{1,0:T(8,128)(2,1)S(1)}, u32[]{:S(2)}, u32[]{:S(2)}) collective-permute-start(bf16[16,1280]{1,0:T(8,128)(2,1)S(1)} %get-tuple-element.61), channel_id=1, source_target_pairs={{0,1},{1,2},{2,3},{3,4},{4,5},{5,6},{6,7},{7,8},{8,9},{9,10},{10,1... | collective-permute-start | bytes 122888 | tf_op jit(solution)/shard_map/ppermute | solution.py:36
  26.7 3.6 %all-to-all-done = bf16[8,40,640]{2,1,0:T(8,128)(2,1)S(1)} async-done(((bf16[8,40,640]{2,1,0:T(8,128)(2,1)}), bf16[8,40,640]{2,1,0:T(8,128)(2,1)S(1)}, u32[]{:S(2)}, u32[]{:S(2)}) %all-to-all-start) | async-done | bytes 409632 | tf_op jit(solution)/shard_map/all_to_all | solution.py:44
  31.6 6.9 %all-to-all-start.1 = ((bf16[4,8,40,640]{3,2,1,0:T(8,128)(2,1)}), bf16[4,8,40,640]{3,2,1,0:T(8,128)(2,1)}, u32[]{:S(2)}, u32[]{:S(2)}) async-start(bf16[4,8,40,640]{3,2,1,0:T(8,128)(2,1)} %broadcast_in_dim.92), calls=%async_computation.1 | async-start | bytes 3276800 | tf_op jit(solution)/shard_map/all_to_all | solution.py:44
  39.2 3.5 %collective-permute-start.2 = (bf16[128,640]{1,0:T(8,128)(2,1)}, bf16[128,640]{1,0:T(8,128)(2,1)S(1)}, u32[]{:S(2)}, u32[]{:S(2)}) collective-permute-start(bf16[128,640]{1,0:T(8,128)(2,1)} %constant_dynamic-slice_fusion.6), channel_id=1, source_target_pairs={{0,1},{1,0},{2,3},{3,2},{4,5},{5,4},{6,7},{7,6},{8,9},{9,8},{10,11... | collective-permute-start | bytes 491528 | tf_op jit(solution)/shard_map/ppermute | solution.py:69
  47.5 7.6 %attention_probs.1 = (bf16[4,2048,512]{2,1,0:T(8,128)(2,1)}, f32[80,2048]{1,0:T(8,128)S(1)}, f32[1,2048]{1,0:T(1,128)S(1)}) custom-call(s32[2,4]{1,0:T(2,128)S(1)} %pad_add_fusion.bounds, bf16[80,2048]{1,0:T(8,128)(2,1)S(1)} %bitcast.24, bf16[2048,80]{1,0:T(8,128)(2,1)S(1)} %copy.38.k, bf16[80,2048]{1,0:T(8,128)(2,1)S(1)} %bitcast.25, ...), custom_call_target="tpu_custom_call" | custom-call | flops 1342177280 | bytes 8388608 | tf_op jit(solution)/shard_map/attention_probs/pallas_call | solution.py:243
  55.1 4.7 %all-to-all-done.1 = bf16[4,8,40,640]{3,2,1,0:T(8,128)(2,1)} async-done(((bf16[4,8,40,640]{3,2,1,0:T(8,128)(2,1)}), bf16[4,8,40,640]{3,2,1,0:T(8,128)(2,1)}, u32[]{:S(2)}, u32[]{:S(2)}) %all-to-all-start.1) | async-done | bytes 1638432 | tf_op jit(solution)/shard_map/all_to_all | solution.py:44
  62.0 4.3 %collective-permute-start.3 = (bf16[128,1280]{1,0:T(8,128)(2,1)S(1)}, bf16[128,1280]{1,0:T(8,128)(2,1)S(1)}, u32[]{:S(2)}, u32[]{:S(2)}) collective-permute-start(bf16[128,1280]{1,0:T(8,128)(2,1)S(1)} %convolution_convert_fusion), channel_id=1, source_target_pairs={{0,1},{1,0},{2,3},{3,2},{4,5},{5,4},{6,7},{7,6},{8,9},{9,8},{10,11... | collective-permute-start | bytes 983048 | tf_op jit(solution)/shard_map/ppermute | solution.py:69
  67.7 4.6 %collective-permute-start.4 = (bf16[16,1280]{1,0:T(8,128)(2,1)S(1)}, bf16[16,1280]{1,0:T(8,128)(2,1)S(1)}, u32[]{:S(2)}, u32[]{:S(2)}) collective-permute-start(bf16[16,1280]{1,0:T(8,128)(2,1)S(1)} %get-tuple-element.59), channel_id=1, source_target_pairs={{0,1},{1,2},{2,3},{3,4},{4,5},{5,6},{6,7},{7,8},{8,9},{9,10},{10,1... | collective-permute-start | bytes 122888 | tf_op jit(solution)/shard_map/ppermute | solution.py:36
  74.3 3.8 %collective-permute-done.5 = bf16[16,1280]{1,0:T(8,128)(2,1)S(1)} collective-permute-done((bf16[16,1280]{1,0:T(8,128)(2,1)S(1)}, bf16[16,1280]{1,0:T(8,128)(2,1)S(1)}, u32[]{:S(2)}, u32[]{:S(2)}) %collective-permute-start.5) | collective-permute-done | bytes 40992 | tf_op jit(solution)/shard_map/ppermute | solution.py:37
  78.1 6.5 %conv_grads.1 = (bf16[128,1280]{1,0:T(8,128)(2,1)S(1)}, bf16[128,1280]{1,0:T(8,128)(2,1)S(1)}, f32[32,1280]{1,0:T(8,128)S(1)}) custom-call(s32[160,128]{1,0:T(8,128)S(1)} %broadcast_in_dim.56.seg, bf16[160,1280]{1,0:T(8,128)(2,1)S(1)} %pad_maximum_fusion.1.grad, bf16[160,1280]{1,0:T(8,128)(2,1)S(1)} %pad_maximum_fusion.glu, bf16[128,2560]{1,0:T(8,128)(2,1)S(1)} %copy-done.1, ...), custom_call_target="tpu_custom_call" | custom-call | flops 40632320 | bytes 2621440 | tf_op jit(solution)/shard_map/conv_grads/pallas_call | solution.py:155
  85.4 9.7 %all-to-all-start.2 = ((f32[16,2,1280]{2,1,0:T(2,128)}), f32[16,2,1280]{2,1,0:T(2,128)S(1)}, u32[]{:S(2)}, u32[]{:S(2)}) async-start(f32[16,2,1280]{2,1,0:T(2,128)} %bitcast.9), calls=%async_computation.2 | async-start | bytes 327680 | tf_op jit(solution)/shard_map/all_to_all | solution.py:401
  97.4 7.4 %all-to-all-done.2 = f32[16,2,1280]{2,1,0:T(2,128)S(1)} async-done(((f32[16,2,1280]{2,1,0:T(2,128)}), f32[16,2,1280]{2,1,0:T(2,128)S(1)}, u32[]{:S(2)}, u32[]{:S(2)}) %all-to-all-start.2) | async-done | bytes 163872 | tf_op jit(solution)/shard_map/all_to_all | solution.py:401
  104.8 7.1 %all-gather.3.cloned.1.call-done = bf16[1280,2560]{1,0:T(8,128)(2,1)} async-done(((bf16[40,2560]{1,0:T(8,128)(2,1)}), bf16[1280,2560]{1,0:T(8,128)(2,1)}) %all-gather.3.cloned.1.call-update) | async-done | bytes 6553616 | tf_op jit(solution)/shard_map/all_gather | solution.py:368
  111.9 3.3 %fusion.6 = bf16[128,1280]{1,0:T(8,128)(2,1)S(1)} fusion(bf16[128,1280]{1,0:T(8,128)(2,1)S(1)} %collective-permute-done.6, bf16[1280,2560]{1,0:T(8,128)(2,1)} %all-gather.3.cloned.1.call-done), kind=kOutput, calls=%fused_computation.6 | convolution fusion | flops 419594240 | bytes 3932160 | tf_op jit(solution)/shard_map/tc,rc->tr/dot_general | solution.py:58
  119.3 3.4 %fusion.22 = (f32[1280]{0:T(1024)S(1)}, f32[128]{0:T(128)S(1)}, f32[128]{0:T(128)S(1)}, f32[128,1280]{1,0:T(8,128)S(1)}) fusion(bf16[128,1280]{1,0:T(8,128)(2,1)S(1)} %copy-done.7, f32[128]{0:T(128)S(1)} %add_rsqrt_fusion, f32[128]{0:T(128)S(1)} %broadcast_multiply_fusion.2, f32[1280]{0:T(1024)S(1)} %copy-done.12, ...), kind=kOutput, calls=%fused_computation.21 | convolution fusion | flops 421886464 | bytes 4927488 | tf_op jit(solution)/shard_map/tc,rc->tr/dot_general | solution.py:58
  129.6 4.9 %collective-permute-start.9 = (f32[3,1280]{1,0:T(4,128)S(1)}, f32[3,1280]{1,0:T(4,128)S(1)}, u32[]{:S(2)}, u32[]{:S(2)}) collective-permute-start(f32[3,1280]{1,0:T(4,128)S(1)} %pad_maximum_fusion.4), channel_id=1, source_target_pairs={{0,32},{16,48},{32,0},{48,16},{1,33},{17,49},{33,1},{49,17},{2,34}... | collective-permute-start | bytes 46088 | tf_op jit(solution)/shard_map/ppermute | solution.py:51
  134.6 8.6 %all-to-all-start.3 = ((bf16[16,80,128]{2,1,0:T(8,128)(2,1)}), bf16[16,80,128]{2,1,0:T(8,128)(2,1)S(1)}, u32[]{:S(2)}, u32[]{:S(2)}) async-start(bf16[16,80,128]{2,1,0:T(8,128)(2,1)} %bitcast.10), calls=%async_computation.3 | async-start | bytes 655360 | tf_op jit(solution)/shard_map/all_to_all | solution.py:426
  146.2 3.7 %collective-permute-start.12 = (f32[3,1280]{1,0:T(4,128)S(1)}, f32[3,1280]{1,0:T(4,128)S(1)}, u32[]{:S(2)}, u32[]{:S(2)}) collective-permute-start(f32[3,1280]{1,0:T(4,128)S(1)} %add_add_fusion.1), channel_id=1, source_target_pairs={{0,128},{64,192},{128,0},{192,64},{256,384},{320,448},{384,256},{4... | collective-permute-start | bytes 46088 | tf_op jit(solution)/shard_map/ppermute | solution.py:51
  152.5 5.0 %collective-permute-start.14 = (f32[3,1280]{1,0:T(4,128)S(1)}, f32[3,1280]{1,0:T(4,128)S(1)}, u32[]{:S(2)}, u32[]{:S(2)}) collective-permute-start(f32[3,1280]{1,0:T(4,128)S(1)} %add_add_fusion.1), channel_id=1, source_target_pairs={{0,256},{64,320},{128,384},{192,448},{256,0},{320,64},{384,128},{4... | collective-permute-start | bytes 46088 | tf_op jit(solution)/shard_map/ppermute | solution.py:51
  160.7 4.4 %collective-permute-start.16 = (f32[3,1280]{1,0:T(4,128)S(1)}, f32[3,1280]{1,0:T(4,128)S(1)}, u32[]{:S(2)}, u32[]{:S(2)}) collective-permute-start(f32[3,1280]{1,0:T(4,128)S(1)} %add_add_fusion.1), channel_id=1, source_target_pairs={{0,384},{64,448},{128,256},{192,320},{256,128},{320,192},{384,0},{... | collective-permute-start | bytes 46088 | tf_op jit(solution)/shard_map/ppermute | solution.py:51
  171.7 6.5 %all-to-all-start.4 = ((f32[8,3,1280]{2,1,0:T(4,128)}), f32[8,3,1280]{2,1,0:T(4,128)S(1)}, u32[]{:S(2)}, u32[]{:S(2)}) async-start(f32[8,3,1280]{2,1,0:T(4,128)} %broadcast_in_dim.96), calls=%async_computation.4 | async-start | bytes 327680 | tf_op jit(solution)/shard_map/all_to_all | solution.py:44
  178.2 9.1 %attention_grads.1 = (bf16[80,2048]{1,0:T(8,128)(2,1)}, bf16[80,2048]{1,0:T(8,128)(2,1)}, bf16[80,2048]{1,0:T(8,128)(2,1)}) custom-call(s32[2,4]{1,0:T(2,128)S(1)} %pad_add_fusion.bounds, bf16[4,2048,512]{2,1,0:T(8,128)(2,1)} %get-tuple-element.41.probs, bf16[16,80,128]{2,1,0:T(8,128)(2,1)S(1)} %all-to-all-done.3.ctx_t, ...), custom_call_target="tpu_custom_call" | custom-call | flops 2684354560 | bytes 8388608 | tf_op jit(solution)/shard_map/attention_grads/pallas_call | solution.py:318
  187.4 5.4 %all-gather = f32[16,3,1280]{2,0,1:T(8,128)S(1)} all-gather(f32[8,3,1280]{2,0,1:T(8,128)S(1)} %copy.43), channel_id=2, replica_groups=mesh['y'=8,'x'=4,'z'=8,'core'=2] {'core'}, dimensions={0}, use_global_device_ids=true | all-gather | bytes 368640 | tf_op jit(solution)/shard_map/all_gather | solution.py:436
  (118 shorter events, 49.9 us)
Async XLA Ops:
  7.2 104.7 %all-gather.3.cloned.1.call-start = ((), (), s32[]{:S(2)}) async-start(), calls=%async_computation.5 | async-start | bytes 6758400 | tf_op jit(solution)/shard_map/all_gather | solution.py:368
  10.7 19.6 %all-to-all-start = ((bf16[8,40,640]{2,1,0:T(8,128)(2,1)}), bf16[8,40,640]{2,1,0:T(8,128)(2,1)S(1)}, u32[]{:S(2)}, u32[]{:S(2)}) async-start(bf16[8,40,640]{2,1,0:T(8,128)(2,1)} %broadcast_in_dim.57), calls=%async_computation | async-start | bytes 819200 | tf_op jit(solution)/shard_map/all_to_all | solution.py:44
  19.7 23.7 %collective-permute-start = (bf16[16,1280]{1,0:T(8,128)(2,1)S(1)}, bf16[16,1280]{1,0:T(8,128)(2,1)S(1)}, u32[]{:S(2)}, u32[]{:S(2)}) collective-permute-start(bf16[16,1280]{1,0:T(8,128)(2,1)S(1)} %get-tuple-element.61), channel_id=1, source_target_pairs={{0,1},{1,2},{2,3},{3,4},{4,5},{5,6},{6,7},{7,8},{8,9},{9,10},{10,1... | collective-permute-start | bytes 122888 | tf_op jit(solution)/shard_map/ppermute | solution.py:36
  24.5 18.9 %collective-permute-start.1 = (bf16[16,1280]{1,0:T(8,128)(2,1)S(1)}, bf16[16,1280]{1,0:T(8,128)(2,1)S(1)}, u32[]{:S(2)}, u32[]{:S(2)}) collective-permute-start(bf16[16,1280]{1,0:T(8,128)(2,1)S(1)} %get-tuple-element.62), channel_id=1, source_target_pairs={{1,0},{2,1},{3,2},{4,3},{5,4},{6,5},{7,6},{8,7},{9,8},{10,9},{11,1... | collective-permute-start | bytes 122888 | tf_op jit(solution)/shard_map/ppermute | solution.py:37
  31.6 28.1 %all-to-all-start.1 = ((bf16[4,8,40,640]{3,2,1,0:T(8,128)(2,1)}), bf16[4,8,40,640]{3,2,1,0:T(8,128)(2,1)}, u32[]{:S(2)}, u32[]{:S(2)}) async-start(bf16[4,8,40,640]{3,2,1,0:T(8,128)(2,1)} %broadcast_in_dim.92), calls=%async_computation.1 | async-start | bytes 3276800 | tf_op jit(solution)/shard_map/all_to_all | solution.py:44
  39.2 22.1 %collective-permute-start.2 = (bf16[128,640]{1,0:T(8,128)(2,1)}, bf16[128,640]{1,0:T(8,128)(2,1)S(1)}, u32[]{:S(2)}, u32[]{:S(2)}) collective-permute-start(bf16[128,640]{1,0:T(8,128)(2,1)} %constant_dynamic-slice_fusion.6), channel_id=1, source_target_pairs={{0,1},{1,0},{2,3},{3,2},{4,5},{5,4},{6,7},{7,6},{8,9},{9,8},{10,11... | collective-permute-start | bytes 491528 | tf_op jit(solution)/shard_map/ppermute | solution.py:69
  62.0 5.6 %collective-permute-start.3 = (bf16[128,1280]{1,0:T(8,128)(2,1)S(1)}, bf16[128,1280]{1,0:T(8,128)(2,1)S(1)}, u32[]{:S(2)}, u32[]{:S(2)}) collective-permute-start(bf16[128,1280]{1,0:T(8,128)(2,1)S(1)} %convolution_convert_fusion), channel_id=1, source_target_pairs={{0,1},{1,0},{2,3},{3,2},{4,5},{5,4},{6,7},{7,6},{8,9},{9,8},{10,11... | collective-permute-start | bytes 983048 | tf_op jit(solution)/shard_map/ppermute | solution.py:69
  67.7 6.6 %collective-permute-start.4 = (bf16[16,1280]{1,0:T(8,128)(2,1)S(1)}, bf16[16,1280]{1,0:T(8,128)(2,1)S(1)}, u32[]{:S(2)}, u32[]{:S(2)}) collective-permute-start(bf16[16,1280]{1,0:T(8,128)(2,1)S(1)} %get-tuple-element.59), channel_id=1, source_target_pairs={{0,1},{1,2},{2,3},{3,4},{4,5},{5,6},{6,7},{7,8},{8,9},{9,10},{10,1... | collective-permute-start | bytes 122888 | tf_op jit(solution)/shard_map/ppermute | solution.py:36
  72.4 5.7 %collective-permute-start.5 = (bf16[16,1280]{1,0:T(8,128)(2,1)S(1)}, bf16[16,1280]{1,0:T(8,128)(2,1)S(1)}, u32[]{:S(2)}, u32[]{:S(2)}) collective-permute-start(bf16[16,1280]{1,0:T(8,128)(2,1)S(1)} %get-tuple-element.60), channel_id=1, source_target_pairs={{1,0},{2,1},{3,2},{4,3},{5,4},{6,5},{7,6},{8,7},{9,8},{10,9},{11,1... | collective-permute-start | bytes 122888 | tf_op jit(solution)/shard_map/ppermute | solution.py:37
  85.4 19.3 %all-to-all-start.2 = ((f32[16,2,1280]{2,1,0:T(2,128)}), f32[16,2,1280]{2,1,0:T(2,128)S(1)}, u32[]{:S(2)}, u32[]{:S(2)}) async-start(f32[16,2,1280]{2,1,0:T(2,128)} %bitcast.9), calls=%async_computation.2 | async-start | bytes 327680 | tf_op jit(solution)/shard_map/all_to_all | solution.py:401
  95.3 16.7 %collective-permute-start.6 = (bf16[128,1280]{1,0:T(8,128)(2,1)S(1)}, bf16[128,1280]{1,0:T(8,128)(2,1)S(1)}, u32[]{:S(2)}, u32[]{:S(2)}) collective-permute-start(bf16[128,1280]{1,0:T(8,128)(2,1)S(1)} %pad_maximum_fusion.2), channel_id=1, source_target_pairs={{0,1},{1,0},{2,3},{3,2},{4,5},{5,4},{6,7},{7,6},{8,9},{9,8},{10,11... | collective-permute-start | bytes 983048 | tf_op jit(solution)/shard_map/ppermute | solution.py:69
  115.2 4.1 %collective-permute-start.7 = (bf16[128,1280]{1,0:T(8,128)(2,1)S(1)}, bf16[128,1280]{1,0:T(8,128)(2,1)S(1)}, u32[]{:S(2)}, u32[]{:S(2)}) collective-permute-start(bf16[128,1280]{1,0:T(8,128)(2,1)S(1)} %fusion.6), channel_id=1, source_target_pairs={{0,1},{1,0},{2,3},{3,2},{4,5},{5,4},{6,7},{7,6},{8,9},{9,8},{10,11... | collective-permute-start | bytes 983048 | tf_op jit(solution)/shard_map/ppermute | solution.py:69
  125.0 18.2 %collective-permute-start.10 = (f32[3,1280]{1,0:T(4,128)S(1)}, f32[3,1280]{1,0:T(4,128)S(1)}, u32[]{:S(2)}, u32[]{:S(2)}) collective-permute-start(f32[3,1280]{1,0:T(4,128)S(1)} %pad_maximum_fusion.4), channel_id=1, source_target_pairs={{0,48},{16,32},{32,16},{48,0},{1,49},{17,33},{33,17},{49,1},{2,50}... | collective-permute-start | bytes 46088 | tf_op jit(solution)/shard_map/ppermute | solution.py:51
  127.4 15.7 %collective-permute-start.8 = (f32[3,1280]{1,0:T(4,128)S(1)}, f32[3,1280]{1,0:T(4,128)S(1)}, u32[]{:S(2)}, u32[]{:S(2)}) collective-permute-start(f32[3,1280]{1,0:T(4,128)S(1)} %pad_maximum_fusion.4), channel_id=1, source_target_pairs={{0,16},{16,0},{32,48},{48,32},{1,17},{17,1},{33,49},{49,33},{2,18}... | collective-permute-start | bytes 46088 | tf_op jit(solution)/shard_map/ppermute | solution.py:51
  129.6 13.6 %collective-permute-start.9 = (f32[3,1280]{1,0:T(4,128)S(1)}, f32[3,1280]{1,0:T(4,128)S(1)}, u32[]{:S(2)}, u32[]{:S(2)}) collective-permute-start(f32[3,1280]{1,0:T(4,128)S(1)} %pad_maximum_fusion.4), channel_id=1, source_target_pairs={{0,32},{16,48},{32,0},{48,16},{1,33},{17,49},{33,1},{49,17},{2,34}... | collective-permute-start | bytes 46088 | tf_op jit(solution)/shard_map/ppermute | solution.py:51
  134.6 36.4 %all-to-all-start.3 = ((bf16[16,80,128]{2,1,0:T(8,128)(2,1)}), bf16[16,80,128]{2,1,0:T(8,128)(2,1)S(1)}, u32[]{:S(2)}, u32[]{:S(2)}) async-start(bf16[16,80,128]{2,1,0:T(8,128)(2,1)} %bitcast.10), calls=%async_computation.3 | async-start | bytes 655360 | tf_op jit(solution)/shard_map/all_to_all | solution.py:426
  143.2 17.5 %collective-permute-start.11 = (f32[3,1280]{1,0:T(4,128)S(1)}, f32[3,1280]{1,0:T(4,128)S(1)}, u32[]{:S(2)}, u32[]{:S(2)}) collective-permute-start(f32[3,1280]{1,0:T(4,128)S(1)} %add_add_fusion.1), channel_id=1, source_target_pairs={{0,64},{64,0},{128,192},{192,128},{256,320},{320,256},{384,448},{4... | collective-permute-start | bytes 46088 | tf_op jit(solution)/shard_map/ppermute | solution.py:51
  146.2 19.0 %collective-permute-start.12 = (f32[3,1280]{1,0:T(4,128)S(1)}, f32[3,1280]{1,0:T(4,128)S(1)}, u32[]{:S(2)}, u32[]{:S(2)}) collective-permute-start(f32[3,1280]{1,0:T(4,128)S(1)} %add_add_fusion.1), channel_id=1, source_target_pairs={{0,128},{64,192},{128,0},{192,64},{256,384},{320,448},{384,256},{4... | collective-permute-start | bytes 46088 | tf_op jit(solution)/shard_map/ppermute | solution.py:51
  149.9 18.9 %collective-permute-start.13 = (f32[3,1280]{1,0:T(4,128)S(1)}, f32[3,1280]{1,0:T(4,128)S(1)}, u32[]{:S(2)}, u32[]{:S(2)}) collective-permute-start(f32[3,1280]{1,0:T(4,128)S(1)} %add_add_fusion.1), channel_id=1, source_target_pairs={{0,192},{64,128},{128,64},{192,0},{256,448},{320,384},{384,320},{4... | collective-permute-start | bytes 46088 | tf_op jit(solution)/shard_map/ppermute | solution.py:51
  152.5 16.3 %collective-permute-start.14 = (f32[3,1280]{1,0:T(4,128)S(1)}, f32[3,1280]{1,0:T(4,128)S(1)}, u32[]{:S(2)}, u32[]{:S(2)}) collective-permute-start(f32[3,1280]{1,0:T(4,128)S(1)} %add_add_fusion.1), channel_id=1, source_target_pairs={{0,256},{64,320},{128,384},{192,448},{256,0},{320,64},{384,128},{4... | collective-permute-start | bytes 46088 | tf_op jit(solution)/shard_map/ppermute | solution.py:51
  157.5 11.3 %collective-permute-start.15 = (f32[3,1280]{1,0:T(4,128)S(1)}, f32[3,1280]{1,0:T(4,128)S(1)}, u32[]{:S(2)}, u32[]{:S(2)}) collective-permute-start(f32[3,1280]{1,0:T(4,128)S(1)} %add_add_fusion.1), channel_id=1, source_target_pairs={{0,320},{64,256},{128,448},{192,384},{256,64},{320,0},{384,192},{4... | collective-permute-start | bytes 46088 | tf_op jit(solution)/shard_map/ppermute | solution.py:51
  160.7 8.1 %collective-permute-start.16 = (f32[3,1280]{1,0:T(4,128)S(1)}, f32[3,1280]{1,0:T(4,128)S(1)}, u32[]{:S(2)}, u32[]{:S(2)}) collective-permute-start(f32[3,1280]{1,0:T(4,128)S(1)} %add_add_fusion.1), channel_id=1, source_target_pairs={{0,384},{64,448},{128,256},{192,320},{256,128},{320,192},{384,0},{... | collective-permute-start | bytes 46088 | tf_op jit(solution)/shard_map/ppermute | solution.py:51
  165.2 5.7 %collective-permute-start.17 = (f32[3,1280]{1,0:T(4,128)S(1)}, f32[3,1280]{1,0:T(4,128)S(1)}, u32[]{:S(2)}, u32[]{:S(2)}) collective-permute-start(f32[3,1280]{1,0:T(4,128)S(1)} %add_add_fusion.1), channel_id=1, source_target_pairs={{0,448},{64,384},{128,320},{192,256},{256,192},{320,128},{384,64},... | collective-permute-start | bytes 46088 | tf_op jit(solution)/shard_map/ppermute | solution.py:51
  171.7 15.7 %all-to-all-start.4 = ((f32[8,3,1280]{2,1,0:T(4,128)}), f32[8,3,1280]{2,1,0:T(4,128)S(1)}, u32[]{:S(2)}, u32[]{:S(2)}) async-start(f32[8,3,1280]{2,1,0:T(4,128)} %broadcast_in_dim.96), calls=%async_computation.4 | async-start | bytes 327680 | tf_op jit(solution)/shard_map/all_to_all | solution.py:44
  (16 other events, 243.4 us)
Sparse Core Ops, SparseCore 0:
  11.8 100.1 all-gather.2

commit v7 on v5

--- a/solution.py
+++ b/solution.py
@@ -333,6 +333,67 @@
     )(bounds, probs, ctx_t, out_t, inv_sum, queries, k_t, values)
 
 
+def pick_kernel(core, low, high, attn, out):
+    width = low.shape[1]
+    out[:, :width] = low[...]
+    out[:, width : 2 * width] = high[...]
+    out[:, 2 * width :] = attn[...]
+
+
+def picked_weights(core, w_in, w_attn_out):
+    rows, width = w_attn_out.shape
+    half = pl.BlockSpec((rows, width // 2), lambda i, c: (0, c[0]))
+    return pl.pallas_call(
+        pick_kernel,
+        grid_spec=pltpu.PrefetchScalarGridSpec(
+            num_scalar_prefetch=1,
+            grid=(1,),
+            in_specs=[
+                half,
+                pl.BlockSpec((rows, width // 2), lambda i, c: (0, c[0] + 2)),
+                pl.BlockSpec((rows, width), lambda i, c: (0, 0)),
+            ],
+            out_specs=pl.BlockSpec((rows, 2 * width), lambda i, c: (0, 0)),
+        ),
+        out_shape=jax.ShapeDtypeStruct((rows, 2 * width), w_in.dtype),
+        cost_estimate=pl.CostEstimate(
+            flops=0, transcendentals=0, bytes_accessed=8 * rows * width
+        ),
+        name="picked_weights",
+    )(core.reshape(1).astype(jnp.int32), w_in, w_in, w_attn_out)
+
+
+def norm_kernel(own, other, piece, mine, theirs):
+    over = (((1,), (1,)), ((), ()))
+    weights = piece[...]
+    mine[...] = lax.dot_general(own[...], weights, over, preferred_element_type=jnp.float32)
+    part = lax.dot_general(other[...], weights, over, preferred_element_type=jnp.float32)
+    theirs[...] = part.astype(jnp.bfloat16)
+
+
+def norm_products(own, other, gathered):
+    rows, width = own.shape
+    out = gathered.shape[0]
+    gathered = pltpu.with_memory_space_constraint(gathered, pltpu.HBM)
+    whole = pl.BlockSpec((rows, width), lambda i: (0, 0))
+    lanes = pl.BlockSpec((rows, BLK), lambda i: (0, i))
+    return pl.pallas_call(
+        norm_kernel,
+        grid=(out // BLK,),
+        in_specs=[whole, whole, pl.BlockSpec((BLK, width), lambda i: (i, 0))],
+        out_specs=[lanes, lanes],
+        out_shape=[
+            jax.ShapeDtypeStruct((rows, out), jnp.float32),
+            jax.ShapeDtypeStruct((rows, out), jnp.bfloat16),
+        ],
+        compiler_params=pltpu.CompilerParams(vmem_limit_bytes=10 << 20),
+        cost_estimate=pl.CostEstimate(
+            flops=4 * rows * width * out, transcendentals=0, bytes_accessed=2 * width * out
+        ),
+        name="norm_products",
+    )(own, other, gathered)
+
+
 def local(
     grad_out,
     saved_input,
@@ -353,11 +414,7 @@
     core = lax.axis_index("core")
     ends = frame_ends(frame_counts[0])
 
-    in_low, _ = halves(w_in[:, :width], core)
-    in_high, _ = halves(w_in[:, width:], core)
-    gathered = lax.all_gather(
-        jnp.concatenate([in_low, in_high, w_attn_out], axis=1), GROUPS, axis=0, tiled=True
-    )
+    gathered = lax.all_gather(picked_weights(core, w_in, w_attn_out), GROUPS, axis=0, tiled=True)
 
     positions = jnp.arange(total, dtype=jnp.int32)
     passed = positions[None, :] >= ends[:, None]
@@ -391,13 +448,12 @@
     rows = jnp.sum(lax.all_to_all(rows, TIME, split_axis=0, concat_axis=0), axis=0)
 
     gathered, rows = lax.optimization_barrier((gathered, rows))
-    w_in_half = gathered[:, :width]
     w_attn = gathered[:, width:]
-    norm_grad = pair_product(
-        jnp.concatenate([low_own, high_own], axis=1),
-        jnp.concatenate([low_away, high_away], axis=1),
-        w_in_half,
+    away = swap(jnp.concatenate([low_away, high_away], axis=1))
+    norm_grad, back = norm_products(
+        jnp.concatenate([low_own, high_own], axis=1), away, gathered
     )
+    norm_grad = norm_grad + swap(back).astype(jnp.float32)
     inputs = saved_input.astype(jnp.float32)
     centred = inputs - jnp.mean(inputs, axis=1, keepdims=True)
     inv_std = 1.0 / jnp.sqrt(jnp.mean(centred * centred, axis=1, keepdims=True) + 1e-05)
@@ -415,14 +471,15 @@
     ctx_t, gain = lax.optimization_barrier((ctx_t, gain))
     ctx_t = lax.all_to_all(ctx_t, TIME, split_axis=0, concat_axis=0)
     sums = jnp.concatenate([rows, gain], axis=0)
-    for axis in (("far", "y"), "x"):
-        sums = jnp.sum(lax.all_gather(sums, axis), axis=0)
+    for bit in (1, 2):
+        sums = sums + lax.ppermute(sums, "y", [(i, i ^ bit) for i in range(lax.axis_size("y"))])
     ctx_t, sums = lax.optimization_barrier((ctx_t, sums))
     probs = pltpu.with_memory_space_constraint(probs, pltpu.HBM)
-    stacked = spread(sums, "z")
+    stacked = spread(sums, ("far", "x"))
     grads = attention_grads(bounds, probs, ctx_t, out_t, inv_sum, queries, keys.T, values)
     query_grad, key_grad, value_grad = [array.T for array in grads]
     stacked, query_grad = lax.optimization_barrier((stacked, query_grad))
+    stacked = spread(jnp.sum(stacked, axis=0), "z")
     stacked = lax.all_gather(stacked, "core", axis=0)
     kernel_grad = stacked[:, :, :-1].reshape(KW + 1, width)[:KW]
     gain_grad = jnp.sum(stacked[:, :, -1], axis=(0, 1))

time: 200 us -> 189 us (0.945)
  blocking collectives: 39.1 us -> 18 us
  waiting for transfers between devices: 26.1 us -> 36.5 us
  matrix products: 9.62 us -> 3.88 us
  starting transfers between devices: 64.4 us -> 69.3 us
  Pallas kernels: 29.7 us -> 33.4 us
  other arithmetic: 4.94 us -> 2.62 us
    all_gather x2 -> x0, blocking collectives: 27.8 us -> none  [local(): sums = jnp.sum(lax.all_gather(sums, axis), axis=0)]
    all_to_all x0 -> x1, blocking collectives: none -> 11.2 us  [spread(): return lax.all_to_all(copies, axis, split_axis=0, concat_axis=0)]
    pallas_call x0 -> x2, Pallas kernels: none -> 7.26 us  [the longest x1 5.55 us: norm_products(): pl.pallas_call(norm_kernel, grid=(out // BLK,), in_specs=[whole, whole, p...]
    ppermute x0 -> x2, starting transfers between devices: none -> 6.39 us  [local(): lax.ppermute(sums, 'y', [(i, i ^ bit) for i in range(lax.axis_size('y'))])]
    dot_general x4 -> x2, matrix products: 7.87 us -> 2.14 us  [row_product(): jnp.einsum('tc,rc->tr', active, piece, preferred_element_type=jnp.float32)]
    all_to_all x3, waiting for transfers between devices: 6.22 us -> 10.7 us  [spread(): return lax.all_to_all(copies, axis, split_axis=0, concat_axis=0)]
    all_gather x1, blocking collectives: 11.2 us -> 6.85 us  [local(): stacked = lax.all_gather(stacked, 'core', axis=0)]
    ppermute x0 -> x2, waiting for transfers between devices: none -> 3.59 us  [local(): lax.ppermute(sums, 'y', [(i, i ^ bit) for i in range(lax.axis_size('y'))])]
  transfers between devices with their start and end apart: 14 -> 16, of which waited for: 7 -> 11; matrix products, arithmetic and copies ran while one was open for 5% -> 6% of each run, Pallas kernels for 15% -> 14%
where the time goes in v7:
time: 189 us; the launch traced here: 188 us
  starting transfers between devices  69.3 us (37%)
  waiting for transfers between devices  36.5 us (19%)
  Pallas kernels  33.4 us (18%)
  blocking collectives  18 us (10%)
  between operations  14.6 us (8%)
  local copies, waits for them, and re-layouts  9.78 us (5%)
  matrix products  3.88 us (2%)
  other arithmetic  2.62 us (1%)
    all_to_all x3, starting transfers between devices, spread(): return lax.all_to_all(copies, axis, split_axis=0, concat_axis=0)  19.8 us
    ppermute x4, starting transfers between devices, swap(): return lax.ppermute(array, 'core', [(0, 1), (1, 0)])  12.4 us
    all_to_all x1, blocking collectives, spread(): return lax.all_to_all(copies, axis, split_axis=0, concat_axis=0)  11.2 us
    all_to_all x3, waiting for transfers between devices, spread(): return lax.all_to_all(copies, axis, split_axis=0, concat_axis=0)  10.7 us
    all_to_all x1, starting transfers between devices, local(): lax.all_to_all(rows, TIME, split_axis=0, concat_axis=0)  10.1 us
    all_to_all x1, waiting for transfers between devices, local(): lax.all_to_all(rows, TIME, split_axis=0, concat_axis=0)  9.61 us
    pallas_call x1, Pallas kernels, attention_grads(): pl.pallas_call(grads_kernel, grid_spec=pltpu.PrefetchScalarGridSpec(num_s...  9.11 us
    ppermute x2, starting transfers between devices, padded(): low = lax.ppermute(block[block.shape[0] - width:], TIME, forward)  8.89 us
  transfers between devices with their start and end apart: 16, of which 11 were waited for; matrix products, arithmetic and copies ran while one was open for 6% of the time, Pallas kernels for 14%

profile of v7, /device:TPU:1, one launch (start us, length us, event | category | flops | bytes accessed | tf_op | source)
XLA Modules:
  0.0 188.0 jit_solution(3960661251001112096)
XLA Ops:
  9.8 7.7 %all-to-all-start = ((bf16[8,40,640]{2,1,0:T(8,128)(2,1)}), bf16[8,40,640]{2,1,0:T(8,128)(2,1)S(1)}, u32[]{:S(2)}, u32[]{:S(2)}) async-start(bf16[8,40,640]{2,1,0:T(8,128)(2,1)} %broadcast_in_dim.59), calls=%async_computation | async-start | bytes 819200 | tf_op jit(solution)/shard_map/all_to_all | solution.py:44
  17.7 4.8 %collective-permute-start = (bf16[16,1280]{1,0:T(8,128)(2,1)S(1)}, bf16[16,1280]{1,0:T(8,128)(2,1)S(1)}, u32[]{:S(2)}, u32[]{:S(2)}) collective-permute-start(bf16[16,1280]{1,0:T(8,128)(2,1)S(1)} %get-tuple-element.65), channel_id=1, source_target_pairs={{0,1},{1,2},{2,3},{3,4},{4,5},{5,6},{6,7},{7,8},{8,9},{9,10},{10,1... | collective-permute-start | bytes 122888 | tf_op jit(solution)/shard_map/ppermute | solution.py:36
  24.7 4.7 %all-to-all-done = bf16[8,40,640]{2,1,0:T(8,128)(2,1)S(1)} async-done(((bf16[8,40,640]{2,1,0:T(8,128)(2,1)}), bf16[8,40,640]{2,1,0:T(8,128)(2,1)S(1)}, u32[]{:S(2)}, u32[]{:S(2)}) %all-to-all-start) | async-done | bytes 409632 | tf_op jit(solution)/shard_map/all_to_all | solution.py:44
  30.8 6.9 %all-to-all-start.1 = ((bf16[4,8,40,640]{3,2,1,0:T(8,128)(2,1)}), bf16[4,8,40,640]{3,2,1,0:T(8,128)(2,1)}, u32[]{:S(2)}, u32[]{:S(2)}) async-start(bf16[4,8,40,640]{3,2,1,0:T(8,128)(2,1)} %broadcast_in_dim.98), calls=%async_computation.1 | async-start | bytes 3276800 | tf_op jit(solution)/shard_map/all_to_all | solution.py:44
  38.4 3.5 %collective-permute-start.2 = (bf16[128,640]{1,0:T(8,128)(2,1)}, bf16[128,640]{1,0:T(8,128)(2,1)}, u32[]{:S(2)}, u32[]{:S(2)}) collective-permute-start(bf16[128,640]{1,0:T(8,128)(2,1)} %constant_dynamic-slice_fusion.4), channel_id=1, source_target_pairs={{0,1},{1,0},{2,3},{3,2},{4,5},{5,4},{6,7},{7,6},{8,9},{9,8},{10,11... | collective-permute-start | bytes 491528 | tf_op jit(solution)/shard_map/ppermute | solution.py:59
  43.4 2.9 %conv_factor.1 = f32[128,1280]{1,0:T(8,128)S(1)} custom-call(s32[160,128]{1,0:T(8,128)S(1)} %broadcast_in_dim.58.seg, bf16[160,1280]{1,0:T(8,128)(2,1)S(1)} %pad_maximum_fusion.glu, f32[31,1280]{1,0:T(8,128)S(1)} %copy-done.3), custom_call_target="tpu_custom_call" | custom-call | flops 20316160 | bytes 1310720 | tf_op jit(solution)/shard_map/conv_factor/pallas_call | solution.py:96
  47.4 7.5 %attention_probs.1 = (bf16[4,2048,512]{2,1,0:T(8,128)(2,1)}, f32[80,2048]{1,0:T(8,128)S(1)}, f32[1,2048]{1,0:T(1,128)S(1)}) custom-call(s32[2,4]{1,0:T(2,128)S(1)} %pad_add_fusion.bounds, bf16[80,2048]{1,0:T(8,128)(2,1)S(1)} %bitcast.24, bf16[2048,80]{1,0:T(8,128)(2,1)S(1)} %copy-done.4, bf16[80,2048]{1,0:T(8,128)(2,1)S(1)} %bitcast.25, ...), custom_call_target="tpu_custom_call" | custom-call | flops 1342177280 | bytes 8388608 | tf_op jit(solution)/shard_map/attention_probs/pallas_call | solution.py:233
  54.9 4.9 %all-to-all-done.1 = bf16[4,8,40,640]{3,2,1,0:T(8,128)(2,1)} async-done(((bf16[4,8,40,640]{3,2,1,0:T(8,128)(2,1)}), bf16[4,8,40,640]{3,2,1,0:T(8,128)(2,1)}, u32[]{:S(2)}, u32[]{:S(2)}) %all-to-all-start.1) | async-done | bytes 1638432 | tf_op jit(solution)/shard_map/all_to_all | solution.py:44
  62.9 3.9 %collective-permute-start.3 = (bf16[128,1280]{1,0:T(8,128)(2,1)S(1)}, bf16[128,1280]{1,0:T(8,128)(2,1)S(1)}, u32[]{:S(2)}, u32[]{:S(2)}) collective-permute-start(bf16[128,1280]{1,0:T(8,128)(2,1)S(1)} %convolution_convert_fusion), channel_id=1, source_target_pairs={{0,1},{1,0},{2,3},{3,2},{4,5},{5,4},{6,7},{7,6},{8,9},{9,8},{10,11... | collective-permute-start | bytes 983048 | tf_op jit(solution)/shard_map/ppermute | solution.py:59
  68.2 4.0 %collective-permute-start.4 = (bf16[16,1280]{1,0:T(8,128)(2,1)S(1)}, bf16[16,1280]{1,0:T(8,128)(2,1)S(1)}, u32[]{:S(2)}, u32[]{:S(2)}) collective-permute-start(bf16[16,1280]{1,0:T(8,128)(2,1)S(1)} %get-tuple-element.63), channel_id=1, source_target_pairs={{0,1},{1,2},{2,3},{3,4},{4,5},{5,6},{6,7},{7,8},{8,9},{9,10},{10,1... | collective-permute-start | bytes 122888 | tf_op jit(solution)/shard_map/ppermute | solution.py:36
  74.3 3.7 %collective-permute-done.5 = bf16[16,1280]{1,0:T(8,128)(2,1)S(1)} collective-permute-done((bf16[16,1280]{1,0:T(8,128)(2,1)S(1)}, bf16[16,1280]{1,0:T(8,128)(2,1)S(1)}, u32[]{:S(2)}, u32[]{:S(2)}) %collective-permute-start.5) | collective-permute-done | bytes 40992 | tf_op jit(solution)/shard_map/ppermute | solution.py:37
  78.0 6.5 %conv_grads.1 = (bf16[128,1280]{1,0:T(8,128)(2,1)S(1)}, bf16[128,1280]{1,0:T(8,128)(2,1)S(1)}, f32[32,1280]{1,0:T(8,128)S(1)}) custom-call(s32[160,128]{1,0:T(8,128)S(1)} %broadcast_in_dim.58.seg, bf16[160,1280]{1,0:T(8,128)(2,1)S(1)} %pad_maximum_fusion.1.grad, bf16[160,1280]{1,0:T(8,128)(2,1)S(1)} %pad_maximum_fusion.glu, bf16[128,2560]{1,0:T(8,128)(2,1)S(1)} %copy-done.1, ...), custom_call_target="tpu_custom_call" | custom-call | flops 40632320 | bytes 2621440 | tf_op jit(solution)/shard_map/conv_grads/pallas_call | solution.py:145
  87.4 10.1 %all-to-all-start.2 = ((f32[16,2,1280]{2,1,0:T(2,128)}), f32[16,2,1280]{2,1,0:T(2,128)S(1)}, u32[]{:S(2)}, u32[]{:S(2)}) async-start(f32[16,2,1280]{2,1,0:T(2,128)} %bitcast.10), calls=%async_computation.2 | async-start | bytes 327680 | tf_op jit(solution)/shard_map/all_to_all | solution.py:448
  97.5 9.6 %all-to-all-done.2 = f32[16,2,1280]{2,1,0:T(2,128)S(1)} async-done(((f32[16,2,1280]{2,1,0:T(2,128)}), f32[16,2,1280]{2,1,0:T(2,128)S(1)}, u32[]{:S(2)}, u32[]{:S(2)}) %all-to-all-start.2) | async-done | bytes 163872 | tf_op jit(solution)/shard_map/all_to_all | solution.py:448
  107.2 4.8 %all-gather.3.cloned.1.call-done.piece = bf16[1280,2560]{1,0:T(8,128)(2,1)} async-done(((bf16[40,2560]{1,0:T(8,128)(2,1)}), bf16[1280,2560]{1,0:T(8,128)(2,1)}) %all-gather.3.cloned.1.call-update) | async-done | bytes 6553616 | tf_op jit(solution)/shard_map/all_gather | solution.py:417
  112.0 5.6 %norm_products.1 = (f32[128,1280]{1,0:T(8,128)S(1)}, bf16[128,1280]{1,0:T(8,128)(2,1)S(1)}) custom-call(bf16[128,1280]{1,0:T(8,128)(2,1)S(1)} %pad_maximum_fusion.2.own, bf16[128,1280]{1,0:T(8,128)(2,1)S(1)} %collective-permute-done.6.other, bf16[1280,2560]{1,0:T(8,128)(2,1)} %all-gather.3.cloned.1.call-done.piece), custom_call_target="tpu_custom_call" | custom-call | flops 838860800 | bytes 3276800 | tf_op jit(solution)/shard_map/norm_products/pallas_call | solution.py:380
  117.5 3.0 %collective-permute-start.7 = (bf16[128,1280]{1,0:T(8,128)(2,1)S(1)}, bf16[128,1280]{1,0:T(8,128)(2,1)S(1)}, u32[]{:S(2)}, u32[]{:S(2)}) collective-permute-start(bf16[128,1280]{1,0:T(8,128)(2,1)S(1)} %get-tuple-element.40), channel_id=1, source_target_pairs={{0,1},{1,0},{2,3},{3,2},{4,5},{5,4},{6,7},{7,6},{8,9},{9,8},{10,11... | collective-permute-start | bytes 983048 | tf_op jit(solution)/shard_map/ppermute | solution.py:59
  124.4 7.9 %all-to-all-start.3 = ((bf16[16,80,128]{2,1,0:T(8,128)(2,1)}), bf16[16,80,128]{2,1,0:T(8,128)(2,1)S(1)}, u32[]{:S(2)}, u32[]{:S(2)}) async-start(bf16[16,80,128]{2,1,0:T(8,128)(2,1)} %bitcast.11), calls=%async_computation.3 | async-start | bytes 655360 | tf_op jit(solution)/shard_map/all_to_all | solution.py:472
  132.3 3.0 %collective-permute-start.8 = (f32[3,1280]{1,0:T(4,128)S(1)}, f32[3,1280]{1,0:T(4,128)S(1)}, u32[]{:S(2)}, u32[]{:S(2)}) collective-permute-start(f32[3,1280]{1,0:T(4,128)S(1)} %pad_maximum_fusion.4), channel_id=1, source_target_pairs={{0,64},{64,0},{128,192},{192,128},{1,65},{65,1},{129,193},{193,129... | collective-permute-start | bytes 46088 | tf_op jit(solution)/shard_map/ppermute | solution.py:475
  137.1 3.4 %collective-permute-start.9 = (f32[3,1280]{1,0:T(4,128)S(1)}, f32[3,1280]{1,0:T(4,128)S(1)}, u32[]{:S(2)}, u32[]{:S(2)}) collective-permute-start(f32[3,1280]{1,0:T(4,128)S(1)} %fusion.20), channel_id=1, source_target_pairs={{0,128},{64,192},{128,0},{192,64},{1,129},{65,193},{129,1},{193,65... | collective-permute-start | bytes 46088 | tf_op jit(solution)/shard_map/ppermute | solution.py:475
  146.0 5.2 %all-to-all-start.4 = ((f32[8,3,1280]{2,1,0:T(4,128)}), f32[8,3,1280]{2,1,0:T(4,128)S(1)}, u32[]{:S(2)}, u32[]{:S(2)}) async-start(f32[8,3,1280]{2,1,0:T(4,128)} %broadcast_in_dim.102), calls=%async_computation.4 | async-start | bytes 327680 | tf_op jit(solution)/shard_map/all_to_all | solution.py:44
  151.3 9.1 %attention_grads.1 = (bf16[80,2048]{1,0:T(8,128)(2,1)}, bf16[80,2048]{1,0:T(8,128)(2,1)}, bf16[80,2048]{1,0:T(8,128)(2,1)}) custom-call(s32[2,4]{1,0:T(2,128)S(1)} %pad_add_fusion.bounds, bf16[4,2048,512]{2,1,0:T(8,128)(2,1)} %get-tuple-element.45.probs, bf16[16,80,128]{2,1,0:T(8,128)(2,1)S(1)} %all-to-all-done.3.ctx_t, ...), custom_call_target="tpu_custom_call" | custom-call | flops 2684354560 | bytes 8388608 | tf_op jit(solution)/shard_map/attention_grads/pallas_call | solution.py:308
  161.6 11.2 %all_to_all.30 = f32[8,3,1280]{2,1,0:T(4,128)S(1)} all-to-all(f32[8,3,1280]{2,1,0:T(4,128)S(1)} %broadcast_in_dim.103), channel_id=1, replica_groups=mesh['far'=2,'y'=4,'x'=4,'z'=8,'core'=2] {'z'}, dimensions={0} | all-to-all | bytes 245760 | tf_op jit(solution)/shard_map/all_to_all | solution.py:44
  172.7 6.8 %all-gather = f32[16,3,1280]{2,0,1:T(8,128)S(1)} all-gather(f32[8,3,1280]{2,0,1:T(8,128)S(1)} %copy.43), channel_id=2, replica_groups=mesh['far'=2,'y'=4,'x'=4,'z'=8,'core'=2] {'core'}, dimensions={0}, use_global_device_ids=true | all-gather | bytes 368640 | tf_op jit(solution)/shard_map/all_gather | solution.py:483
  (105 shorter events, 32.6 us)
Async XLA Ops:
  7.2 10.3 %copy-start.1 = (bf16[128,2560]{1,0:T(8,128)(2,1)S(1)}, bf16[128,2560]{1,0:T(8,128)(2,1)}, u32[]{:S(2)}) copy-start(bf16[128,2560]{1,0:T(8,128)(2,1)} %gate_ref.1) | copy-start | bytes 1966084
  7.2 104.8 %all-gather.3.cloned.1.call-start = ((), (), s32[]{:S(2)}) async-start(), calls=%async_computation.6 | async-start | bytes 6758400 | tf_op jit(solution)/shard_map/all_gather | solution.py:417
  7.2 17.2 %copy-start.16 = (s32[1,8]{1,0:T(1,128)S(1)}, s32[1,8]{1,0:T(1,128)}, u32[]{:S(2)}) copy-start(s32[1,8]{1,0:T(1,128)} %param.18) | copy-start | bytes 100
  9.8 19.6 %all-to-all-start = ((bf16[8,40,640]{2,1,0:T(8,128)(2,1)}), bf16[8,40,640]{2,1,0:T(8,128)(2,1)S(1)}, u32[]{:S(2)}, u32[]{:S(2)}) async-start(bf16[8,40,640]{2,1,0:T(8,128)(2,1)} %broadcast_in_dim.59), calls=%async_computation | async-start | bytes 819200 | tf_op jit(solution)/shard_map/all_to_all | solution.py:44
  17.7 25.6 %collective-permute-start = (bf16[16,1280]{1,0:T(8,128)(2,1)S(1)}, bf16[16,1280]{1,0:T(8,128)(2,1)S(1)}, u32[]{:S(2)}, u32[]{:S(2)}) collective-permute-start(bf16[16,1280]{1,0:T(8,128)(2,1)S(1)} %get-tuple-element.65), channel_id=1, source_target_pairs={{0,1},{1,2},{2,3},{3,4},{4,5},{5,6},{6,7},{7,8},{8,9},{9,10},{10,1... | collective-permute-start | bytes 122888 | tf_op jit(solution)/shard_map/ppermute | solution.py:36
  22.5 20.7 %collective-permute-start.1 = (bf16[16,1280]{1,0:T(8,128)(2,1)S(1)}, bf16[16,1280]{1,0:T(8,128)(2,1)S(1)}, u32[]{:S(2)}, u32[]{:S(2)}) collective-permute-start(bf16[16,1280]{1,0:T(8,128)(2,1)S(1)} %get-tuple-element.66), channel_id=1, source_target_pairs={{1,0},{2,1},{3,2},{4,3},{5,4},{6,5},{7,6},{8,7},{9,8},{10,9},{11,1... | collective-permute-start | bytes 122888 | tf_op jit(solution)/shard_map/ppermute | solution.py:37
  30.8 11.5 %copy-start.2 = (bf16[2048,80]{0,1:T(8,128)(2,1)S(1)}, bf16[2048,80]{0,1:T(8,128)(2,1)}, u32[]{:S(2)}) copy-start(bf16[2048,80]{0,1:T(8,128)(2,1)} %param.16) | copy-start | bytes 983044
  30.8 29.0 %all-to-all-start.1 = ((bf16[4,8,40,640]{3,2,1,0:T(8,128)(2,1)}), bf16[4,8,40,640]{3,2,1,0:T(8,128)(2,1)}, u32[]{:S(2)}, u32[]{:S(2)}) async-start(bf16[4,8,40,640]{3,2,1,0:T(8,128)(2,1)} %broadcast_in_dim.98), calls=%async_computation.1 | async-start | bytes 3276800 | tf_op jit(solution)/shard_map/all_to_all | solution.py:44
  37.7 8.7 %copy-start.5 = (bf16[2048,80]{0,1:T(8,128)(2,1)S(1)}, bf16[2048,80]{0,1:T(8,128)(2,1)}, u32[]{:S(2)}) copy-start(bf16[2048,80]{0,1:T(8,128)(2,1)} %param.15) | copy-start | bytes 983044
  38.4 23.0 %collective-permute-start.2 = (bf16[128,640]{1,0:T(8,128)(2,1)}, bf16[128,640]{1,0:T(8,128)(2,1)}, u32[]{:S(2)}, u32[]{:S(2)}) collective-permute-start(bf16[128,640]{1,0:T(8,128)(2,1)} %constant_dynamic-slice_fusion.4), channel_id=1, source_target_pairs={{0,1},{1,0},{2,3},{3,2},{4,5},{5,4},{6,7},{7,6},{8,9},{9,8},{10,11... | collective-permute-start | bytes 491528 | tf_op jit(solution)/shard_map/ppermute | solution.py:59
  62.9 5.1 %collective-permute-start.3 = (bf16[128,1280]{1,0:T(8,128)(2,1)S(1)}, bf16[128,1280]{1,0:T(8,128)(2,1)S(1)}, u32[]{:S(2)}, u32[]{:S(2)}) collective-permute-start(bf16[128,1280]{1,0:T(8,128)(2,1)S(1)} %convolution_convert_fusion), channel_id=1, source_target_pairs={{0,1},{1,0},{2,3},{3,2},{4,5},{5,4},{6,7},{7,6},{8,9},{9,8},{10,11... | collective-permute-start | bytes 983048 | tf_op jit(solution)/shard_map/ppermute | solution.py:59
  68.2 6.1 %collective-permute-start.4 = (bf16[16,1280]{1,0:T(8,128)(2,1)S(1)}, bf16[16,1280]{1,0:T(8,128)(2,1)S(1)}, u32[]{:S(2)}, u32[]{:S(2)}) collective-permute-start(bf16[16,1280]{1,0:T(8,128)(2,1)S(1)} %get-tuple-element.63), channel_id=1, source_target_pairs={{0,1},{1,2},{2,3},{3,4},{4,5},{5,6},{6,7},{7,8},{8,9},{9,10},{10,1... | collective-permute-start | bytes 122888 | tf_op jit(solution)/shard_map/ppermute | solution.py:36
  72.2 5.7 %collective-permute-start.5 = (bf16[16,1280]{1,0:T(8,128)(2,1)S(1)}, bf16[16,1280]{1,0:T(8,128)(2,1)S(1)}, u32[]{:S(2)}, u32[]{:S(2)}) collective-permute-start(bf16[16,1280]{1,0:T(8,128)(2,1)S(1)} %get-tuple-element.64), channel_id=1, source_target_pairs={{1,0},{2,1},{3,2},{4,3},{5,4},{6,5},{7,6},{8,7},{9,8},{10,9},{11,1... | collective-permute-start | bytes 122888 | tf_op jit(solution)/shard_map/ppermute | solution.py:37
  84.7 27.3 %collective-permute-start.6 = (bf16[128,1280]{1,0:T(8,128)(2,1)S(1)}, bf16[128,1280]{1,0:T(8,128)(2,1)S(1)}, u32[]{:S(2)}, u32[]{:S(2)}) collective-permute-start(bf16[128,1280]{1,0:T(8,128)(2,1)S(1)} %pad_maximum_fusion.3), channel_id=1, source_target_pairs={{0,1},{1,0},{2,3},{3,2},{4,5},{5,4},{6,7},{7,6},{8,9},{9,8},{10,11... | collective-permute-start | bytes 983048 | tf_op jit(solution)/shard_map/ppermute | solution.py:59
  87.4 19.7 %all-to-all-start.2 = ((f32[16,2,1280]{2,1,0:T(2,128)}), f32[16,2,1280]{2,1,0:T(2,128)S(1)}, u32[]{:S(2)}, u32[]{:S(2)}) async-start(f32[16,2,1280]{2,1,0:T(2,128)} %bitcast.10), calls=%async_computation.2 | async-start | bytes 327680 | tf_op jit(solution)/shard_map/all_to_all | solution.py:448
  107.2 13.4 %copy-start.10 = (bf16[128,1280]{1,0:T(8,128)(2,1)S(1)}, bf16[128,1280]{1,0:T(8,128)(2,1)}, u32[]{:S(2)}) copy-start(bf16[128,1280]{1,0:T(8,128)(2,1)} %param.13) | copy-start | bytes 983044
  107.2 14.7 %copy-start.15 = (f32[1280]{0:T(1024)S(1)}, f32[1280]{0:T(1024)}, u32[]{:S(2)}) copy-start(f32[1280]{0:T(1024)} %param.19) | copy-start | bytes 15364
  112.0 10.6 %copy-start.8 = (bf16[1280,2560]{1,0:T(8,128)(2,1)S(1)}, bf16[1280,2560]{1,0:T(8,128)(2,1)}, u32[]{:S(2)}) copy-start(bf16[1280,2560]{1,0:T(8,128)(2,1)} %all-gather.3.cloned.1.call-done.piece) | copy-start | bytes 19660804
  117.5 4.3 %collective-permute-start.7 = (bf16[128,1280]{1,0:T(8,128)(2,1)S(1)}, bf16[128,1280]{1,0:T(8,128)(2,1)S(1)}, u32[]{:S(2)}, u32[]{:S(2)}) collective-permute-start(bf16[128,1280]{1,0:T(8,128)(2,1)S(1)} %get-tuple-element.40), channel_id=1, source_target_pairs={{0,1},{1,0},{2,3},{3,2},{4,5},{5,4},{6,7},{7,6},{8,9},{9,8},{10,11... | collective-permute-start | bytes 983048 | tf_op jit(solution)/shard_map/ppermute | solution.py:59
  124.3 16.5 %copy-start.7 = (bf16[2048,80]{0,1:T(8,128)(2,1)S(1)}, bf16[2048,80]{0,1:T(8,128)(2,1)}, u32[]{:S(2)}) copy-start(bf16[2048,80]{0,1:T(8,128)(2,1)} %param.17) | copy-start | bytes 983044
  124.4 21.0 %all-to-all-start.3 = ((bf16[16,80,128]{2,1,0:T(8,128)(2,1)}), bf16[16,80,128]{2,1,0:T(8,128)(2,1)S(1)}, u32[]{:S(2)}, u32[]{:S(2)}) async-start(bf16[16,80,128]{2,1,0:T(8,128)(2,1)} %bitcast.11), calls=%async_computation.3 | async-start | bytes 655360 | tf_op jit(solution)/shard_map/all_to_all | solution.py:472
  132.3 4.8 %collective-permute-start.8 = (f32[3,1280]{1,0:T(4,128)S(1)}, f32[3,1280]{1,0:T(4,128)S(1)}, u32[]{:S(2)}, u32[]{:S(2)}) collective-permute-start(f32[3,1280]{1,0:T(4,128)S(1)} %pad_maximum_fusion.4), channel_id=1, source_target_pairs={{0,64},{64,0},{128,192},{192,128},{1,65},{65,1},{129,193},{193,129... | collective-permute-start | bytes 46088 | tf_op jit(solution)/shard_map/ppermute | solution.py:475
  137.1 5.7 %collective-permute-start.9 = (f32[3,1280]{1,0:T(4,128)S(1)}, f32[3,1280]{1,0:T(4,128)S(1)}, u32[]{:S(2)}, u32[]{:S(2)}) collective-permute-start(f32[3,1280]{1,0:T(4,128)S(1)} %fusion.20), channel_id=1, source_target_pairs={{0,128},{64,192},{128,0},{192,64},{1,129},{65,193},{129,1},{193,65... | collective-permute-start | bytes 46088 | tf_op jit(solution)/shard_map/ppermute | solution.py:475
  146.0 15.5 %all-to-all-start.4 = ((f32[8,3,1280]{2,1,0:T(4,128)}), f32[8,3,1280]{2,1,0:T(4,128)S(1)}, u32[]{:S(2)}, u32[]{:S(2)}) async-start(f32[8,3,1280]{2,1,0:T(4,128)} %broadcast_in_dim.102), calls=%async_computation.4 | async-start | bytes 327680 | tf_op jit(solution)/shard_map/all_to_all | solution.py:44
  (9 other events, 37.2 us)
Sparse Core Ops, SparseCore 0:
  11.8 100.1 all-gather.2

commit v8 on v7

--- a/solution.py
+++ b/solution.py
@@ -363,29 +363,38 @@
     )(core.reshape(1).astype(jnp.int32), w_in, w_in, w_attn_out)
 
 
-def norm_kernel(own, other, piece, mine, theirs):
-    over = (((1,), (1,)), ((), ()))
-    weights = piece[...]
-    mine[...] = lax.dot_general(own[...], weights, over, preferred_element_type=jnp.float32)
-    part = lax.dot_general(other[...], weights, over, preferred_element_type=jnp.float32)
-    theirs[...] = part.astype(jnp.bfloat16)
+def norm_kernel(own, other, piece, mine, theirs, both):
+    rows = own.shape[0]
+
+    @pl.when(pl.program_id(0) == 0)
+    def _():
+        both[:rows, :] = own[...]
+        both[rows:, :] = other[...]
+
+    product = lax.dot_general(
+        both[...], piece[...], (((1,), (1,)), ((), ())), preferred_element_type=jnp.float32
+    )
+    mine[...] = product[:rows]
+    theirs[...] = product[rows:].astype(jnp.bfloat16)
 
 
 def norm_products(own, other, gathered):
     rows, width = own.shape
     out = gathered.shape[0]
+    step = out // 2
     gathered = pltpu.with_memory_space_constraint(gathered, pltpu.HBM)
     whole = pl.BlockSpec((rows, width), lambda i: (0, 0))
-    lanes = pl.BlockSpec((rows, BLK), lambda i: (0, i))
+    lanes = pl.BlockSpec((rows, step), lambda i: (0, i))
     return pl.pallas_call(
         norm_kernel,
-        grid=(out // BLK,),
-        in_specs=[whole, whole, pl.BlockSpec((BLK, width), lambda i: (i, 0))],
+        grid=(out // step,),
+        in_specs=[whole, whole, pl.BlockSpec((step, width), lambda i: (i, 0))],
         out_specs=[lanes, lanes],
         out_shape=[
             jax.ShapeDtypeStruct((rows, out), jnp.float32),
             jax.ShapeDtypeStruct((rows, out), jnp.bfloat16),
         ],
+        scratch_shapes=[pltpu.VMEM((2 * rows, width), jnp.bfloat16)],
         compiler_params=pltpu.CompilerParams(vmem_limit_bytes=10 << 20),
         cost_estimate=pl.CostEstimate(
             flops=4 * rows * width * out, transcendentals=0, bytes_accessed=2 * width * out

time: 189 us -> 187 us (0.989)
  waiting for transfers between devices: 36.5 us -> 33.1 us
    all_to_all x3, waiting for transfers between devices: 10.7 us -> 7.48 us  [spread(): return lax.all_to_all(copies, axis, split_axis=0, concat_axis=0)]
    pallas_call x1, Pallas kernels: 5.55 us -> 3.12 us  [norm_products(): pl.pallas_call(norm_kernel, grid=(out // step,), in_specs=[whole, whole,...]
    pallas_call x1, Pallas kernels: 7.52 us -> 9.65 us  [attention_probs(): pl.pallas_call(probs_kernel, grid_spec=pltpu.PrefetchScalarGridSpec(num_s...]
  transfers between devices with their start and end apart: 16 -> 16, of which waited for: 11 -> 10; matrix products, arithmetic and copies ran while one was open for 6% -> 6% of each run, Pallas kernels for 14% -> 16%
where the time goes in v8:
time: 187 us; the launch traced here: 185 us
  starting transfers between devices  69.4 us (37%)
  Pallas kernels  34.6 us (19%)
  waiting for transfers between devices  33.1 us (18%)
  blocking collectives  17.6 us (9%)
  between operations  14.6 us (8%)
  local copies, waits for them, and re-layouts  9.78 us (5%)
  matrix products  3.88 us (2%)
  other arithmetic  2.62 us (1%)
    all_to_all x3, starting transfers between devices, spread(): return lax.all_to_all(copies, axis, split_axis=0, concat_axis=0)  19.8 us
    ppermute x4, starting transfers between devices, swap(): return lax.ppermute(array, 'core', [(0, 1), (1, 0)])  12.4 us
    all_to_all x1, blocking collectives, spread(): return lax.all_to_all(copies, axis, split_axis=0, concat_axis=0)  11.9 us
    pallas_call x1, Pallas kernels, attention_grads(): pl.pallas_call(grads_kernel, grid_spec=pltpu.PrefetchScalarGridSpec(num_s...  10.6 us
    all_to_all x1, starting transfers between devices, local(): lax.all_to_all(rows, TIME, split_axis=0, concat_axis=0)  10.1 us
    pallas_call x1, Pallas kernels, attention_probs(): pl.pallas_call(probs_kernel, grid_spec=pltpu.PrefetchScalarGridSpec(num_s...  9.65 us
    all_to_all x1, waiting for transfers between devices, local(): lax.all_to_all(rows, TIME, split_axis=0, concat_axis=0)  9.61 us
    ppermute x2, starting transfers between devices, padded(): low = lax.ppermute(block[block.shape[0] - width:], TIME, forward)  8.89 us
  transfers between devices with their start and end apart: 16, of which 10 were waited for; matrix products, arithmetic and copies ran while one was open for 6% of the time, Pallas kernels for 16%

profile of v8, /device:TPU:1, one launch (start us, length us, event | category | flops | bytes accessed | tf_op | source)
XLA Modules:
  0.0 185.5 jit_solution(13003680545926514258)
XLA Ops:
  9.8 7.7 %all-to-all-start = ((bf16[8,40,640]{2,1,0:T(8,128)(2,1)}), bf16[8,40,640]{2,1,0:T(8,128)(2,1)S(1)}, u32[]{:S(2)}, u32[]{:S(2)}) async-start(bf16[8,40,640]{2,1,0:T(8,128)(2,1)} %broadcast_in_dim.59), calls=%async_computation | async-start | bytes 819200 | tf_op jit(solution)/shard_map/all_to_all | solution.py:44
  17.7 4.8 %collective-permute-start = (bf16[16,1280]{1,0:T(8,128)(2,1)S(1)}, bf16[16,1280]{1,0:T(8,128)(2,1)S(1)}, u32[]{:S(2)}, u32[]{:S(2)}) collective-permute-start(bf16[16,1280]{1,0:T(8,128)(2,1)S(1)} %get-tuple-element.65), channel_id=1, source_target_pairs={{0,1},{1,2},{2,3},{3,4},{4,5},{5,6},{6,7},{7,8},{8,9},{9,10},{10,1... | collective-permute-start | bytes 122888 | tf_op jit(solution)/shard_map/ppermute | solution.py:36
  24.7 4.7 %all-to-all-done = bf16[8,40,640]{2,1,0:T(8,128)(2,1)S(1)} async-done(((bf16[8,40,640]{2,1,0:T(8,128)(2,1)}), bf16[8,40,640]{2,1,0:T(8,128)(2,1)S(1)}, u32[]{:S(2)}, u32[]{:S(2)}) %all-to-all-start) | async-done | bytes 409632 | tf_op jit(solution)/shard_map/all_to_all | solution.py:44
  30.8 6.9 %all-to-all-start.1 = ((bf16[4,8,40,640]{3,2,1,0:T(8,128)(2,1)}), bf16[4,8,40,640]{3,2,1,0:T(8,128)(2,1)}, u32[]{:S(2)}, u32[]{:S(2)}) async-start(bf16[4,8,40,640]{3,2,1,0:T(8,128)(2,1)} %broadcast_in_dim.98), calls=%async_computation.1 | async-start | bytes 3276800 | tf_op jit(solution)/shard_map/all_to_all | solution.py:44
  38.4 3.5 %collective-permute-start.2 = (bf16[128,640]{1,0:T(8,128)(2,1)}, bf16[128,640]{1,0:T(8,128)(2,1)}, u32[]{:S(2)}, u32[]{:S(2)}) collective-permute-start(bf16[128,640]{1,0:T(8,128)(2,1)} %constant_dynamic-slice_fusion.4), channel_id=1, source_target_pairs={{0,1},{1,0},{2,3},{3,2},{4,5},{5,4},{6,7},{7,6},{8,9},{9,8},{10,11... | collective-permute-start | bytes 491528 | tf_op jit(solution)/shard_map/ppermute | solution.py:59
  43.4 2.9 %conv_factor.1 = f32[128,1280]{1,0:T(8,128)S(1)} custom-call(s32[160,128]{1,0:T(8,128)S(1)} %broadcast_in_dim.58.seg, bf16[160,1280]{1,0:T(8,128)(2,1)S(1)} %pad_maximum_fusion.glu, f32[31,1280]{1,0:T(8,128)S(1)} %copy-done.3), custom_call_target="tpu_custom_call" | custom-call | flops 20316160 | bytes 1310720 | tf_op jit(solution)/shard_map/conv_factor/pallas_call | solution.py:96
  47.4 9.7 %attention_probs.1 = (bf16[4,2048,512]{2,1,0:T(8,128)(2,1)}, f32[80,2048]{1,0:T(8,128)S(1)}, f32[1,2048]{1,0:T(1,128)S(1)}) custom-call(s32[2,4]{1,0:T(2,128)S(1)} %pad_add_fusion.bounds, bf16[80,2048]{1,0:T(8,128)(2,1)S(1)} %bitcast.24, bf16[2048,80]{1,0:T(8,128)(2,1)S(1)} %copy-done.4, bf16[80,2048]{1,0:T(8,128)(2,1)S(1)} %bitcast.25, ...), custom_call_target="tpu_custom_call" | custom-call | flops 1342177280 | bytes 8388608 | tf_op jit(solution)/shard_map/attention_probs/pallas_call | solution.py:233
  57.0 2.8 %all-to-all-done.1 = bf16[4,8,40,640]{3,2,1,0:T(8,128)(2,1)} async-done(((bf16[4,8,40,640]{3,2,1,0:T(8,128)(2,1)}), bf16[4,8,40,640]{3,2,1,0:T(8,128)(2,1)}, u32[]{:S(2)}, u32[]{:S(2)}) %all-to-all-start.1) | async-done | bytes 1638432 | tf_op jit(solution)/shard_map/all_to_all | solution.py:44
  62.9 3.9 %collective-permute-start.3 = (bf16[128,1280]{1,0:T(8,128)(2,1)S(1)}, bf16[128,1280]{1,0:T(8,128)(2,1)S(1)}, u32[]{:S(2)}, u32[]{:S(2)}) collective-permute-start(bf16[128,1280]{1,0:T(8,128)(2,1)S(1)} %convolution_convert_fusion), channel_id=1, source_target_pairs={{0,1},{1,0},{2,3},{3,2},{4,5},{5,4},{6,7},{7,6},{8,9},{9,8},{10,11... | collective-permute-start | bytes 983048 | tf_op jit(solution)/shard_map/ppermute | solution.py:59
  68.2 4.0 %collective-permute-start.4 = (bf16[16,1280]{1,0:T(8,128)(2,1)S(1)}, bf16[16,1280]{1,0:T(8,128)(2,1)S(1)}, u32[]{:S(2)}, u32[]{:S(2)}) collective-permute-start(bf16[16,1280]{1,0:T(8,128)(2,1)S(1)} %get-tuple-element.63), channel_id=1, source_target_pairs={{0,1},{1,2},{2,3},{3,4},{4,5},{5,6},{6,7},{7,8},{8,9},{9,10},{10,1... | collective-permute-start | bytes 122888 | tf_op jit(solution)/shard_map/ppermute | solution.py:36
  74.3 3.7 %collective-permute-done.5 = bf16[16,1280]{1,0:T(8,128)(2,1)S(1)} collective-permute-done((bf16[16,1280]{1,0:T(8,128)(2,1)S(1)}, bf16[16,1280]{1,0:T(8,128)(2,1)S(1)}, u32[]{:S(2)}, u32[]{:S(2)}) %collective-permute-start.5) | collective-permute-done | bytes 40992 | tf_op jit(solution)/shard_map/ppermute | solution.py:37
  78.0 6.5 %conv_grads.1 = (bf16[128,1280]{1,0:T(8,128)(2,1)S(1)}, bf16[128,1280]{1,0:T(8,128)(2,1)S(1)}, f32[32,1280]{1,0:T(8,128)S(1)}) custom-call(s32[160,128]{1,0:T(8,128)S(1)} %broadcast_in_dim.58.seg, bf16[160,1280]{1,0:T(8,128)(2,1)S(1)} %pad_maximum_fusion.1.grad, bf16[160,1280]{1,0:T(8,128)(2,1)S(1)} %pad_maximum_fusion.glu, bf16[128,2560]{1,0:T(8,128)(2,1)S(1)} %copy-done.1, ...), custom_call_target="tpu_custom_call" | custom-call | flops 40632320 | bytes 2621440 | tf_op jit(solution)/shard_map/conv_grads/pallas_call | solution.py:145
  87.4 10.1 %all-to-all-start.2 = ((f32[16,2,1280]{2,1,0:T(2,128)}), f32[16,2,1280]{2,1,0:T(2,128)S(1)}, u32[]{:S(2)}, u32[]{:S(2)}) async-start(f32[16,2,1280]{2,1,0:T(2,128)} %bitcast.10), calls=%async_computation.2 | async-start | bytes 327680 | tf_op jit(solution)/shard_map/all_to_all | solution.py:457
  97.5 9.6 %all-to-all-done.2 = f32[16,2,1280]{2,1,0:T(2,128)S(1)} async-done(((f32[16,2,1280]{2,1,0:T(2,128)}), f32[16,2,1280]{2,1,0:T(2,128)S(1)}, u32[]{:S(2)}, u32[]{:S(2)}) %all-to-all-start.2) | async-done | bytes 163872 | tf_op jit(solution)/shard_map/all_to_all | solution.py:457
  107.2 4.7 %all-gather.3.cloned.1.call-done.piece = bf16[1280,2560]{1,0:T(8,128)(2,1)} async-done(((bf16[40,2560]{1,0:T(8,128)(2,1)}), bf16[1280,2560]{1,0:T(8,128)(2,1)}) %all-gather.3.cloned.1.call-update) | async-done | bytes 6553616 | tf_op jit(solution)/shard_map/all_gather | solution.py:426
  111.9 3.1 %norm_products.1 = (f32[128,1280]{1,0:T(8,128)S(1)}, bf16[128,1280]{1,0:T(8,128)(2,1)S(1)}) custom-call(bf16[128,1280]{1,0:T(8,128)(2,1)S(1)} %pad_maximum_fusion.2.own, bf16[128,1280]{1,0:T(8,128)(2,1)S(1)} %collective-permute-done.6.other, bf16[1280,2560]{1,0:T(8,128)(2,1)} %all-gather.3.cloned.1.call-done.piece), custom_call_target="tpu_custom_call" | custom-call | flops 838860800 | bytes 3276800 | tf_op jit(solution)/shard_map/norm_products/pallas_call | solution.py:388
  115.1 3.0 %collective-permute-start.7 = (bf16[128,1280]{1,0:T(8,128)(2,1)S(1)}, bf16[128,1280]{1,0:T(8,128)(2,1)S(1)}, u32[]{:S(2)}, u32[]{:S(2)}) collective-permute-start(bf16[128,1280]{1,0:T(8,128)(2,1)S(1)} %get-tuple-element.40), channel_id=1, source_target_pairs={{0,1},{1,0},{2,3},{3,2},{4,5},{5,4},{6,7},{7,6},{8,9},{9,8},{10,11... | collective-permute-start | bytes 983048 | tf_op jit(solution)/shard_map/ppermute | solution.py:59
  121.9 7.9 %all-to-all-start.3 = ((bf16[16,80,128]{2,1,0:T(8,128)(2,1)}), bf16[16,80,128]{2,1,0:T(8,128)(2,1)S(1)}, u32[]{:S(2)}, u32[]{:S(2)}) async-start(bf16[16,80,128]{2,1,0:T(8,128)(2,1)} %bitcast.11), calls=%async_computation.3 | async-start | bytes 655360 | tf_op jit(solution)/shard_map/all_to_all | solution.py:481
  129.8 3.0 %collective-permute-start.8 = (f32[3,1280]{1,0:T(4,128)S(1)}, f32[3,1280]{1,0:T(4,128)S(1)}, u32[]{:S(2)}, u32[]{:S(2)}) collective-permute-start(f32[3,1280]{1,0:T(4,128)S(1)} %pad_maximum_fusion.4), channel_id=1, source_target_pairs={{0,64},{64,0},{128,192},{192,128},{1,65},{65,1},{129,193},{193,129... | collective-permute-start | bytes 46088 | tf_op jit(solution)/shard_map/ppermute | solution.py:484
  134.6 3.4 %collective-permute-start.9 = (f32[3,1280]{1,0:T(4,128)S(1)}, f32[3,1280]{1,0:T(4,128)S(1)}, u32[]{:S(2)}, u32[]{:S(2)}) collective-permute-start(f32[3,1280]{1,0:T(4,128)S(1)} %fusion.20), channel_id=1, source_target_pairs={{0,128},{64,192},{128,0},{192,64},{1,129},{65,193},{129,1},{193,65... | collective-permute-start | bytes 46088 | tf_op jit(solution)/shard_map/ppermute | solution.py:484
  143.5 5.2 %all-to-all-start.4 = ((f32[8,3,1280]{2,1,0:T(4,128)}), f32[8,3,1280]{2,1,0:T(4,128)S(1)}, u32[]{:S(2)}, u32[]{:S(2)}) async-start(f32[8,3,1280]{2,1,0:T(4,128)} %broadcast_in_dim.102), calls=%async_computation.4 | async-start | bytes 327680 | tf_op jit(solution)/shard_map/all_to_all | solution.py:44
  148.8 10.6 %attention_grads.1 = (bf16[80,2048]{1,0:T(8,128)(2,1)}, bf16[80,2048]{1,0:T(8,128)(2,1)}, bf16[80,2048]{1,0:T(8,128)(2,1)}) custom-call(s32[2,4]{1,0:T(2,128)S(1)} %pad_add_fusion.bounds, bf16[4,2048,512]{2,1,0:T(8,128)(2,1)} %get-tuple-element.45.probs, bf16[16,80,128]{2,1,0:T(8,128)(2,1)S(1)} %all-to-all-done.3.ctx_t, ...), custom_call_target="tpu_custom_call" | custom-call | flops 2684354560 | bytes 8388608 | tf_op jit(solution)/shard_map/attention_grads/pallas_call | solution.py:308
  159.5 11.9 %all_to_all.30 = f32[8,3,1280]{2,1,0:T(4,128)S(1)} all-to-all(f32[8,3,1280]{2,1,0:T(4,128)S(1)} %broadcast_in_dim.103), channel_id=1, replica_groups=mesh['far'=2,'y'=4,'x'=4,'z'=8,'core'=2] {'z'}, dimensions={0} | all-to-all | bytes 245760 | tf_op jit(solution)/shard_map/all_to_all | solution.py:44
  171.4 5.7 %all-gather = f32[16,3,1280]{2,0,1:T(8,128)S(1)} all-gather(f32[8,3,1280]{2,0,1:T(8,128)S(1)} %copy.43), channel_id=2, replica_groups=mesh['far'=2,'y'=4,'x'=4,'z'=8,'core'=2] {'core'}, dimensions={0}, use_global_device_ids=true | all-gather | bytes 368640 | tf_op jit(solution)/shard_map/all_gather | solution.py:492
  (105 shorter events, 31.4 us)
Async XLA Ops:
  7.2 10.3 %copy-start.1 = (bf16[128,2560]{1,0:T(8,128)(2,1)S(1)}, bf16[128,2560]{1,0:T(8,128)(2,1)}, u32[]{:S(2)}) copy-start(bf16[128,2560]{1,0:T(8,128)(2,1)} %gate_ref.1) | copy-start | bytes 1966084
  7.2 104.7 %all-gather.3.cloned.1.call-start = ((), (), s32[]{:S(2)}) async-start(), calls=%async_computation.6 | async-start | bytes 6758400 | tf_op jit(solution)/shard_map/all_gather | solution.py:426
  7.2 17.2 %copy-start.16 = (s32[1,8]{1,0:T(1,128)S(1)}, s32[1,8]{1,0:T(1,128)}, u32[]{:S(2)}) copy-start(s32[1,8]{1,0:T(1,128)} %param.18) | copy-start | bytes 100
  9.8 19.6 %all-to-all-start = ((bf16[8,40,640]{2,1,0:T(8,128)(2,1)}), bf16[8,40,640]{2,1,0:T(8,128)(2,1)S(1)}, u32[]{:S(2)}, u32[]{:S(2)}) async-start(bf16[8,40,640]{2,1,0:T(8,128)(2,1)} %broadcast_in_dim.59), calls=%async_computation | async-start | bytes 819200 | tf_op jit(solution)/shard_map/all_to_all | solution.py:44
  17.7 25.6 %collective-permute-start = (bf16[16,1280]{1,0:T(8,128)(2,1)S(1)}, bf16[16,1280]{1,0:T(8,128)(2,1)S(1)}, u32[]{:S(2)}, u32[]{:S(2)}) collective-permute-start(bf16[16,1280]{1,0:T(8,128)(2,1)S(1)} %get-tuple-element.65), channel_id=1, source_target_pairs={{0,1},{1,2},{2,3},{3,4},{4,5},{5,6},{6,7},{7,8},{8,9},{9,10},{10,1... | collective-permute-start | bytes 122888 | tf_op jit(solution)/shard_map/ppermute | solution.py:36
  22.5 20.7 %collective-permute-start.1 = (bf16[16,1280]{1,0:T(8,128)(2,1)S(1)}, bf16[16,1280]{1,0:T(8,128)(2,1)S(1)}, u32[]{:S(2)}, u32[]{:S(2)}) collective-permute-start(bf16[16,1280]{1,0:T(8,128)(2,1)S(1)} %get-tuple-element.66), channel_id=1, source_target_pairs={{1,0},{2,1},{3,2},{4,3},{5,4},{6,5},{7,6},{8,7},{9,8},{10,9},{11,1... | collective-permute-start | bytes 122888 | tf_op jit(solution)/shard_map/ppermute | solution.py:37
  30.8 11.5 %copy-start.2 = (bf16[2048,80]{0,1:T(8,128)(2,1)S(1)}, bf16[2048,80]{0,1:T(8,128)(2,1)}, u32[]{:S(2)}) copy-start(bf16[2048,80]{0,1:T(8,128)(2,1)} %param.16) | copy-start | bytes 983044
  30.8 29.0 %all-to-all-start.1 = ((bf16[4,8,40,640]{3,2,1,0:T(8,128)(2,1)}), bf16[4,8,40,640]{3,2,1,0:T(8,128)(2,1)}, u32[]{:S(2)}, u32[]{:S(2)}) async-start(bf16[4,8,40,640]{3,2,1,0:T(8,128)(2,1)} %broadcast_in_dim.98), calls=%async_computation.1 | async-start | bytes 3276800 | tf_op jit(solution)/shard_map/all_to_all | solution.py:44
  37.7 8.7 %copy-start.5 = (bf16[2048,80]{0,1:T(8,128)(2,1)S(1)}, bf16[2048,80]{0,1:T(8,128)(2,1)}, u32[]{:S(2)}) copy-start(bf16[2048,80]{0,1:T(8,128)(2,1)} %param.15) | copy-start | bytes 983044
  38.4 23.0 %collective-permute-start.2 = (bf16[128,640]{1,0:T(8,128)(2,1)}, bf16[128,640]{1,0:T(8,128)(2,1)}, u32[]{:S(2)}, u32[]{:S(2)}) collective-permute-start(bf16[128,640]{1,0:T(8,128)(2,1)} %constant_dynamic-slice_fusion.4), channel_id=1, source_target_pairs={{0,1},{1,0},{2,3},{3,2},{4,5},{5,4},{6,7},{7,6},{8,9},{9,8},{10,11... | collective-permute-start | bytes 491528 | tf_op jit(solution)/shard_map/ppermute | solution.py:59
  62.9 5.1 %collective-permute-start.3 = (bf16[128,1280]{1,0:T(8,128)(2,1)S(1)}, bf16[128,1280]{1,0:T(8,128)(2,1)S(1)}, u32[]{:S(2)}, u32[]{:S(2)}) collective-permute-start(bf16[128,1280]{1,0:T(8,128)(2,1)S(1)} %convolution_convert_fusion), channel_id=1, source_target_pairs={{0,1},{1,0},{2,3},{3,2},{4,5},{5,4},{6,7},{7,6},{8,9},{9,8},{10,11... | collective-permute-start | bytes 983048 | tf_op jit(solution)/shard_map/ppermute | solution.py:59
  68.2 6.1 %collective-permute-start.4 = (bf16[16,1280]{1,0:T(8,128)(2,1)S(1)}, bf16[16,1280]{1,0:T(8,128)(2,1)S(1)}, u32[]{:S(2)}, u32[]{:S(2)}) collective-permute-start(bf16[16,1280]{1,0:T(8,128)(2,1)S(1)} %get-tuple-element.63), channel_id=1, source_target_pairs={{0,1},{1,2},{2,3},{3,4},{4,5},{5,6},{6,7},{7,8},{8,9},{9,10},{10,1... | collective-permute-start | bytes 122888 | tf_op jit(solution)/shard_map/ppermute | solution.py:36
  72.2 5.7 %collective-permute-start.5 = (bf16[16,1280]{1,0:T(8,128)(2,1)S(1)}, bf16[16,1280]{1,0:T(8,128)(2,1)S(1)}, u32[]{:S(2)}, u32[]{:S(2)}) collective-permute-start(bf16[16,1280]{1,0:T(8,128)(2,1)S(1)} %get-tuple-element.64), channel_id=1, source_target_pairs={{1,0},{2,1},{3,2},{4,3},{5,4},{6,5},{7,6},{8,7},{9,8},{10,9},{11,1... | collective-permute-start | bytes 122888 | tf_op jit(solution)/shard_map/ppermute | solution.py:37
  84.7 27.2 %collective-permute-start.6 = (bf16[128,1280]{1,0:T(8,128)(2,1)S(1)}, bf16[128,1280]{1,0:T(8,128)(2,1)S(1)}, u32[]{:S(2)}, u32[]{:S(2)}) collective-permute-start(bf16[128,1280]{1,0:T(8,128)(2,1)S(1)} %pad_maximum_fusion.3), channel_id=1, source_target_pairs={{0,1},{1,0},{2,3},{3,2},{4,5},{5,4},{6,7},{7,6},{8,9},{9,8},{10,11... | collective-permute-start | bytes 983048 | tf_op jit(solution)/shard_map/ppermute | solution.py:59
  87.4 19.7 %all-to-all-start.2 = ((f32[16,2,1280]{2,1,0:T(2,128)}), f32[16,2,1280]{2,1,0:T(2,128)S(1)}, u32[]{:S(2)}, u32[]{:S(2)}) async-start(f32[16,2,1280]{2,1,0:T(2,128)} %bitcast.10), calls=%async_computation.2 | async-start | bytes 327680 | tf_op jit(solution)/shard_map/all_to_all | solution.py:457
  107.2 10.9 %copy-start.10 = (bf16[128,1280]{1,0:T(8,128)(2,1)S(1)}, bf16[128,1280]{1,0:T(8,128)(2,1)}, u32[]{:S(2)}) copy-start(bf16[128,1280]{1,0:T(8,128)(2,1)} %param.13) | copy-start | bytes 983044
  107.2 12.2 %copy-start.15 = (f32[1280]{0:T(1024)S(1)}, f32[1280]{0:T(1024)}, u32[]{:S(2)}) copy-start(f32[1280]{0:T(1024)} %param.19) | copy-start | bytes 15364
  111.9 8.2 %copy-start.8 = (bf16[1280,2560]{1,0:T(8,128)(2,1)S(1)}, bf16[1280,2560]{1,0:T(8,128)(2,1)}, u32[]{:S(2)}) copy-start(bf16[1280,2560]{1,0:T(8,128)(2,1)} %all-gather.3.cloned.1.call-done.piece) | copy-start | bytes 19660804
  115.1 4.3 %collective-permute-start.7 = (bf16[128,1280]{1,0:T(8,128)(2,1)S(1)}, bf16[128,1280]{1,0:T(8,128)(2,1)S(1)}, u32[]{:S(2)}, u32[]{:S(2)}) collective-permute-start(bf16[128,1280]{1,0:T(8,128)(2,1)S(1)} %get-tuple-element.40), channel_id=1, source_target_pairs={{0,1},{1,0},{2,3},{3,2},{4,5},{5,4},{6,7},{7,6},{8,9},{9,8},{10,11... | collective-permute-start | bytes 983048 | tf_op jit(solution)/shard_map/ppermute | solution.py:59
  121.8 16.5 %copy-start.7 = (bf16[2048,80]{0,1:T(8,128)(2,1)S(1)}, bf16[2048,80]{0,1:T(8,128)(2,1)}, u32[]{:S(2)}) copy-start(bf16[2048,80]{0,1:T(8,128)(2,1)} %param.17) | copy-start | bytes 983044
  121.9 21.0 %all-to-all-start.3 = ((bf16[16,80,128]{2,1,0:T(8,128)(2,1)}), bf16[16,80,128]{2,1,0:T(8,128)(2,1)S(1)}, u32[]{:S(2)}, u32[]{:S(2)}) async-start(bf16[16,80,128]{2,1,0:T(8,128)(2,1)} %bitcast.11), calls=%async_computation.3 | async-start | bytes 655360 | tf_op jit(solution)/shard_map/all_to_all | solution.py:481
  129.8 4.8 %collective-permute-start.8 = (f32[3,1280]{1,0:T(4,128)S(1)}, f32[3,1280]{1,0:T(4,128)S(1)}, u32[]{:S(2)}, u32[]{:S(2)}) collective-permute-start(f32[3,1280]{1,0:T(4,128)S(1)} %pad_maximum_fusion.4), channel_id=1, source_target_pairs={{0,64},{64,0},{128,192},{192,128},{1,65},{65,1},{129,193},{193,129... | collective-permute-start | bytes 46088 | tf_op jit(solution)/shard_map/ppermute | solution.py:484
  134.6 5.7 %collective-permute-start.9 = (f32[3,1280]{1,0:T(4,128)S(1)}, f32[3,1280]{1,0:T(4,128)S(1)}, u32[]{:S(2)}, u32[]{:S(2)}) collective-permute-start(f32[3,1280]{1,0:T(4,128)S(1)} %fusion.20), channel_id=1, source_target_pairs={{0,128},{64,192},{128,0},{192,64},{1,129},{65,193},{129,1},{193,65... | collective-permute-start | bytes 46088 | tf_op jit(solution)/shard_map/ppermute | solution.py:484
  143.5 15.9 %all-to-all-start.4 = ((f32[8,3,1280]{2,1,0:T(4,128)}), f32[8,3,1280]{2,1,0:T(4,128)S(1)}, u32[]{:S(2)}, u32[]{:S(2)}) async-start(f32[8,3,1280]{2,1,0:T(4,128)} %broadcast_in_dim.102), calls=%async_computation.4 | async-start | bytes 327680 | tf_op jit(solution)/shard_map/all_to_all | solution.py:44
  (9 other events, 37.2 us)
Sparse Core Ops, SparseCore 0:
  11.8 100.1 all-gather.2
